TPU v7x, 256 devices: a whole 4x4x8 slice. The times are simulated.
256 devices in a mesh: flow: 8 (over z_lo, y), trans: 32 (over z_hi, x, core).
Axes of the slice: x: 4, y: 4, z: 8 (z_hi: 4, z_lo: 2; z = z_hi * 2 + z_lo), core: 2. Of those that a mesh axis runs over, the one named last changes fastest.
Arguments:
- main_pos: float32 [16, 2048, 3, 128], P('flow', 'trans')
- main_vel: float32 [16, 2048, 3, 128], P('flow', 'trans'), may hold values from -6 to 6
- main_force: float32 [16, 2048, 3, 128], P('flow', 'trans'), may hold values from -240 to 240
- main_seed: int32 [16, 2048, 128], P('flow', 'trans'), may hold values from 0 to 4095
- main_count: int32 [16, 2048], P('flow', 'trans'), may hold values from 1 to 128, as said below
- prec_pos: float32 [8, 1024, 3, 128], P('flow', 'trans')
- prec_vel: float32 [8, 1024, 3, 128], P('flow', 'trans'), may hold values from -6 to 6
- prec_force: float32 [8, 1024, 3, 128], P('flow', 'trans'), may hold values from -240 to 240
- prec_seed: int32 [8, 1024, 128], P('flow', 'trans'), may hold values from 0 to 4095
- cross_row: int32 [512], P('trans'), may hold values from 0 to 4095, as said below
- cross_dest: int32 [512], P('trans'), may hold values from 0 to 31, as said below
- cross_cell: int32 [512], P('trans'), may hold values from 0 to 63
- outlet_bin: int32 [2048, 128], P('trans'), may hold values from 0 to 63
- outlet_coef: float32 [64], replicated, may hold values from 2 to 20
Outputs:
- main_pos_out: float32 [16, 2048, 3, 128], P('flow', 'trans')
- main_vel_out: float32 [16, 2048, 3, 128], P('flow', 'trans')
- main_force_out: float32 [16, 2048, 3, 128], P('flow', 'trans')
- prec_pos_out: float32 [8, 1024, 3, 128], P('flow', 'trans')
- prec_vel_out: float32 [8, 1024, 3, 128], P('flow', 'trans')
- prec_force_out: float32 [8, 1024, 3, 128], P('flow', 'trans')
Inputs may be any that keep to these rules, and one draw needn't show every extreme that they name: `main_count`: cells of main flow column 0 hold at most 64 beads, one of them exactly that many; some cell holds 128. `cross_row`: the 16 rows of one trans index name distinct slots. `cross_dest`: among the 16 rows of one trans index no destination appears more than 2 times; one destination appears exactly 2 times among the rows of every trans index.
All inputs are finite; a program needn't handle non-finite values.
Results may differ from a plain program's by a relative error of at most 0.0003.
Values sent between devices are 32-bit elements; how exact they have to be, the bound alone decides.
A program may use at most 192 MiB of HBM per device.

v0:
```python
import jax
import jax.numpy as jnp
from jax import lax
from jax.sharding import PartitionSpec as P

BINS = 64


time_step = 0.01
repulsion = 25.0
friction = 4.5
noise_amp = 30.0
box_height = 16.0
seed_modulus = 4093
unit_spread = 3.4641016151377544


def with_halo(cells, sides, width, closed):
    for axis, dim in sides:
        count = lax.axis_size(axis)
        ends = count if closed else count - 1
        head = lax.slice_in_dim(cells, 0, width, axis=dim)
        tail = lax.slice_in_dim(cells, cells.shape[dim] - width, cells.shape[dim], axis=dim)
        cells = jnp.concatenate(
            [
                lax.ppermute(tail, axis, [(i, (i + 1) % count) for i in range(ends)]),
                cells,
                lax.ppermute(head, axis, [((i + 1) % count, i) for i in range(ends)]),
            ],
            axis=dim,
        )
    return cells


def tile_forces(center, padded, flow_steps=(-1, 0, 1)):
    count_cells = center.shape[0]
    tile_slots = center.shape[2]
    pos_i = center[:, 0:3, :, None]
    vel_i = center[:, 3:6, :, None]
    code_i = center[:, 6, :, None]
    seed_i = (code_i - 1.0).astype(jnp.int32)
    summed = jnp.zeros((count_cells, 3, tile_slots), jnp.float32)
    for step_flow in flow_steps:
        for step_trans in (-1, 0, 1):
            others = lax.slice_in_dim(
                padded[1 + step_flow], 1 + step_trans, 1 + step_trans + count_cells, axis=0
            )
            pos_j = others[:, 0:3, None, :]
            vel_j = others[:, 3:6, None, :]
            code_j = others[:, 6, None, :]
            seed_j = (code_j - 1.0).astype(jnp.int32)
            delta_x = pos_i[:, 0] - (pos_j[:, 0] + float(step_flow))
            delta_y = pos_i[:, 1] - (pos_j[:, 1] + float(step_trans))
            delta_z = pos_i[:, 2] - pos_j[:, 2]
            delta_z = delta_z - box_height * jnp.floor(delta_z / box_height + 0.5)
            pair_mask = (code_i > 0.5) & (code_j > 0.5)
            if step_flow == 0 and step_trans == 0:
                pair_mask = pair_mask & jnp.logical_not(jnp.eye(tile_slots, dtype=bool))
            dist_sq = jnp.where(
                pair_mask, delta_x * delta_x + delta_y * delta_y + delta_z * delta_z, 1.0
            )
            inverse = lax.rsqrt(dist_sq)
            weight = jnp.where(pair_mask, jnp.maximum(1.0 - dist_sq * inverse, 0.0), 0.0)
            along = (
                (vel_i[:, 0] - vel_j[:, 0]) * delta_x
                + (vel_i[:, 1] - vel_j[:, 1]) * delta_y
                + (vel_i[:, 2] - vel_j[:, 2]) * delta_z
            ) * inverse
            hashed = (seed_i * seed_j + seed_i + seed_j) % seed_modulus
            noise_term = (hashed.astype(jnp.float32) / seed_modulus - 0.5) * unit_spread
            scalar = (
                repulsion * weight
                - friction * weight * weight * along
                + noise_amp * weight * noise_term
            ) * inverse
            summed = summed + jnp.stack(
                [
                    jnp.sum(scalar * delta_x, axis=2),
                    jnp.sum(scalar * delta_y, axis=2),
                    jnp.sum(scalar * delta_z, axis=2),
                ],
                axis=1,
            )
    return summed


def drift_state(position, velocity, force):
    half_vel = velocity + 0.5 * time_step * force
    return (position + time_step * half_vel, half_vel)


def block_forces(bead_state, padded):

    def one_row(row_index):
        center = lax.dynamic_index_in_dim(bead_state, row_index, 0, keepdims=False)
        window = lax.dynamic_slice_in_dim(padded, row_index, 3, 0)
        return tile_forces(center, window)

    return lax.map(one_row, jnp.arange(bead_state.shape[0], dtype=jnp.int32))


def shards(
    main_pos,
    main_vel,
    main_force,
    main_seed,
    main_count,
    prec_pos,
    prec_vel,
    prec_force,
    prec_seed,
    cross_row,
    cross_dest,
    cross_cell,
    outlet_bin,
    outlet_coef,
):
    tile_slots = main_pos.shape[3]
    flow_cells = main_pos.shape[0]
    trans_cells = main_pos.shape[1]
    flow_index = lax.axis_index("flow")
    trans_index = lax.axis_index("trans")
    flow_devices = lax.axis_size("flow")
    trans_devices = lax.axis_size("trans")
    src_cell = cross_row // tile_slots
    src_slot = cross_row % tile_slots
    arrived = jnp.concatenate(
        [
            prec_pos[0, src_cell, :, src_slot].T,
            prec_vel[0, src_cell, :, src_slot].T,
            prec_force[0, src_cell, :, src_slot].T,
            prec_seed[0, src_cell, src_slot][None].astype(jnp.float32),
            cross_dest[None].astype(jnp.float32),
            cross_cell[None].astype(jnp.float32),
        ],
        axis=0,
    )
    gathered = lax.all_gather(arrived, "trans", axis=1, tiled=True)
    usable = gathered[10] == trans_index.astype(jnp.float32)
    cells_in = gathered[11]
    payload = gathered[0:10]
    cell_ids = cells_in.astype(jnp.int32)
    cell_hot = (
        (cell_ids[:, None] == jnp.arange(trans_cells, dtype=jnp.int32)[None, :]) & usable[:, None]
    ).astype(jnp.int32)
    earlier = jnp.sum((jnp.cumsum(cell_hot, axis=0) - cell_hot) * cell_hot, axis=1)
    arrivals = jnp.sum(cell_hot, axis=0)
    first_column = flow_index == 0
    target_slot = jnp.where(usable & first_column, main_count[0, cell_ids] + earlier, tile_slots)
    main_pos = main_pos.at[0, cell_ids, :, target_slot].set(payload[0:3].T, mode="drop")
    main_vel = main_vel.at[0, cell_ids, :, target_slot].set(payload[3:6].T, mode="drop")
    main_force = main_force.at[0, cell_ids, :, target_slot].set(payload[6:9].T, mode="drop")
    main_seed = main_seed.at[0, cell_ids, target_slot].set(
        payload[9].astype(jnp.int32), mode="drop"
    )
    new_count = main_count.at[0].add(jnp.where(first_column, arrivals, 0))
    occupied = jnp.arange(tile_slots, dtype=jnp.int32)[None, None, :] < new_count[:, :, None]
    main_code = jnp.where(occupied, main_seed + 1, 0).astype(jnp.float32)[:, :, None, :]
    prec_code = (prec_seed + 1).astype(jnp.float32)[:, :, None, :]
    main_moved, main_half = drift_state(main_pos, main_vel, main_force)
    prec_moved, prec_half = drift_state(prec_pos, prec_vel, prec_force)
    main_state = jnp.concatenate([main_moved, main_half, main_code], axis=2)
    prec_state = jnp.concatenate([prec_moved, prec_half, prec_code], axis=2)
    main_padded = with_halo(main_state, (("flow", 0), ("trans", 1)), 1, False)
    prec_padded = with_halo(prec_state, (("flow", 0), ("trans", 1)), 1, True)
    prec_forces = block_forces(prec_state, prec_padded)
    main_forces = block_forces(main_state, main_padded)
    last_column = occupied[flow_cells - 1]
    bin_hot = (
        (outlet_bin[None, :, :] == jnp.arange(BINS, dtype=jnp.int32)[:, None, None])
        & last_column[None]
    ).astype(jnp.float32)
    profile = jnp.sum(bin_hot, axis=(1, 2))
    total_profile = lax.psum(profile, "trans")
    density = total_profile * BINS / (trans_cells * trans_devices * tile_slots)
    outlet_push = outlet_coef * density
    outlet_force = -jnp.sum(bin_hot * outlet_push[:, None, None], axis=0)
    outlet_force = jnp.where(flow_index == flow_devices - 1, outlet_force, 0.0)
    main_forces = main_forces.at[flow_cells - 1, :, 0, :].add(outlet_force)
    main_vel_out = main_half + 0.5 * time_step * main_forces
    prec_vel_out = prec_half + 0.5 * time_step * prec_forces
    slot_mask = occupied[:, :, None, :]
    return (
        jnp.where(slot_mask, main_moved, 0.0),
        jnp.where(slot_mask, main_vel_out, 0.0),
        jnp.where(slot_mask, main_forces, 0.0),
        prec_moved,
        prec_vel_out,
        prec_forces,
    )


def solution(mesh):
    return jax.shard_map(
        shards,
        mesh=mesh,
        in_specs=(
            P("flow", "trans", None, None),
            P("flow", "trans", None, None),
            P("flow", "trans", None, None),
            P("flow", "trans", None),
            P("flow", "trans"),
            P("flow", "trans", None, None),
            P("flow", "trans", None, None),
            P("flow", "trans", None, None),
            P("flow", "trans", None),
            P("trans"),
            P("trans"),
            P("trans"),
            P("trans", None),
            P(),
        ),
        out_specs=(
            P("flow", "trans", None, None),
            P("flow", "trans", None, None),
            P("flow", "trans", None, None),
            P("flow", "trans", None, None),
            P("flow", "trans", None, None),
            P("flow", "trans", None, None),
        ),
        check_vma=False,
    )
```

profile of v0, /device:TPU:1, one launch (start us, length us, event | category | flops | bytes accessed | tf_op | source)
XLA Modules:
  0.0 810.6 jit_solution(746661977113860053)
XLA Ops:
  3.0 5.0 collective-permute-start.5
  18.4 47.9 %all_gather.3 = f32[12,512]{0,1:T(8,128)S(1)} all-gather(f32[12,16]{0,1:T(8,128)S(1)} %concatenate.247), channel_id=1, replica_groups=mesh['flow'=8,'trans'=32] {'trans'}, dimensions={1}, use_global_device_ids=true | all-gather | bytes 25344 | tf_op jit(solution)/shard_map/all_gather | solution.py:138
  68.9 4.8 gather_fusion.4
  78.5 4.7 copy.133
  83.1 4.7 copy.134
  87.8 30.8 %scatter_fusion.3 = s32[2,64,128]{2,1,0:T(8,128)S(1)} fusion(s32[2,64,128]{2,1,0:T(8,128)S(1)} %copy-done, s32[512]{0:T(512)S(1)} %bitcast.691, s32[512]{0:T(512)S(1)} %get-tuple-element.244), kind=kCustom, calls=%fused_computation.8 | custom fusion | bytes 12288 | tf_op jit(solution)/shard_map/scatter | solution.py:153
  118.7 54.2 %scatter_fusion = f32[2,64,3,128]{2,3,1,0:T(8,128)} fusion(f32[2,64,3,128]{2,3,1,0:T(8,128)} %copy.132, s32[512]{0:T(512)S(1)} %bitcast.692, f32[512,3]{1,0:T(8,128)S(1)} %get-tuple-element.400), kind=kCustom, calls=%fused_computation.5 | custom fusion | bytes 24576 | tf_op jit(solution)/shard_map/scatter | solution.py:150
  172.9 53.9 %scatter_fusion.1 = f32[2,64,3,128]{2,3,1,0:T(8,128)} fusion(f32[2,64,3,128]{2,3,1,0:T(8,128)} %copy.133, s32[512]{0:T(512)S(1)} %bitcast.693, f32[512,3]{1,0:T(8,128)S(1)} %get-tuple-element.399), kind=kCustom, calls=%fused_computation.6 | custom fusion | bytes 24576 | tf_op jit(solution)/shard_map/scatter | solution.py:151
  226.8 54.1 %scatter_fusion.2 = f32[2,64,3,128]{2,3,1,0:T(8,128)} fusion(f32[2,64,3,128]{2,3,1,0:T(8,128)} %copy.134, s32[512]{0:T(512)S(1)} %bitcast.694, f32[512,3]{1,0:T(8,128)S(1)} %get-tuple-element.398), kind=kCustom, calls=%fused_computation.7 | custom fusion | bytes 24576 | tf_op jit(solution)/shard_map/scatter | solution.py:152
  280.9 19.6 %broadcast_select_fusion.1 = (f32[2,64,3,128]{2,3,1,0:T(8,128)}, f32[2,64,3,128]{2,3,1,0:T(8,128)}, f32[2,64,3,128]{2,3,1,0:T(8,128)}) fusion(pred[2,64,128]{2,1,0:T(8,128)(4,1)S(1)} %iota_compare_fusion.5, f32[2,64,3,128]{2,3,1,0:T(8,128)} %scatter_fusion, f32[2,64,3,128]{2,3,1,0:T(8,128)} %scatter_fusion.1, f32[2,64,3,128]{2,3,1,0:T(8,128)} %scatter_fusion.2), kind=kLoop, calls=%fused_computation.533 | loop fusion | flops 245760 | bytes 1196032 | tf_op jit(solution)/shard_map/jit(_where)/select_n | solution.py:184
  300.6 5.2 copy.136
  305.8 5.2 copy.135
  312.4 13.3 %collective-permute-start = (f32[1,64,7,128]{3,1,2,0:T(8,128)S(1)}, f32[1,64,7,128]{3,1,2,0:T(8,128)S(1)}, u32[]{:S(2)}, u32[]{:S(2)}) collective-permute-start(f32[1,64,7,128]{3,1,2,0:T(8,128)S(1)} %get-tuple-element.388), channel_id=1, source_target_pairs={{0,32},{32,64},{64,96},{96,128},{128,160},{160,192},{192,224},{1,3... | collective-permute-start | bytes 688136 | tf_op jit(solution)/shard_map/ppermute | solution.py:26
  325.9 5.9 copy.145
  332.3 84.4 %psum.7 = f32[64]{0:T(128)S(1)} all-reduce(f32[64]{0:T(128)S(1)} %convert_reduce_fusion), channel_id=1, replica_groups=mesh['flow'=8,'trans'=32] {'trans'}, use_global_device_ids=true, to_apply=%region_38.39 | all-reduce | flops 64 | bytes 512 | tf_op jit(solution)/shard_map/psum | solution.py:174
  416.8 7.4 fusion.457
  426.7 7.4 fusion.469
  434.1 7.4 fusion.445
  441.9 7.4 fusion.473
  449.3 7.4 fusion.465
  456.7 7.4 fusion.461
  464.1 7.4 fusion.453
  471.4 7.4 fusion.449
  478.8 7.4 fusion.441
  493.6 274.3 %while.19 = (s32[]{:T(128)}, f32[2,64,3,128]{3,1,2,0:T(8,128)S(1)}, s32[2]{0:T(128)S(1)}, f32[2,64,7,128]{3,1,2,0:T(8,128)S(1)}, f32[4,66,7,128]{3,1,2,0:T(8,128...) while((s32[]{:T(128)}, f32[2,64,3,128]{3,1,2,0:T(8,128)S(1)}, ...), condition=%wide.region_36.37_spmd, body=%wide.region_8.36_spmd.sunk | while | flops 530325504 | bytes 19693832 | solution.py:99
  498.0 14.8 %fusion.571 = (f32[64,128]{1,0:T(8,128)S(1)}, f32[64,128]{1,0:T(8,128)S(1)}, f32[64,128]{1,0:T(8,128)S(1)}) fusion(f32[64,128]{1,0:T(8,128)S(1)} %get-tuple-element.663, f32[64,128]{1,0:T(8,128)S(1)} %get-tuple-element.666, s32[64,128]{1,0:T(8,128)S(1)} %convert_bitcast_fusion.34, s32[64,128]{1,0:T(8,128)S(1)} %convert_bitcast_fusion.35, ...), kind=kLoop, calls=%fused_computation.317.clone.1 | loop fusion | flops 58695680 | bytes 573440 | tf_op jit(solution)/shard_map/while/body/eval_jaxpr/reduce_sum | solution.py:78
  512.9 14.8 %fusion.572 = (f32[64,128]{1,0:T(8,128)S(1)}, f32[64,128]{1,0:T(8,128)S(1)}, f32[64,128]{1,0:T(8,128)S(1)}) fusion(f32[64,128]{1,0:T(8,128)S(1)} %get-tuple-element.684, f32[64,128]{1,0:T(8,128)S(1)} %get-tuple-element.666, s32[64,128]{1,0:T(8,128)S(1)} %convert_bitcast_fusion.36, s32[64,128]{1,0:T(8,128)S(1)} %convert_bitcast_fusion.35, ...), kind=kLoop, calls=%fused_computation.321.clone.1 | loop fusion | flops 58695680 | bytes 573440 | tf_op jit(solution)/shard_map/while/body/eval_jaxpr/reduce_sum | solution.py:78
  527.8 14.8 %fusion.574 = (f32[64,128]{1,0:T(8,128)S(1)}, f32[64,128]{1,0:T(8,128)S(1)}, f32[64,128]{1,0:T(8,128)S(1)}) fusion(f32[64,128]{1,0:T(8,128)S(1)} %get-tuple-element.696, f32[64,128]{1,0:T(8,128)S(1)} %get-tuple-element.666, s32[64,128]{1,0:T(8,128)S(1)} %convert_bitcast_fusion.37, s32[64,128]{1,0:T(8,128)S(1)} %convert_bitcast_fusion.35, ...), kind=kLoop, calls=%fused_computation.325.clone.1 | loop fusion | flops 58695680 | bytes 573440 | tf_op jit(solution)/shard_map/while/body/eval_jaxpr/reduce_sum | solution.py:78
  542.7 14.8 %fusion.576 = (f32[64,128]{1,0:T(8,128)S(1)}, f32[64,128]{1,0:T(8,128)S(1)}, f32[64,128]{1,0:T(8,128)S(1)}) fusion(f32[64,128]{1,0:T(8,128)S(1)} %get-tuple-element.708, f32[64,128]{1,0:T(8,128)S(1)} %get-tuple-element.666, s32[64,128]{1,0:T(8,128)S(1)} %convert_bitcast_fusion.38, s32[64,128]{1,0:T(8,128)S(1)} %convert_bitcast_fusion.35, ...), kind=kLoop, calls=%fused_computation.329.clone.1 | loop fusion | flops 58695680 | bytes 573440 | tf_op jit(solution)/shard_map/while/body/eval_jaxpr/reduce_sum | solution.py:78
  557.6 13.6 %fusion.578 = (f32[64,128]{1,0:T(8,128)S(1)}, f32[64,128]{1,0:T(8,128)S(1)}, f32[64,128]{1,0:T(8,128)S(1)}) fusion(f32[64,128]{1,0:T(8,128)S(1)} %get-tuple-element.720, f32[64,128]{1,0:T(8,128)S(1)} %get-tuple-element.666, s32[64,128]{1,0:T(8,128)S(1)} %convert_bitcast_fusion.39, s32[64,128]{1,0:T(8,128)S(1)} %convert_bitcast_fusion.35, ...), kind=kLoop, calls=%fused_computation.333.clone.1 | loop fusion | flops 59744256 | bytes 589824 | tf_op jit(solution)/shard_map/while/body/eval_jaxpr/reduce_sum | solution.py:78
  571.3 14.8 %fusion.580 = (f32[64,128]{1,0:T(8,128)S(1)}, f32[64,128]{1,0:T(8,128)S(1)}, f32[64,128]{1,0:T(8,128)S(1)}) fusion(f32[64,128]{1,0:T(8,128)S(1)} %get-tuple-element.732, f32[64,128]{1,0:T(8,128)S(1)} %get-tuple-element.666, s32[64,128]{1,0:T(8,128)S(1)} %convert_bitcast_fusion.40, s32[64,128]{1,0:T(8,128)S(1)} %convert_bitcast_fusion.35, ...), kind=kLoop, calls=%fused_computation.337.clone.1 | loop fusion | flops 58695680 | bytes 573440 | tf_op jit(solution)/shard_map/while/body/eval_jaxpr/reduce_sum | solution.py:78
  586.2 14.8 %fusion.582 = (f32[64,128]{1,0:T(8,128)S(1)}, f32[64,128]{1,0:T(8,128)S(1)}, f32[64,128]{1,0:T(8,128)S(1)}) fusion(f32[64,128]{1,0:T(8,128)S(1)} %get-tuple-element.744, f32[64,128]{1,0:T(8,128)S(1)} %get-tuple-element.666, s32[64,128]{1,0:T(8,128)S(1)} %convert_bitcast_fusion.41, s32[64,128]{1,0:T(8,128)S(1)} %convert_bitcast_fusion.35, ...), kind=kLoop, calls=%fused_computation.341.clone.1 | loop fusion | flops 58695680 | bytes 573440 | tf_op jit(solution)/shard_map/while/body/eval_jaxpr/reduce_sum | solution.py:78
  601.1 14.8 %fusion.583 = (f32[64,128]{1,0:T(8,128)S(1)}, f32[64,128]{1,0:T(8,128)S(1)}, f32[64,128]{1,0:T(8,128)S(1)}) fusion(f32[64,128]{1,0:T(8,128)S(1)} %get-tuple-element.756, f32[64,128]{1,0:T(8,128)S(1)} %get-tuple-element.666, s32[64,128]{1,0:T(8,128)S(1)} %convert_bitcast_fusion.42, s32[64,128]{1,0:T(8,128)S(1)} %convert_bitcast_fusion.35, ...), kind=kLoop, calls=%fused_computation.345.clone.1 | loop fusion | flops 58695680 | bytes 573440 | tf_op jit(solution)/shard_map/while/body/eval_jaxpr/reduce_sum | solution.py:78
  615.9 14.8 %fusion.585 = (f32[64,128]{1,0:T(8,128)S(1)}, f32[64,128]{1,0:T(8,128)S(1)}, f32[64,128]{1,0:T(8,128)S(1)}) fusion(f32[64,128]{1,0:T(8,128)S(1)} %get-tuple-element.768, f32[64,128]{1,0:T(8,128)S(1)} %get-tuple-element.666, s32[64,128]{1,0:T(8,128)S(1)} %convert_bitcast_fusion.43, s32[64,128]{1,0:T(8,128)S(1)} %convert_bitcast_fusion.35, ...), kind=kLoop, calls=%fused_computation.349.clone.1 | loop fusion | flops 58695680 | bytes 573440 | tf_op jit(solution)/shard_map/while/body/eval_jaxpr/reduce_sum | solution.py:78
  635.1 14.8 %fusion.571 = (f32[64,128]{1,0:T(8,128)S(1)}, f32[64,128]{1,0:T(8,128)S(1)}, f32[64,128]{1,0:T(8,128)S(1)}) fusion(f32[64,128]{1,0:T(8,128)S(1)} %get-tuple-element.663, f32[64,128]{1,0:T(8,128)S(1)} %get-tuple-element.666, s32[64,128]{1,0:T(8,128)S(1)} %convert_bitcast_fusion.34, s32[64,128]{1,0:T(8,128)S(1)} %convert_bitcast_fusion.35, ...), kind=kLoop, calls=%fused_computation.317.clone.1 | loop fusion | flops 58695680 | bytes 573440 | tf_op jit(solution)/shard_map/while/body/eval_jaxpr/reduce_sum | solution.py:78
  650.0 14.8 %fusion.572 = (f32[64,128]{1,0:T(8,128)S(1)}, f32[64,128]{1,0:T(8,128)S(1)}, f32[64,128]{1,0:T(8,128)S(1)}) fusion(f32[64,128]{1,0:T(8,128)S(1)} %get-tuple-element.684, f32[64,128]{1,0:T(8,128)S(1)} %get-tuple-element.666, s32[64,128]{1,0:T(8,128)S(1)} %convert_bitcast_fusion.36, s32[64,128]{1,0:T(8,128)S(1)} %convert_bitcast_fusion.35, ...), kind=kLoop, calls=%fused_computation.321.clone.1 | loop fusion | flops 58695680 | bytes 573440 | tf_op jit(solution)/shard_map/while/body/eval_jaxpr/reduce_sum | solution.py:78
  664.9 14.8 %fusion.574 = (f32[64,128]{1,0:T(8,128)S(1)}, f32[64,128]{1,0:T(8,128)S(1)}, f32[64,128]{1,0:T(8,128)S(1)}) fusion(f32[64,128]{1,0:T(8,128)S(1)} %get-tuple-element.696, f32[64,128]{1,0:T(8,128)S(1)} %get-tuple-element.666, s32[64,128]{1,0:T(8,128)S(1)} %convert_bitcast_fusion.37, s32[64,128]{1,0:T(8,128)S(1)} %convert_bitcast_fusion.35, ...), kind=kLoop, calls=%fused_computation.325.clone.1 | loop fusion | flops 58695680 | bytes 573440 | tf_op jit(solution)/shard_map/while/body/eval_jaxpr/reduce_sum | solution.py:78
  679.7 14.8 %fusion.576 = (f32[64,128]{1,0:T(8,128)S(1)}, f32[64,128]{1,0:T(8,128)S(1)}, f32[64,128]{1,0:T(8,128)S(1)}) fusion(f32[64,128]{1,0:T(8,128)S(1)} %get-tuple-element.708, f32[64,128]{1,0:T(8,128)S(1)} %get-tuple-element.666, s32[64,128]{1,0:T(8,128)S(1)} %convert_bitcast_fusion.38, s32[64,128]{1,0:T(8,128)S(1)} %convert_bitcast_fusion.35, ...), kind=kLoop, calls=%fused_computation.329.clone.1 | loop fusion | flops 58695680 | bytes 573440 | tf_op jit(solution)/shard_map/while/body/eval_jaxpr/reduce_sum | solution.py:78
  694.6 13.6 %fusion.578 = (f32[64,128]{1,0:T(8,128)S(1)}, f32[64,128]{1,0:T(8,128)S(1)}, f32[64,128]{1,0:T(8,128)S(1)}) fusion(f32[64,128]{1,0:T(8,128)S(1)} %get-tuple-element.720, f32[64,128]{1,0:T(8,128)S(1)} %get-tuple-element.666, s32[64,128]{1,0:T(8,128)S(1)} %convert_bitcast_fusion.39, s32[64,128]{1,0:T(8,128)S(1)} %convert_bitcast_fusion.35, ...), kind=kLoop, calls=%fused_computation.333.clone.1 | loop fusion | flops 59744256 | bytes 589824 | tf_op jit(solution)/shard_map/while/body/eval_jaxpr/reduce_sum | solution.py:78
  708.4 14.8 %fusion.580 = (f32[64,128]{1,0:T(8,128)S(1)}, f32[64,128]{1,0:T(8,128)S(1)}, f32[64,128]{1,0:T(8,128)S(1)}) fusion(f32[64,128]{1,0:T(8,128)S(1)} %get-tuple-element.732, f32[64,128]{1,0:T(8,128)S(1)} %get-tuple-element.666, s32[64,128]{1,0:T(8,128)S(1)} %convert_bitcast_fusion.40, s32[64,128]{1,0:T(8,128)S(1)} %convert_bitcast_fusion.35, ...), kind=kLoop, calls=%fused_computation.337.clone.1 | loop fusion | flops 58695680 | bytes 573440 | tf_op jit(solution)/shard_map/while/body/eval_jaxpr/reduce_sum | solution.py:78
  723.2 14.8 %fusion.582 = (f32[64,128]{1,0:T(8,128)S(1)}, f32[64,128]{1,0:T(8,128)S(1)}, f32[64,128]{1,0:T(8,128)S(1)}) fusion(f32[64,128]{1,0:T(8,128)S(1)} %get-tuple-element.744, f32[64,128]{1,0:T(8,128)S(1)} %get-tuple-element.666, s32[64,128]{1,0:T(8,128)S(1)} %convert_bitcast_fusion.41, s32[64,128]{1,0:T(8,128)S(1)} %convert_bitcast_fusion.35, ...), kind=kLoop, calls=%fused_computation.341.clone.1 | loop fusion | flops 58695680 | bytes 573440 | tf_op jit(solution)/shard_map/while/body/eval_jaxpr/reduce_sum | solution.py:78
  738.1 14.8 %fusion.583 = (f32[64,128]{1,0:T(8,128)S(1)}, f32[64,128]{1,0:T(8,128)S(1)}, f32[64,128]{1,0:T(8,128)S(1)}) fusion(f32[64,128]{1,0:T(8,128)S(1)} %get-tuple-element.756, f32[64,128]{1,0:T(8,128)S(1)} %get-tuple-element.666, s32[64,128]{1,0:T(8,128)S(1)} %convert_bitcast_fusion.42, s32[64,128]{1,0:T(8,128)S(1)} %convert_bitcast_fusion.35, ...), kind=kLoop, calls=%fused_computation.345.clone.1 | loop fusion | flops 58695680 | bytes 573440 | tf_op jit(solution)/shard_map/while/body/eval_jaxpr/reduce_sum | solution.py:78
  753.0 14.8 %fusion.585 = (f32[64,128]{1,0:T(8,128)S(1)}, f32[64,128]{1,0:T(8,128)S(1)}, f32[64,128]{1,0:T(8,128)S(1)}) fusion(f32[64,128]{1,0:T(8,128)S(1)} %get-tuple-element.768, f32[64,128]{1,0:T(8,128)S(1)} %get-tuple-element.666, s32[64,128]{1,0:T(8,128)S(1)} %convert_bitcast_fusion.43, s32[64,128]{1,0:T(8,128)S(1)} %convert_bitcast_fusion.35, ...), kind=kLoop, calls=%fused_computation.349.clone.1 | loop fusion | flops 58695680 | bytes 573440 | tf_op jit(solution)/shard_map/while/body/eval_jaxpr/reduce_sum | solution.py:78
  767.9 4.7 copy.143
  775.2 11.0 %scatter-add.9 = f32[2,64,3,128]{2,3,1,0:T(8,128)} dynamic-update-slice(f32[2,64,3,128]{2,3,1,0:T(8,128)} %copy.143, f32[1,64,1,128]{2,3,1,0:T(8,128)} %copy.144, s32[]{:T(128)} %constant.433.clone.1, s32[]{:T(128)} %constant.432.clone.1, s32[]{:T(128)} %constant.432.clone.1, s32[]{:T(128)} %constant.432.clone.1) | dynamic-update-slice | bytes 65540 | tf_op jit(solution)/shard_map/scatter-add | solution.py:179
  786.2 12.2 %broadcast_select_fusion = (f32[2,64,3,128]{2,3,1,0:T(8,128)}, f32[2,64,3,128]{2,3,1,0:T(8,128)}) fusion(f32[2,64,3,128]{2,3,1,0:T(8,128)} %scatter-add.9, pred[2,64,128]{2,1,0:T(8,128)(4,1)S(1)} %iota_compare_fusion.5, f32[2,64,3,128]{2,3,1,0:T(8,128)} %get-tuple-element.293), kind=kLoop, calls=%fused_computation.532 | loop fusion | flops 196608 | bytes 802816 | tf_op jit(solution)/shard_map/jit(_where)/select_n | solution.py:186
  798.5 5.9 copy.146
  804.3 5.9 copy.147
  (239 shorter events, 37.6 us)
Async XLA Ops:
  0.6 12.9 %copy-start.3 = (f32[1,32,3,128]{3,1,2,0:T(8,128)S(1)}, f32[1,32,3,128]{3,1,2,0:T(8,128)}, u32[]{:S(2)}) copy-start(f32[1,32,3,128]{3,1,2,0:T(8,128)} %param.27) | copy-start | bytes 147460
  0.6 13.6 %copy-start.1 = (s32[1,32,128]{2,1,0:T(8,128)S(1)}, s32[1,32,128]{2,1,0:T(8,128)}, u32[]{:S(2)}) copy-start(s32[1,32,128]{2,1,0:T(8,128)} %param.28) | copy-start | bytes 49156
  0.7 13.5 %copy-start.8 = (s32[16]{0:T(128)S(1)}, s32[16]{0:T(128)}, u32[]{:S(2)}) copy-start(s32[16]{0:T(128)} %param.29) | copy-start | bytes 196
  0.7 17.5 %copy-start.9 = (s32[16]{0:T(128)S(1)}, s32[16]{0:T(128)}, u32[]{:S(2)}) copy-start(s32[16]{0:T(128)} %param.30) | copy-start | bytes 196
  0.7 17.6 %copy-start.10 = (s32[16]{0:T(128)S(1)}, s32[16]{0:T(128)}, u32[]{:S(2)}) copy-start(s32[16]{0:T(128)} %param.31) | copy-start | bytes 196
  3.0 438.6 %copy-start.2 = (f32[1,32,3,128]{3,1,2,0:T(8,128)}, f32[1,32,3,128]{3,1,2,0:T(8,128)S(1)}, u32[]{:S(2)}) copy-start(f32[1,32,3,128]{3,1,2,0:T(8,128)S(1)} %get-tuple-element.289) | copy-start | bytes 147460
  3.0 421.7 %collective-permute-start.5 = (f32[1,32,7,128]{3,1,2,0:T(8,128)S(1)}, f32[1,32,7,128]{3,1,2,0:T(8,128)S(1)}, u32[]{:S(2)}, u32[]{:S(2)}) collective-permute-start(f32[1,32,7,128]{3,1,2,0:T(8,128)S(1)} %get-tuple-element.422), channel_id=1, source_target_pairs={{32,0},{64,32},{96,64},{128,96},{160,128},{192,160},{224,192},{0,2... | collective-permute-start | bytes 344072 | tf_op jit(solution)/shard_map/ppermute | solution.py:28
  8.0 416.7 %collective-permute-start.4 = (f32[1,32,7,128]{3,1,2,0:T(8,128)S(1)}, f32[1,32,7,128]{3,1,2,0:T(8,128)S(1)}, u32[]{:S(2)}, u32[]{:S(2)}) collective-permute-start(f32[1,32,7,128]{3,1,2,0:T(8,128)S(1)} %get-tuple-element.422), channel_id=1, source_target_pairs={{0,32},{32,64},{64,96},{96,128},{128,160},{160,192},{192,224},{224... | collective-permute-start | bytes 344072 | tf_op jit(solution)/shard_map/ppermute | solution.py:26
  13.5 60.3 %copy-start.4 = (f32[2,64,3,128]{3,1,2,0:T(8,128)S(1)}, f32[2,64,3,128]{3,1,2,0:T(8,128)}, u32[]{:S(2)}) copy-start(f32[2,64,3,128]{3,1,2,0:T(8,128)} %param.20) | copy-start | bytes 589828
  73.8 4.6 copy-start.5
  78.5 4.7 copy-start.6
  83.1 4.7 copy-start
  311.1 175.1 %collective-permute-start.1 = (f32[1,64,7,128]{3,1,2,0:T(8,128)S(1)}, f32[1,64,7,128]{3,1,2,0:T(8,128)S(1)}, u32[]{:S(2)}, u32[]{:S(2)}) collective-permute-start(f32[1,64,7,128]{3,1,2,0:T(8,128)S(1)} %get-tuple-element.389), channel_id=1, source_target_pairs={{32,0},{64,32},{96,64},{128,96},{160,128},{192,160},{224,192},{33,... | collective-permute-start | bytes 688136 | tf_op jit(solution)/shard_map/ppermute | solution.py:28
  312.4 173.8 %collective-permute-start = (f32[1,64,7,128]{3,1,2,0:T(8,128)S(1)}, f32[1,64,7,128]{3,1,2,0:T(8,128)S(1)}, u32[]{:S(2)}, u32[]{:S(2)}) collective-permute-start(f32[1,64,7,128]{3,1,2,0:T(8,128)S(1)} %get-tuple-element.388), channel_id=1, source_target_pairs={{0,32},{32,64},{64,96},{96,128},{128,160},{160,192},{192,224},{1,3... | collective-permute-start | bytes 688136 | tf_op jit(solution)/shard_map/ppermute | solution.py:26
  325.8 5.9 copy-start.7
  325.8 90.9 %copy-start.11 = (f32[64]{0:T(128)S(1)}, f32[64]{0:T(128)}, u32[]{:S(2)}) copy-start(f32[64]{0:T(128)} %param.33) | copy-start | bytes 772
  424.8 16.6 %collective-permute-start.7 = (f32[3,1,7,128]{3,1,2,0:T(1,128)S(1)}, f32[3,1,7,128]{3,1,2,0:T(1,128)S(1)}, u32[]{:S(2)}, u32[]{:S(2)}) collective-permute-start(f32[3,1,7,128]{3,1,2,0:T(1,128)S(1)} %get-tuple-element.397), channel_id=1, source_target_pairs={{1,0},{2,1},{3,2},{4,3},{5,4},{6,5},{7,6},{8,7},{9,8},{10,9},{11,1... | collective-permute-start | bytes 32264 | tf_op jit(solution)/shard_map/ppermute | solution.py:28
  425.1 16.5 %collective-permute-start.6 = (f32[3,1,7,128]{3,1,2,0:T(1,128)S(1)}, f32[3,1,7,128]{3,1,2,0:T(1,128)S(1)}, u32[]{:S(2)}, u32[]{:S(2)}) collective-permute-start(f32[3,1,7,128]{3,1,2,0:T(1,128)S(1)} %get-tuple-element.396), channel_id=1, source_target_pairs={{0,1},{1,2},{2,3},{3,4},{4,5},{5,6},{6,7},{7,8},{8,9},{9,10},{10,1... | collective-permute-start | bytes 32264 | tf_op jit(solution)/shard_map/ppermute | solution.py:26
  486.3 6.9 collective-permute-start.3
  488.3 5.0 collective-permute-start.2
where the time goes:
time: 825 us; the launch traced here: 811 us
  other arithmetic  369 us (45%)
  local copies, waits for them, and re-layouts  273 us (33%)
  blocking collectives  132 us (16%)
  starting transfers between devices  27 us (3%)
    reduce_sum x27, other arithmetic, tile_forces(): jnp.sum(scalar * delta_x, axis=2)  330 us
    psum x1, blocking collectives, shards(): total_profile = lax.psum(profile, 'trans')  84.4 us
    scatter x1, local copies, waits for them, and re-layouts, shards(): main_pos.at[0, cell_ids, :, target_slot].set(payload[0:3].T, mode='drop')  54.2 us
    scatter x1, local copies, waits for them, and re-layouts, shards(): main_force.at[0, cell_ids, :, target_slot].set(payload[6:9].T, mode='drop')  54.1 us
    scatter x1, local copies, waits for them, and re-layouts, shards(): main_vel.at[0, cell_ids, :, target_slot].set(payload[3:6].T, mode='drop')  53.9 us
    all_gather x1, blocking collectives, shards(): gathered = lax.all_gather(arrived, 'trans', axis=1, tiled=True)  47.9 us
    unnamed x34, local copies, waits for them, and re-layouts  38.5 us
    scatter x1, local copies, waits for them, and re-layouts, shards(): main_seed.at[0, cell_ids, target_slot]  30.8 us
  transfers between devices with their start and end apart: 8, of which 0 were waited for; matrix products, arithmetic and copies ran while one was open for 41% of the time, Pallas kernels for 0%

commit v1 on v0

v1 whole, which is shorter than its diff:
```python
import jax
import jax.numpy as jnp
from jax import lax
from jax.experimental import pallas as pl
from jax.experimental.pallas import tpu as pltpu
from jax.sharding import PartitionSpec as P

BINS = 64
LANES = 128
SHARE = 4
CLASSES = LANES // SHARE

time_step = 0.01
repulsion = 25.0
friction = 4.5
noise_amp = 30.0
box_height = 16.0
seed_modulus = 4093
unit_spread = 3.4641016151377544

reach = 1.0005
nowhere = 1000.0
table_rate = 8.0
hash_shift = 2047.0 / 4093.0
noise_slope = noise_amp * unit_spread
noise_base = repulsion - noise_slope * 0.5 / 4093.0

VMEM = pltpu.VMEM
SMEM = pltpu.SMEM


def take(rows, lanes):
    return jnp.take_along_axis(rows, lanes, axis=1, mode="promise_in_bounds")


def lane_iota(rows):
    return lax.broadcasted_iota(jnp.int32, (rows, LANES), 1)


def centred(seed):
    code = seed + 1
    code = jnp.where(code > 2046, code - seed_modulus, code)
    return jnp.where(code > 2046, code - seed_modulus, code)


def start_kernel(row_ref, dest_ref, cell_ref, count_ref, pos_ref, vel_ref, force_ref, seed_ref,
                 bin_ref, out_ref, profile_ref):
    rows = row_ref.shape[0]
    lane3 = lane_iota(3)
    lane1 = lane_iota(1)
    parts = [jnp.zeros((3, LANES), jnp.float32) for _ in range(3)]
    tail = [jnp.zeros((1, LANES), jnp.float32) for _ in range(3)]
    for q in range(rows):
        cell = row_ref[q] // LANES
        slot = row_ref[q] % LANES
        hit = lane3 == slot
        for a, ref in enumerate((pos_ref, vel_ref, force_ref)):
            value = jnp.sum(jnp.where(hit, ref[0, cell], 0.0), axis=1, keepdims=True)
            parts[a] = jnp.where(lane3 == q, value, parts[a])
        seed = jnp.where(lane1 == slot, seed_ref[0, pl.ds(cell, 1), :].astype(jnp.float32), 0.0)
        seed = jnp.sum(seed, axis=1, keepdims=True)
        here = lane1 == q
        tail[0] = jnp.where(here, seed, tail[0])
        tail[1] = jnp.where(here, dest_ref[q].astype(jnp.float32), tail[1])
        tail[2] = jnp.where(here, cell_ref[q].astype(jnp.float32), tail[2])
    for a in range(3):
        out_ref[3 * a : 3 * a + 3, :] = parts[a][:, 0:rows]
        out_ref[9 + a : 10 + a, :] = tail[a][:, 0:rows]
    last = count_ref.shape[0] // 2
    bins = jnp.where(lane_iota(last) < count_ref[last:, :], bin_ref[...], BINS)
    lane = lane_iota(1)
    profile = jnp.zeros((1, LANES), jnp.float32)
    for b in range(BINS):
        hits = jnp.sum((bins == b).astype(jnp.float32), axis=0, keepdims=True)
        profile = jnp.where(lane == b, jnp.sum(hits, axis=1, keepdims=True), profile)
    profile_ref[...] = profile


def sorted_by(key, rows):
    lane = lane_iota(rows)
    load = lane
    size = 2
    while size <= LANES:
        dist = size // 2
        while dist >= 1:
            partner = lane ^ dist
            low = ((lane & size) == 0) == ((lane & dist) == 0)
            sign = jnp.where(low, 1.0, -1.0)
            other_key = take(key, partner)
            other_load = take(load, partner)
            swap = (other_key - key) * sign < 0.0
            key = jnp.where(swap, other_key, key)
            load = jnp.where(swap, other_load, load)
            dist //= 2
        size *= 2
    return key, load


def first_at_least(sorted_rows, bound, rows):
    at = jnp.zeros((rows, LANES), jnp.int32)
    step = LANES // 2
    while step >= 1:
        below = take(sorted_rows, at + (step - 1)) < bound
        at = jnp.where(below, at + step, at)
        step //= 2
    return jnp.where(take(sorted_rows, at) < bound, at + 1, at)


def prep_kernel(dest_ref, cell_ref, pay_ref, me_ref, count0_ref, count_ref,
                mpos_ref, mvel_ref, mforce_ref, mseed_ref,
                ppos_ref, pvel_ref, pforce_ref, pseed_ref,
                msort_ref, psort_ref, mraw_ref, praw_ref, mrank_ref, prank_ref,
                raw_ref, filled_ref):
    flow_rows, cells = mseed_ref.shape[0], mseed_ref.shape[1]
    sources = pay_ref.shape[0] // 256
    per = dest_ref.shape[0] // sources
    for f in range(flow_rows):
        for c in range(3):
            raw_ref[c, f * cells : (f + 1) * cells, :] = mpos_ref[f, :, c, :]
            raw_ref[3 + c, f * cells : (f + 1) * cells, :] = mvel_ref[f, :, c, :]
            raw_ref[6 + c, f * cells : (f + 1) * cells, :] = mforce_ref[f, :, c, :]
        seed = mseed_ref[f]
        occupied = lane_iota(cells) < count_ref[f * cells : (f + 1) * cells, :]
        raw_ref[9, f * cells : (f + 1) * cells, :] = jnp.where(occupied, seed, -1).astype(jnp.float32)

    me = me_ref[0]

    def fill(cell, carry):
        filled_ref[cell] = count0_ref[cell]
        return carry

    lax.fori_loop(0, cells, fill, 0)
    lane1 = lane_iota(1)

    def look(block, carry):
        start = block * 8
        found = dest_ref[start] == me
        for u in range(1, 8):
            found = found | (dest_ref[start + u] == me)

        @pl.when(found)
        def _():
            def one(u, inner):
                q = start + u

                @pl.when(dest_ref[q] == me)
                def _():
                    cell = cell_ref[q]
                    slot = filled_ref[cell]
                    filled_ref[cell] = slot + 1
                    origin = (q // per) * 256 + q % per
                    for c in range(10):
                        row = raw_ref[c, pl.ds(cell, 1), :]
                        raw_ref[c, pl.ds(cell, 1), :] = jnp.where(
                            lane1 == slot, pay_ref[origin + c * per], row
                        )

                return inner

            lax.fori_loop(0, 8, one, 0)

        return carry

    lax.fori_loop(0, dest_ref.shape[0] // 8, look, 0)

    def finish(state, seed, rows, sort_ref, rank_ref, raw_out, f, at):
        occupied = seed >= 0
        half = [state[3 + c] + 0.5 * time_step * state[6 + c] for c in range(3)]
        moved = [state[c] + time_step * half[c] for c in range(3)]
        for c in range(3):
            raw_out[c, at : at + rows, :] = moved[c]
            raw_out[3 + c, at : at + rows, :] = half[c]
        raw_out[6, at : at + rows, :] = seed.astype(jnp.float32)
        height = moved[2] - box_height * jnp.floor(moved[2] * (1.0 / box_height))
        key, order = sorted_by(jnp.where(occupied, height, nowhere), rows)
        _, rank = sorted_by(order.astype(jnp.float32), rows)
        rank_ref[at : at + rows, :] = rank
        hashed = centred(seed).astype(jnp.float32) / seed_modulus
        fields = [moved[0], moved[1], None] + [friction * v for v in half] + [hashed]
        for c, field in enumerate(fields):
            if field is None:
                sort_ref[c, f, :, :] = key
            else:
                sort_ref[c, f, :, :] = take(jnp.where(occupied, field, 0.0), order)
        edges = lane_iota(rows).astype(jnp.float32) * (1.0 / table_rate)
        sort_ref[7, f, :, :] = first_at_least(key, edges, rows).astype(jnp.float32)

    for f in range(flow_rows):
        at = f * cells
        state = [raw_ref[c, at : at + cells, :] for c in range(9)]
        finish(state, raw_ref[9, at : at + cells, :].astype(jnp.int32), cells,
               msort_ref, mrank_ref, mraw_ref, f, at)
    state = [ref[0, :, c, :] for ref in (ppos_ref, pvel_ref, pforce_ref) for c in range(3)]
    finish(state, pseed_ref[0], pseed_ref.shape[1], psort_ref, prank_ref, praw_ref, 0, 0)


def assemble(j_ref, sort_ref, below, above, left_ref, right_ref, shift, open_ends):
    fields, flow_rows, cells, _ = sort_ref.shape

    def keep(c, value, here):
        if open_ends is None or c != 2:
            return value
        return jnp.where(here, value, nowhere)

    for c in range(fields):
        for f in range(flow_rows):
            j_ref[c, 1 + f, 8 : 8 + cells, :] = sort_ref[c, f]
        ends = open_ends or (True,) * 4
        j_ref[c, 0, 8 : 8 + cells, :] = keep(c, below(c), ends[0])
        j_ref[c, 1 + flow_rows, 8 : 8 + cells, :] = keep(c, above(c), ends[1])
        for f in range(flow_rows + 2):
            inside_left, inside_right = ends[2], ends[3]
            if open_ends is not None and f == 0:
                inside_left, inside_right = ends[2] & ends[0], ends[3] & ends[0]
            if open_ends is not None and f == flow_rows + 1:
                inside_left, inside_right = ends[2] & ends[1], ends[3] & ends[1]
            j_ref[c, f, 7:8, :] = keep(c, left_ref[c, shift + f : shift + f + 1, :], inside_left)
            j_ref[c, f, 8 + cells : 9 + cells, :] = keep(
                c, right_ref[c, shift + f : shift + f + 1, :], inside_right
            )


def search(j_ref, f, cells, i_ref, base_ref, count_ref, held_ref, reach_ref, combo0):
    at = f * cells
    low = i_ref[2 * SHARE, at : at + cells, :]
    high = jnp.full((cells, LANES), -nowhere, jnp.float32)
    for v in range(SHARE):
        height = i_ref[2 * SHARE + v, at : at + cells, :]
        high = jnp.maximum(high, jnp.where(height < 500.0, height, -nowhere))
    used = low < 500.0
    low = jnp.where(used, low - reach, 0.0)
    high = jnp.where(used, high + reach, 0.0)
    below = low < 0.0
    above = high >= box_height
    low = jnp.where(below, low + box_height, low)
    high = jnp.where(above, high - box_height, high)
    low_bin = jnp.clip((low * table_rate).astype(jnp.int32), 0, LANES - 1)
    high_bin = jnp.floor(high * table_rate).astype(jnp.int32) + 1
    high_in = jnp.clip(high_bin, 0, LANES - 1)
    quarter = lane_iota(cells) // CLASSES
    most = jnp.zeros((cells, LANES), jnp.int32)
    for nb in range(9):
        df, dt = nb // 3, nb % 3
        heights = j_ref[2, f + df, 7 + dt : 7 + dt + cells, :]
        table = j_ref[7, f + df, 7 + dt : 7 + dt + cells, :]
        held = held_ref[f + df, 7 + dt : 7 + dt + cells, :]
        first = take(table, low_bin).astype(jnp.int32)
        step = (first < LANES - 1) & (take(heights, jnp.minimum(first + 1, LANES - 1)) < low)
        first = jnp.where(step, first + 2, first)
        step = (first < LANES) & (take(heights, jnp.minimum(first, LANES - 1)) < low)
        first = jnp.where(step, first + 1, first)
        last = jnp.where(high_bin >= LANES, held, take(table, high_in).astype(jnp.int32))
        step = (last >= 2) & (take(heights, jnp.maximum(last - 2, 0)) > high)
        last = jnp.where(step, last - 2, last)
        step = (last >= 1) & (take(heights, jnp.maximum(last - 1, 0)) > high)
        last = jnp.where(step, last - 1, last)
        first = jnp.where(below, first - held, first)
        last = jnp.where(above, last + held, last)
        count = jnp.where(used, last - first, 0)
        most = jnp.maximum(most, count)
        base_ref[combo0 + nb, at : at + cells, :] = first + quarter
        count_ref[combo0 + nb, at : at + cells, :] = count - quarter
    reach_ref[at : at + cells, :] = most


def pair_sums(j_ref, f, r0, i_ref, i0, base_ref, count_ref, held_ref, steps):
    beads = [[i_ref[c * SHARE + v, pl.ds(i0, 8), :] for c in range(7)] for v in range(SHARE)]

    def body(t, sums):
        sums = list(sums)
        k = t * SHARE
        for nb in range(9):
            df, dt = nb // 3, nb % 3
            rows = pl.ds(r0 + (7 + dt), 8)
            held = held_ref[f + df, rows, :]
            at = base_ref[nb, pl.ds(i0, 8), :] + k
            under, over = at < 0, at >= held
            lanes = (at + jnp.where(under, held, jnp.where(over, -held, 0))) & (LANES - 1)
            turn = jnp.where(under, -box_height, jnp.where(over, box_height, 0.0))
            turn = jnp.where(count_ref[nb, pl.ds(i0, 8), :] > k, turn, 10.0 * nowhere)
            other = [take(j_ref[c, f + df, rows, :], lanes) for c in range(7)]
            if df != 1:
                other[0] = other[0] + (df - 1.0)
            if dt != 1:
                other[1] = other[1] + (dt - 1.0)
            other[2] = other[2] + turn
            for v in range(SHARE):
                own = beads[v]
                dx, dy, dz = own[0] - other[0], own[1] - other[1], own[2] - other[2]
                dist_sq = jnp.maximum(dx * dx + dy * dy + dz * dz, 1e-30)
                weight = jnp.maximum(lax.rsqrt(dist_sq) - 1.0, 0.0)
                along = ((own[3] - other[3]) * dx + (own[4] - other[4]) * dy
                         + (own[5] - other[5]) * dz)
                ratio = own[6] * other[6] - hash_shift
                noise = ratio - jnp.round(ratio)
                scalar = weight * ((noise_slope * noise + noise_base) - weight * along)
                sums[v] = sums[v] + scalar * dx
                sums[SHARE + v] = sums[SHARE + v] + scalar * dy
                sums[2 * SHARE + v] = sums[2 * SHARE + v] + scalar * dz
        return tuple(sums)

    zero = jnp.zeros((8, LANES), jnp.float32)
    return lax.fori_loop(0, steps, body, (zero,) * (3 * SHARE))


def unsorted_sums(sums, rank):
    lanes = rank // SHARE
    which = rank % SHARE
    out = []
    for c in range(3):
        total = None
        for v in range(SHARE):
            part = sums[c * SHARE + v]
            part = part + pltpu.roll(part, LANES // 2, 1)
            part = part + pltpu.roll(part, LANES // 4, 1)
            part = take(part, lanes)
            total = part if total is None else jnp.where(which == v, part, total)
        out.append(total)
    return out


def arrange(i_ref, sort_ref, f, cells, at):
    lane = lane_iota(cells) % CLASSES
    for v in range(SHARE):
        lanes = lane * SHARE + v
        for c in range(7):
            field = take(sort_ref[c, f], lanes)
            if c == 6:
                field = jnp.round(field * seed_modulus)
            i_ref[c * SHARE + v, at : at + cells, :] = field


def force_kernel(end_ref, msort_ref, psort_ref, mraw_ref, praw_ref, mrank_ref, prank_ref,
                 below_ref, above_ref, left_ref, right_ref, bin_ref, push_ref,
                 mpos_out, mvel_out, mforce_out, ppos_out, pvel_out, pforce_out,
                 mj_ref, pj_ref, mi_ref, pi_ref, mbase_ref, mcount_ref, pbase_ref, pcount_ref,
                 mheld_ref, pheld_ref, mreach_ref, preach_ref, steps_ref):
    flow_rows, cells = msort_ref.shape[1], msort_ref.shape[2]
    prec_cells = psort_ref.shape[2]
    ends = tuple(end_ref[e] > 0 for e in range(4))
    assemble(mj_ref, msort_ref, lambda c: below_ref[c, 0:cells, :], lambda c: above_ref[c, 0:cells, :],
             left_ref, right_ref, 0, ends)
    assemble(pj_ref, psort_ref, lambda c: below_ref[c, cells : cells + prec_cells, :],
             lambda c: above_ref[c, cells : cells + prec_cells, :], left_ref, right_ref,
             flow_rows + 2, None)
    for j_ref, held_ref, n in ((mj_ref, mheld_ref, cells), (pj_ref, pheld_ref, prec_cells)):
        for f in range(held_ref.shape[0]):
            real = (j_ref[2, f, 0 : n + 16, :] < 500.0).astype(jnp.float32)
            held = jnp.sum(real, axis=1, keepdims=True).astype(jnp.int32)
            held_ref[f] = jnp.broadcast_to(held, (n + 16, LANES))
    for f in range(flow_rows):
        arrange(mi_ref, msort_ref, f, cells, f * cells)
    arrange(pi_ref, psort_ref, 0, prec_cells, 0)
    for f in range(flow_rows):
        search(mj_ref, f, cells, mi_ref, mbase_ref, mcount_ref, mheld_ref, mreach_ref, 0)
    search(pj_ref, 0, prec_cells, pi_ref, pbase_ref, pcount_ref, pheld_ref, preach_ref, 0)
    groups = flow_rows * cells // 8
    prec_groups = prec_cells // 8
    for g in range(groups):
        steps_ref[g] = (jnp.max(mreach_ref[8 * g : 8 * g + 8, :]) + (SHARE - 1)) // SHARE
    for g in range(prec_groups):
        steps_ref[groups + g] = (jnp.max(preach_ref[8 * g : 8 * g + 8, :]) + (SHARE - 1)) // SHARE

    def main_group(g, carry):
        f = g // (cells // 8)
        r0 = pl.multiple_of((g % (cells // 8)) * 8, 8)
        i0 = pl.multiple_of(g * 8, 8)
        sums = pair_sums(mj_ref, f, r0, mi_ref, i0, mbase_ref, mcount_ref, mheld_ref, steps_ref[g])
        force = unsorted_sums(sums, mrank_ref[pl.ds(i0, 8), :])
        occupied = mraw_ref[6, pl.ds(i0, 8), :] >= 0.0
        push = take(jnp.broadcast_to(push_ref[...], (8, LANES)), bin_ref[pl.ds(r0, 8), :])
        force[0] = force[0] + push * (f == flow_rows - 1).astype(jnp.float32)
        for c in range(3):
            half = mraw_ref[3 + c, pl.ds(i0, 8), :]
            mforce_out[f, pl.ds(r0, 8), c, :] = jnp.where(occupied, force[c], 0.0)
            mvel_out[f, pl.ds(r0, 8), c, :] = jnp.where(
                occupied, half + 0.5 * time_step * force[c], 0.0
            )
            mpos_out[f, pl.ds(r0, 8), c, :] = jnp.where(
                occupied, mraw_ref[c, pl.ds(i0, 8), :], 0.0
            )
        return carry

    def prec_group(g, carry):
        r0 = pl.multiple_of(g * 8, 8)
        sums = pair_sums(pj_ref, 0, r0, pi_ref, r0, pbase_ref, pcount_ref, pheld_ref,
                         steps_ref[groups + g])
        force = unsorted_sums(sums, prank_ref[pl.ds(r0, 8), :])
        for c in range(3):
            half = praw_ref[3 + c, pl.ds(r0, 8), :]
            pforce_out[0, pl.ds(r0, 8), c, :] = force[c]
            pvel_out[0, pl.ds(r0, 8), c, :] = half + 0.5 * time_step * force[c]
            ppos_out[0, pl.ds(r0, 8), c, :] = praw_ref[c, pl.ds(r0, 8), :]
        return carry

    lax.fori_loop(0, prec_groups, prec_group, 0)
    lax.fori_loop(0, groups, main_group, 0)


def whole(space, n):
    return [pl.BlockSpec(memory_space=space)] * n


def shape(dims, dtype=jnp.float32):
    return jax.ShapeDtypeStruct(dims, dtype)


def shards(
    main_pos,
    main_vel,
    main_force,
    main_seed,
    main_count,
    prec_pos,
    prec_vel,
    prec_force,
    prec_seed,
    cross_row,
    cross_dest,
    cross_cell,
    outlet_bin,
    outlet_coef,
):
    flow_rows, cells = main_seed.shape[0], main_seed.shape[1]
    prec_cells = prec_seed.shape[1]
    flow_index = lax.axis_index("flow")
    trans_index = lax.axis_index("trans")
    flow_devices = lax.axis_size("flow")
    trans_devices = lax.axis_size("trans")
    rows = cross_row.shape[0]
    count_column = main_count.reshape(flow_rows * cells, 1)
    big = pltpu.CompilerParams(vmem_limit_bytes=48 << 20)

    payload, profile = pl.pallas_call(
        start_kernel,
        out_shape=(shape((16, rows)), shape((1, LANES))),
        in_specs=whole(SMEM, 3) + whole(VMEM, 6),
        out_specs=tuple(whole(VMEM, 2)),
        compiler_params=big,
        name="start",
    )(cross_row, cross_dest, cross_cell, count_column, prec_pos, prec_vel, prec_force, prec_seed,
      outlet_bin)
    gathered = lax.all_gather(payload, "trans", axis=0)
    total_profile = lax.psum(profile[0, 0:BINS], "trans")
    density = total_profile * BINS / (cells * trans_devices * LANES)
    push = -outlet_coef * density
    push = jnp.where(flow_index == flow_devices - 1, push, 0.0)
    push = jnp.concatenate([push, jnp.zeros((LANES - BINS,), jnp.float32)])[None]
    dests = gathered[:, 10, :].reshape(-1).astype(jnp.int32)
    places = gathered[:, 11, :].reshape(-1).astype(jnp.int32)
    me = jnp.where(flow_index == 0, trans_index, -1).astype(jnp.int32)[None]

    total = flow_rows * cells
    msort, psort, mraw, praw, mrank, prank = pl.pallas_call(
        prep_kernel,
        out_shape=(
            shape((8, flow_rows, cells, LANES)),
            shape((8, 1, prec_cells, LANES)),
            shape((7, total, LANES)),
            shape((7, prec_cells, LANES)),
            shape((total, LANES), jnp.int32),
            shape((prec_cells, LANES), jnp.int32),
        ),
        in_specs=whole(SMEM, 5) + whole(VMEM, 9),
        out_specs=tuple(whole(VMEM, 6)),
        scratch_shapes=[VMEM((10, total, LANES), jnp.float32), SMEM((cells,), jnp.int32)],
        compiler_params=big,
        name="prep",
    )(dests, places, gathered.reshape(-1), me, main_count[0], count_column,
      main_pos, main_vel, main_force, main_seed, prec_pos, prec_vel, prec_force, prec_seed)

    def ring(value, axis, step):
        count = lax.axis_size(axis)
        return lax.ppermute(value, axis, [(i, (i + step) % count) for i in range(count)])

    top = jnp.concatenate([msort[:, flow_rows - 1], psort[:, 0]], axis=1)
    bottom = jnp.concatenate([msort[:, 0], psort[:, 0]], axis=1)
    below = ring(top, "flow", 1)
    above = ring(bottom, "flow", -1)

    def column(at_main, at_prec):
        return jnp.stack(
            [below[:, at_main]]
            + [msort[:, f, at_main] for f in range(flow_rows)]
            + [above[:, at_main], below[:, cells + at_prec], psort[:, 0, at_prec],
               above[:, cells + at_prec]],
            axis=1,
        )

    left = ring(column(cells - 1, prec_cells - 1), "trans", 1)
    right = ring(column(0, 0), "trans", -1)
    ends = jnp.stack([
        flow_index > 0,
        flow_index < flow_devices - 1,
        trans_index > 0,
        trans_index < trans_devices - 1,
    ]).astype(jnp.int32)

    out_main = shape((flow_rows, cells, 3, LANES))
    out_prec = shape((1, prec_cells, 3, LANES))
    return pl.pallas_call(
        force_kernel,
        out_shape=(out_main, out_main, out_main, out_prec, out_prec, out_prec),
        in_specs=whole(SMEM, 1) + whole(VMEM, 12),
        out_specs=tuple(whole(VMEM, 6)),
        scratch_shapes=[
            VMEM((8, flow_rows + 2, cells + 16, LANES), jnp.float32),
            VMEM((8, 3, prec_cells + 16, LANES), jnp.float32),
            VMEM((7 * SHARE, total, LANES), jnp.float32),
            VMEM((7 * SHARE, prec_cells, LANES), jnp.float32),
            VMEM((9, total, LANES), jnp.int32),
            VMEM((9, total, LANES), jnp.int32),
            VMEM((9, prec_cells, LANES), jnp.int32),
            VMEM((9, prec_cells, LANES), jnp.int32),
            VMEM((flow_rows + 2, cells + 16, LANES), jnp.int32),
            VMEM((3, prec_cells + 16, LANES), jnp.int32),
            VMEM((total, LANES), jnp.int32),
            VMEM((prec_cells, LANES), jnp.int32),
            SMEM((total // 8 + prec_cells // 8,), jnp.int32),
        ],
        compiler_params=big,
        name="force",
    )(ends, msort, psort, mraw, praw, mrank, prank, below, above, left, right, outlet_bin, push)


def solution(mesh):
    return jax.shard_map(
        shards,
        mesh=mesh,
        in_specs=(
            P("flow", "trans", None, None),
            P("flow", "trans", None, None),
            P("flow", "trans", None, None),
            P("flow", "trans", None),
            P("flow", "trans"),
            P("flow", "trans", None, None),
            P("flow", "trans", None, None),
            P("flow", "trans", None, None),
            P("flow", "trans", None),
            P("trans"),
            P("trans"),
            P("trans"),
            P("trans", None),
            P(),
        ),
        out_specs=(
            P("flow", "trans", None, None),
            P("flow", "trans", None, None),
            P("flow", "trans", None, None),
            P("flow", "trans", None, None),
            P("flow", "trans", None, None),
            P("flow", "trans", None, None),
        ),
        check_vma=False,
    )
```

time: 825 us -> 218 us (0.26)
  the two profiles are of different devices: /device:TPU:1 before, /device:TPU:231 now
where the time goes in v1:
time: 218 us
  blocking collectives  116 us (53%)
  Pallas kernels  72.1 us (33%)
  local copies, waits for them, and re-layouts  11.2 us (5%)
  starting transfers between devices  10.1 us (5%)
  waiting for transfers between devices  7.47 us (3%)
    psum x1, blocking collectives, shards(): total_profile = lax.psum(profile[0, 0:BINS], 'trans')  76.6 us
    pallas_call x1, Pallas kernels, shards(): pl.pallas_call(force_kernel, out_shape=(out_main, out_main, out_main, out...  63.2 us
    all_gather x1, blocking collectives, shards(): gathered = lax.all_gather(payload, 'trans', axis=0)  39.2 us
    ppermute x4, starting transfers between devices, ring(): lax.ppermute(value, axis, [(i, (i + step) % count) for i in range(count)])  10.1 us
    pallas_call x1, Pallas kernels, shards(): pl.pallas_call(prep_kernel, out_shape=(shape((8, flow_rows, cells, LANES)...  7.81 us
    ppermute x4, waiting for transfers between devices, ring(): lax.ppermute(value, axis, [(i, (i + step) % count) for i in range(count)])  7.47 us
    unnamed x34, local copies, waits for them, and re-layouts  6.25 us
  transfers between devices with their start and end apart: 4, of which 2 were waited for; matrix products, arithmetic and copies ran while one was open for 0% of the time, Pallas kernels for 0%

profile of v1, /device:TPU:231, one launch (start us, length us, event | category | flops | bytes accessed | tf_op | source)
XLA Modules:
  0.0 217.7 jit_solution(9248771126928887363)
XLA Ops:
  0.6 0.0 copy-start.12
  0.6 0.0 copy-start.9
  0.7 0.7 copy-done.12
  1.3 0.1 reshape.24.count_ref
  1.5 0.0 copy-done.9
  1.5 0.0 copy-start.10
  1.5 0.7 copy-done.10
  2.3 0.8 copy-done.11
  3.1 0.0 copy-start.5
  3.1 0.7 copy-done
  3.8 0.0 copy-done.3
  3.8 0.0 copy-done.5
  3.8 1.0 start.1
  4.9 39.2 %all-gather = f32[512,16]{1,0:T(8,128)S(1)} all-gather(f32[16,16]{1,0:T(8,128)S(1)} %get-tuple-element.14), channel_id=2, replica_groups=mesh['flow'=8,'trans'=32] {'trans'}, dimensions={0}, use_global_device_ids=true | all-gather | bytes 33792 | tf_op jit(solution)/shard_map/all_gather | solution.py:443
  44.1 0.1 reshape.21.pay_ref
  44.3 0.1 convert_element_type.17.cell_ref
  44.4 0.1 convert_element_type.15.dest_ref
  44.5 0.6 copy-done.6
  45.0 0.1 copy.52.mpos_ref
  45.2 0.8 copy-done.7
  46.0 0.1 copy.53.mvel_ref
  46.1 0.8 copy-done.8
  46.9 0.1 copy.54.mforce_ref
  47.0 0.7 copy-done.2
  47.7 7.8 %prep.1 = (f32[8,2,64,128]{3,2,1,0:T(8,128)S(1)}, f32[8,1,32,128]{3,2,1,0:T(8,128)S(1)}, f32[7,128,128]{2,1,0:T(8,128)S(1)}, f32[7,32,128]{2,1,0:T(8,128)S(1)}, ...) custom-call(s32[512]{0:T(512)S(1)} %convert_element_type.15.dest_ref, s32[512]{0:T(512)S(1)} %convert_element_type.17.cell_ref, ...), custom_call_target="tpu_custom_call" | custom-call | tf_op jit(solution)/shard_map/prep/pallas_call | solution.py:454
  55.6 0.1 pad_maximum_fusion
  55.7 3.3 %collective-permute-start.1 = (f32[8,96,128]{2,1,0:T(8,128)S(1)}, f32[8,96,128]{2,1,0:T(8,128)S(1)}, u32[]{:S(2)}, u32[]{:S(2)}) collective-permute-start(f32[8,96,128]{2,1,0:T(8,128)S(1)} %get-tuple-element.52), channel_id=1, source_target_pairs={{0,224},{32,0},{64,32},{96,64},{128,96},{160,128},{192,160},{224,1... | collective-permute-start | bytes 1179656 | tf_op jit(solution)/shard_map/ppermute | solution.py:474
  58.9 0.0 collective-permute-start
  58.9 0.1 copy.62
  59.0 0.3 copy.60
  59.4 0.0 copy-start.13
  59.4 76.6 %psum.7 = f32[64]{0:T(128)S(1)} all-reduce(f32[64]{0:T(128)S(1)} %slice_bitcast_fusion.2), channel_id=1, replica_groups=mesh['flow'=8,'trans'=32] {'trans'}, use_global_device_ids=true, to_apply=%region_0.0 | all-reduce | flops 64 | bytes 512 | tf_op jit(solution)/shard_map/psum | solution.py:444
  136.0 0.0 collective-permute-done.1.above_ref
  136.0 0.0 collective-permute-done.below_ref
  136.0 0.1 stack.26
  136.1 6.6 %collective-permute-start.2 = (f32[8,7,128]{2,1,0:T(8,128)S(1)}, f32[8,7,128]{2,1,0:T(8,128)S(1)}, u32[]{:S(2)}, u32[]{:S(2)}) collective-permute-start(f32[8,7,128]{2,1,0:T(8,128)S(1)} %stack.26), channel_id=1, source_target_pairs={{0,1},{1,2},{2,3},{3,4},{4,5},{5,6},{6,7},{7,8},{8,9},{9,10},{10,1... | collective-permute-start | bytes 86024 | tf_op jit(solution)/shard_map/ppermute | solution.py:474
  142.7 0.1 stack.27
  142.7 0.3 collective-permute-start.3
  143.0 0.1 add_convert_fusion.end_ref
  143.1 0.6 collective-permute-done.2.left_ref
  143.7 6.8 %collective-permute-done.3.right_ref = f32[8,7,128]{2,1,0:T(8,128)S(1)} collective-permute-done((f32[8,7,128]{2,1,0:T(8,128)S(1)}, f32[8,7,128]{2,1,0:T(8,128)S(1)}, u32[]{:S(2)}, u32[]{:S(2)}) %collective-permute-start.3) | collective-permute-done | bytes 28704 | tf_op jit(solution)/shard_map/ppermute | solution.py:474
  150.5 63.2 %force.1 = (f32[2,64,3,128]{3,2,1,0:T(4,128)S(1)}, f32[2,64,3,128]{3,2,1,0:T(4,128)S(1)}, f32[2,64,3,128]{3,2,1,0:T(4,128)S(1)}, f32[1,32,3,128]{3,2,1,0:T(4,128...) custom-call(s32[4]{0:T(128)S(1)} %add_convert_fusion.end_ref, ...), custom_call_target="tpu_custom_call" | custom-call | tf_op jit(solution)/shard_map/force/pallas_call | solution.py:501
  213.8 0.7 copy.66
  214.5 0.6 copy.69
  215.1 0.6 copy.70
  215.7 0.6 copy.71
  216.3 0.7 copy.67
  217.0 0.7 copy.68
  (27 shorter events, 0.3 us)
Async XLA Ops:
  0.6 0.7 copy-start.12
  0.6 0.8 copy-start.9
  1.5 0.8 copy-start.10
  2.3 0.8 copy-start.11
  3.1 0.8 copy-start
  3.1 0.8 copy-start.1
  3.1 0.8 copy-start.3
  3.1 0.8 copy-start.4
  3.1 0.8 copy-start.5
  44.1 0.9 copy-start.6
  45.0 0.9 copy-start.7
  46.0 0.9 copy-start.8
  46.9 0.8 copy-start.2
  55.7 80.3 %collective-permute-start.1 = (f32[8,96,128]{2,1,0:T(8,128)S(1)}, f32[8,96,128]{2,1,0:T(8,128)S(1)}, u32[]{:S(2)}, u32[]{:S(2)}) collective-permute-start(f32[8,96,128]{2,1,0:T(8,128)S(1)} %get-tuple-element.52), channel_id=1, source_target_pairs={{0,224},{32,0},{64,32},{96,64},{128,96},{160,128},{192,160},{224,1... | collective-permute-start | bytes 1179656 | tf_op jit(solution)/shard_map/ppermute | solution.py:474
  58.9 77.1 %collective-permute-start = (f32[8,96,128]{2,1,0:T(8,128)S(1)}, f32[8,96,128]{2,1,0:T(8,128)S(1)}, u32[]{:S(2)}, u32[]{:S(2)}) collective-permute-start(f32[8,96,128]{2,1,0:T(8,128)S(1)} %get-tuple-element.53), channel_id=1, source_target_pairs={{0,32},{32,64},{64,96},{96,128},{128,160},{160,192},{192,224},{224... | collective-permute-start | bytes 1179656 | tf_op jit(solution)/shard_map/ppermute | solution.py:474
  59.4 76.6 %copy-start.13 = (f32[64]{0:T(128)S(1)}, f32[64]{0:T(128)}, u32[]{:S(2)}) copy-start(f32[64]{0:T(128)} %param.27) | copy-start | bytes 772
  136.1 7.6 %collective-permute-start.2 = (f32[8,7,128]{2,1,0:T(8,128)S(1)}, f32[8,7,128]{2,1,0:T(8,128)S(1)}, u32[]{:S(2)}, u32[]{:S(2)}) collective-permute-start(f32[8,7,128]{2,1,0:T(8,128)S(1)} %stack.26), channel_id=1, source_target_pairs={{0,1},{1,2},{2,3},{3,4},{4,5},{5,6},{6,7},{7,8},{8,9},{9,10},{10,1... | collective-permute-start | bytes 86024 | tf_op jit(solution)/shard_map/ppermute | solution.py:474
  142.7 7.8 %collective-permute-start.3 = (f32[8,7,128]{2,1,0:T(8,128)S(1)}, f32[8,7,128]{2,1,0:T(8,128)S(1)}, u32[]{:S(2)}, u32[]{:S(2)}) collective-permute-start(f32[8,7,128]{2,1,0:T(8,128)S(1)} %stack.27), channel_id=1, source_target_pairs={{0,31},{1,0},{2,1},{3,2},{4,3},{5,4},{6,5},{7,6},{8,7},{9,8},{10,9... | collective-permute-start | bytes 86024 | tf_op jit(solution)/shard_map/ppermute | solution.py:474

commit v2 on v1

--- a/solution.py
+++ b/solution.py
@@ -44,36 +44,111 @@
 
 
 def start_kernel(row_ref, dest_ref, cell_ref, count_ref, pos_ref, vel_ref, force_ref, seed_ref,
-                 bin_ref, out_ref, profile_ref):
+                 bin_ref, out_ref):
     rows = row_ref.shape[0]
-    lane3 = lane_iota(3)
-    lane1 = lane_iota(1)
-    parts = [jnp.zeros((3, LANES), jnp.float32) for _ in range(3)]
-    tail = [jnp.zeros((1, LANES), jnp.float32) for _ in range(3)]
+    lane = lane_iota(1)
+    lines = [jnp.zeros((1, LANES), jnp.float32) for _ in range(2)]
+
+    def put(field, q, value):
+        at = field * rows + q
+        lines[at // LANES] = jnp.where(lane == at % LANES, value, lines[at // LANES])
+
     for q in range(rows):
         cell = row_ref[q] // LANES
         slot = row_ref[q] % LANES
-        hit = lane3 == slot
+        hit = lane == slot
         for a, ref in enumerate((pos_ref, vel_ref, force_ref)):
-            value = jnp.sum(jnp.where(hit, ref[0, cell], 0.0), axis=1, keepdims=True)
-            parts[a] = jnp.where(lane3 == q, value, parts[a])
-        seed = jnp.where(lane1 == slot, seed_ref[0, pl.ds(cell, 1), :].astype(jnp.float32), 0.0)
-        seed = jnp.sum(seed, axis=1, keepdims=True)
-        here = lane1 == q
-        tail[0] = jnp.where(here, seed, tail[0])
-        tail[1] = jnp.where(here, dest_ref[q].astype(jnp.float32), tail[1])
-        tail[2] = jnp.where(here, cell_ref[q].astype(jnp.float32), tail[2])
-    for a in range(3):
-        out_ref[3 * a : 3 * a + 3, :] = parts[a][:, 0:rows]
-        out_ref[9 + a : 10 + a, :] = tail[a][:, 0:rows]
+            for c in range(3):
+                value = jnp.where(hit, ref[0, c, pl.ds(cell, 1), :], 0.0)
+                put(3 * a + c, q, jnp.sum(value, axis=1, keepdims=True))
+        seed = jnp.where(hit, seed_ref[0, pl.ds(cell, 1), :].astype(jnp.float32), 0.0)
+        put(9, q, jnp.sum(seed, axis=1, keepdims=True))
+        put(10, q, dest_ref[q].astype(jnp.float32))
+        put(11, q, cell_ref[q].astype(jnp.float32))
     last = count_ref.shape[0] // 2
     bins = jnp.where(lane_iota(last) < count_ref[last:, :], bin_ref[...], BINS)
-    lane = lane_iota(1)
     profile = jnp.zeros((1, LANES), jnp.float32)
     for b in range(BINS):
         hits = jnp.sum((bins == b).astype(jnp.float32), axis=0, keepdims=True)
         profile = jnp.where(lane == b, jnp.sum(hits, axis=1, keepdims=True), profile)
-    profile_ref[...] = profile
+    out_ref[...] = jnp.zeros(out_ref.shape, jnp.float32)
+    out_ref[0:1, :] = lines[0]
+    out_ref[1:2, :] = lines[1]
+    out_ref[2:3, :] = profile
+
+
+def exchange_kernel(own_ref, out_ref, send_sem, recv_sem):
+    me = lax.axis_index("trans")
+    count = out_ref.shape[0]
+    barrier = pltpu.get_barrier_semaphore()
+
+    def greet(s, carry):
+        pl.semaphore_signal(barrier, inc=1, device_id={"trans": lax.rem(me + s, count)},
+                            device_id_type=pl.DeviceIdType.MESH)
+        return carry
+
+    lax.fori_loop(1, count, greet, 0)
+    pl.semaphore_wait(barrier, count - 1)
+
+    def copy(s, slot):
+        return pltpu.make_async_remote_copy(
+            src_ref=own_ref, dst_ref=out_ref.at[slot], send_sem=send_sem.at[s],
+            recv_sem=recv_sem.at[slot], device_id={"trans": lax.rem(me + s, count)},
+            device_id_type=pl.DeviceIdType.MESH)
+
+    def send(s, carry):
+        copy(s, me).start()
+        return carry
+
+    def finish(s, carry):
+        copy(s, lax.rem(me + count - s, count)).wait_recv()
+        copy(s, me).wait_send()
+        return carry
+
+    lax.fori_loop(1, count, send, 0)
+    out_ref[me] = own_ref[...]
+    lax.fori_loop(1, count, finish, 0)
+
+
+def halo_kernel(msort_ref, psort_ref, left_ref, right_ref, below_ref, above_ref, side_ref,
+                send_sem, recv_sem):
+    flow, trans = lax.axis_index("flow"), lax.axis_index("trans")
+    flows, transes = lax.axis_size("flow"), lax.axis_size("trans")
+    flow_rows, cells = msort_ref.shape[1], msort_ref.shape[2]
+    prec_cells = psort_ref.shape[2]
+
+    def at(df, dt):
+        return (lax.rem(flow + flows + df, flows), lax.rem(trans + transes + dt, transes))
+
+    mesh_id = pl.DeviceIdType.MESH
+    barrier = pltpu.get_barrier_semaphore()
+    around = [(df, dt) for df in (-1, 0, 1) for dt in (-1, 0, 1) if (df, dt) != (0, 0)]
+    for df, dt in around:
+        pl.semaphore_signal(barrier, inc=1, device_id=at(df, dt), device_id_type=mesh_id)
+    pl.semaphore_wait(barrier, len(around))
+    main_part, prec_part = pl.ds(0, cells), pl.ds(cells, prec_cells)
+    plan = [
+        (msort_ref.at[:, flow_rows - 1], below_ref.at[:, main_part], (1, 0)),
+        (msort_ref.at[:, 0], above_ref.at[:, main_part], (-1, 0)),
+        (psort_ref.at[:, 0], below_ref.at[:, prec_part], (1, 0)),
+        (psort_ref.at[:, 0], above_ref.at[:, prec_part], (-1, 0)),
+        (right_ref, side_ref.at[0], (0, 1)),
+        (right_ref, side_ref.at[1], (1, 1)),
+        (right_ref, side_ref.at[2], (-1, 1)),
+        (left_ref, side_ref.at[3], (0, -1)),
+        (left_ref, side_ref.at[4], (1, -1)),
+        (left_ref, side_ref.at[5], (-1, -1)),
+    ]
+    copies = [
+        pltpu.make_async_remote_copy(src_ref=src, dst_ref=dst, send_sem=send_sem.at[n],
+                                     recv_sem=recv_sem.at[n], device_id=at(*step),
+                                     device_id_type=mesh_id)
+        for n, (src, dst, step) in enumerate(plan)
+    ]
+    for copy in copies:
+        copy.start()
+    for copy in copies:
+        copy.wait()
 
 
 def sorted_by(key, rows):
@@ -106,19 +181,22 @@
     return jnp.where(take(sorted_rows, at) < bound, at + 1, at)
 
 
-def prep_kernel(dest_ref, cell_ref, pay_ref, me_ref, count0_ref, count_ref,
+def prep_kernel(pay_ref, me_ref, count0_ref, share_ref, count_ref, coef_ref, got_ref,
                 mpos_ref, mvel_ref, mforce_ref, mseed_ref,
                 ppos_ref, pvel_ref, pforce_ref, pseed_ref,
                 msort_ref, psort_ref, mraw_ref, praw_ref, mrank_ref, prank_ref,
-                raw_ref, filled_ref):
+                left_ref, right_ref, push_ref, raw_ref, filled_ref):
     flow_rows, cells = mseed_ref.shape[0], mseed_ref.shape[1]
-    sources = pay_ref.shape[0] // 256
-    per = dest_ref.shape[0] // sources
+    sources = got_ref.shape[0]
+    stride = pay_ref.shape[0] // sources
+    per = 16
+    profile = jnp.sum(got_ref[:, 2:3, :], axis=0)
+    push_ref[...] = -coef_ref[...] * (profile * share_ref[0])
     for f in range(flow_rows):
         for c in range(3):
-            raw_ref[c, f * cells : (f + 1) * cells, :] = mpos_ref[f, :, c, :]
-            raw_ref[3 + c, f * cells : (f + 1) * cells, :] = mvel_ref[f, :, c, :]
-            raw_ref[6 + c, f * cells : (f + 1) * cells, :] = mforce_ref[f, :, c, :]
+            raw_ref[c, f * cells : (f + 1) * cells, :] = mpos_ref[f, c]
+            raw_ref[3 + c, f * cells : (f + 1) * cells, :] = mvel_ref[f, c]
+            raw_ref[6 + c, f * cells : (f + 1) * cells, :] = mforce_ref[f, c]
         seed = mseed_ref[f]
         occupied = lane_iota(cells) < count_ref[f * cells : (f + 1) * cells, :]
         raw_ref[9, f * cells : (f + 1) * cells, :] = jnp.where(occupied, seed, -1).astype(jnp.float32)
@@ -132,23 +210,22 @@
     lax.fori_loop(0, cells, fill, 0)
     lane1 = lane_iota(1)
 
-    def look(block, carry):
-        start = block * 8
-        found = dest_ref[start] == me
-        for u in range(1, 8):
-            found = found | (dest_ref[start + u] == me)
+    def look(source, carry):
+        start = source * stride
+        found = pay_ref[start + 10 * per] == me
+        for u in range(1, per):
+            found = found | (pay_ref[start + 10 * per + u] == me)
 
         @pl.when(found)
         def _():
             def one(u, inner):
-                q = start + u
-
-                @pl.when(dest_ref[q] == me)
+                origin = start + u
+
+                @pl.when(pay_ref[origin + 10 * per] == me)
                 def _():
-                    cell = cell_ref[q]
+                    cell = pay_ref[origin + 11 * per].astype(jnp.int32)
                     slot = filled_ref[cell]
                     filled_ref[cell] = slot + 1
-                    origin = (q // per) * 256 + q % per
                     for c in range(10):
                         row = raw_ref[c, pl.ds(cell, 1), :]
                         raw_ref[c, pl.ds(cell, 1), :] = jnp.where(
@@ -157,11 +234,13 @@
 
                 return inner
 
-            lax.fori_loop(0, 8, one, 0)
+            lax.fori_loop(0, per, one, 0)
 
         return carry
 
-    lax.fori_loop(0, dest_ref.shape[0] // 8, look, 0)
+    @pl.when(me >= 0.0)
+    def _():
+        lax.fori_loop(0, sources, look, 0)
 
     def finish(state, seed, rows, sort_ref, rank_ref, raw_out, f, at):
         occupied = seed >= 0
@@ -190,11 +269,20 @@
         state = [raw_ref[c, at : at + cells, :] for c in range(9)]
         finish(state, raw_ref[9, at : at + cells, :].astype(jnp.int32), cells,
                msort_ref, mrank_ref, mraw_ref, f, at)
-    state = [ref[0, :, c, :] for ref in (ppos_ref, pvel_ref, pforce_ref) for c in range(3)]
-    finish(state, pseed_ref[0], pseed_ref.shape[1], psort_ref, prank_ref, praw_ref, 0, 0)
-
-
-def assemble(j_ref, sort_ref, below, above, left_ref, right_ref, shift, open_ends):
+    state = [ref[0, c] for ref in (ppos_ref, pvel_ref, pforce_ref) for c in range(3)]
+    prec_cells = pseed_ref.shape[1]
+    finish(state, pseed_ref[0], prec_cells, psort_ref, prank_ref, praw_ref, 0, 0)
+    left_ref[...] = jnp.zeros(left_ref.shape, jnp.float32)
+    right_ref[...] = jnp.zeros(right_ref.shape, jnp.float32)
+    for c in range(msort_ref.shape[0]):
+        for f in range(flow_rows):
+            left_ref[c, f : f + 1, :] = msort_ref[c, f, 0:1, :]
+            right_ref[c, f : f + 1, :] = msort_ref[c, f, cells - 1 : cells, :]
+        left_ref[c, flow_rows : flow_rows + 1, :] = psort_ref[c, 0, 0:1, :]
+        right_ref[c, flow_rows : flow_rows + 1, :] = psort_ref[c, 0, prec_cells - 1 : prec_cells, :]
+
+
+def assemble(j_ref, sort_ref, below, above, side_ref, shift, open_ends):
     fields, flow_rows, cells, _ = sort_ref.shape
 
     def keep(c, value, here):
@@ -214,9 +302,11 @@
                 inside_left, inside_right = ends[2] & ends[0], ends[3] & ends[0]
             if open_ends is not None and f == flow_rows + 1:
                 inside_left, inside_right = ends[2] & ends[1], ends[3] & ends[1]
-            j_ref[c, f, 7:8, :] = keep(c, left_ref[c, shift + f : shift + f + 1, :], inside_left)
+            part = 1 if f == 0 else 2 if f == flow_rows + 1 else 0
+            row = shift + (flow_rows - 1 if f == 0 else 0 if f == flow_rows + 1 else f - 1)
+            j_ref[c, f, 7:8, :] = keep(c, side_ref[part, c, row : row + 1, :], inside_left)
             j_ref[c, f, 8 + cells : 9 + cells, :] = keep(
-                c, right_ref[c, shift + f : shift + f + 1, :], inside_right
+                c, side_ref[3 + part, c, row : row + 1, :], inside_right
             )
 
 
@@ -331,7 +421,7 @@
 
 
 def force_kernel(end_ref, msort_ref, psort_ref, mraw_ref, praw_ref, mrank_ref, prank_ref,
-                 below_ref, above_ref, left_ref, right_ref, bin_ref, push_ref,
+                 below_ref, above_ref, side_ref, bin_ref, push_ref,
                  mpos_out, mvel_out, mforce_out, ppos_out, pvel_out, pforce_out,
                  mj_ref, pj_ref, mi_ref, pi_ref, mbase_ref, mcount_ref, pbase_ref, pcount_ref,
                  mheld_ref, pheld_ref, mreach_ref, preach_ref, steps_ref):
@@ -339,10 +429,10 @@
     prec_cells = psort_ref.shape[2]
     ends = tuple(end_ref[e] > 0 for e in range(4))
     assemble(mj_ref, msort_ref, lambda c: below_ref[c, 0:cells, :], lambda c: above_ref[c, 0:cells, :],
-             left_ref, right_ref, 0, ends)
+             side_ref, 0, ends)
     assemble(pj_ref, psort_ref, lambda c: below_ref[c, cells : cells + prec_cells, :],
-             lambda c: above_ref[c, cells : cells + prec_cells, :], left_ref, right_ref,
-             flow_rows + 2, None)
+             lambda c: above_ref[c, cells : cells + prec_cells, :], side_ref,
+             flow_rows, None)
     for j_ref, held_ref, n in ((mj_ref, mheld_ref, cells), (pj_ref, pheld_ref, prec_cells)):
         for f in range(held_ref.shape[0]):
             real = (j_ref[2, f, 0 : n + 16, :] < 500.0).astype(jnp.float32)
@@ -372,11 +462,11 @@
         force[0] = force[0] + push * (f == flow_rows - 1).astype(jnp.float32)
         for c in range(3):
             half = mraw_ref[3 + c, pl.ds(i0, 8), :]
-            mforce_out[f, pl.ds(r0, 8), c, :] = jnp.where(occupied, force[c], 0.0)
-            mvel_out[f, pl.ds(r0, 8), c, :] = jnp.where(
+            mforce_out[f, c, pl.ds(r0, 8), :] = jnp.where(occupied, force[c], 0.0)
+            mvel_out[f, c, pl.ds(r0, 8), :] = jnp.where(
                 occupied, half + 0.5 * time_step * force[c], 0.0
             )
-            mpos_out[f, pl.ds(r0, 8), c, :] = jnp.where(
+            mpos_out[f, c, pl.ds(r0, 8), :] = jnp.where(
                 occupied, mraw_ref[c, pl.ds(i0, 8), :], 0.0
             )
         return carry
@@ -388,9 +478,9 @@
         force = unsorted_sums(sums, prank_ref[pl.ds(r0, 8), :])
         for c in range(3):
             half = praw_ref[3 + c, pl.ds(r0, 8), :]
-            pforce_out[0, pl.ds(r0, 8), c, :] = force[c]
-            pvel_out[0, pl.ds(r0, 8), c, :] = half + 0.5 * time_step * force[c]
-            ppos_out[0, pl.ds(r0, 8), c, :] = praw_ref[c, pl.ds(r0, 8), :]
+            pforce_out[0, c, pl.ds(r0, 8), :] = force[c]
+            pvel_out[0, c, pl.ds(r0, 8), :] = half + 0.5 * time_step * force[c]
+            ppos_out[0, c, pl.ds(r0, 8), :] = praw_ref[c, pl.ds(r0, 8), :]
         return carry
 
     lax.fori_loop(0, prec_groups, prec_group, 0)
@@ -427,31 +517,43 @@
     trans_index = lax.axis_index("trans")
     flow_devices = lax.axis_size("flow")
     trans_devices = lax.axis_size("trans")
-    rows = cross_row.shape[0]
-    count_column = main_count.reshape(flow_rows * cells, 1)
+    total = flow_rows * cells
+    count_column = main_count.reshape(total, 1)
     big = pltpu.CompilerParams(vmem_limit_bytes=48 << 20)
 
-    payload, profile = pl.pallas_call(
+    def planes(value):
+        return jnp.transpose(value, (0, 2, 1, 3))
+
+    main_state = [planes(v) for v in (main_pos, main_vel, main_force)]
+    prec_state = [planes(v) for v in (prec_pos, prec_vel, prec_force)]
+
+    def linked(n):
+        return pltpu.CompilerParams(vmem_limit_bytes=48 << 20, collective_id=n,
+                                    has_side_effects=True)
+
+    own = pl.pallas_call(
         start_kernel,
-        out_shape=(shape((16, rows)), shape((1, LANES))),
+        out_shape=shape((8, LANES)),
         in_specs=whole(SMEM, 3) + whole(VMEM, 6),
-        out_specs=tuple(whole(VMEM, 2)),
+        out_specs=pl.BlockSpec(memory_space=VMEM),
         compiler_params=big,
         name="start",
-    )(cross_row, cross_dest, cross_cell, count_column, prec_pos, prec_vel, prec_force, prec_seed,
-      outlet_bin)
-    gathered = lax.all_gather(payload, "trans", axis=0)
-    total_profile = lax.psum(profile[0, 0:BINS], "trans")
-    density = total_profile * BINS / (cells * trans_devices * LANES)
-    push = -outlet_coef * density
-    push = jnp.where(flow_index == flow_devices - 1, push, 0.0)
-    push = jnp.concatenate([push, jnp.zeros((LANES - BINS,), jnp.float32)])[None]
-    dests = gathered[:, 10, :].reshape(-1).astype(jnp.int32)
-    places = gathered[:, 11, :].reshape(-1).astype(jnp.int32)
-    me = jnp.where(flow_index == 0, trans_index, -1).astype(jnp.int32)[None]
-
-    total = flow_rows * cells
-    msort, psort, mraw, praw, mrank, prank = pl.pallas_call(
+    )(cross_row, cross_dest, cross_cell, count_column, *prec_state, prec_seed, outlet_bin)
+    got = pl.pallas_call(
+        exchange_kernel,
+        out_shape=shape((trans_devices, 8, LANES)),
+        in_specs=whole(VMEM, 1),
+        out_specs=pl.BlockSpec(memory_space=VMEM),
+        scratch_shapes=[pltpu.SemaphoreType.DMA((trans_devices,))] * 2,
+        compiler_params=linked(0),
+        name="exchange",
+    )(own)
+    share = BINS / (cells * trans_devices * LANES)
+    share = jnp.where(flow_index == flow_devices - 1, jnp.float32(share), 0.0)[None]
+    coef = jnp.concatenate([outlet_coef, jnp.zeros((LANES - BINS,), jnp.float32)])[None]
+    me = jnp.where(flow_index == 0, trans_index, -1).astype(jnp.float32)[None]
+
+    msort, psort, mraw, praw, mrank, prank, left, right, push = pl.pallas_call(
         prep_kernel,
         out_shape=(
             shape((8, flow_rows, cells, LANES)),
@@ -460,35 +562,28 @@
             shape((7, prec_cells, LANES)),
             shape((total, LANES), jnp.int32),
             shape((prec_cells, LANES), jnp.int32),
+            shape((8, 8, LANES)),
+            shape((8, 8, LANES)),
+            shape((1, LANES)),
         ),
-        in_specs=whole(SMEM, 5) + whole(VMEM, 9),
-        out_specs=tuple(whole(VMEM, 6)),
+        in_specs=whole(SMEM, 4) + whole(VMEM, 11),
+        out_specs=tuple(whole(VMEM, 9)),
         scratch_shapes=[VMEM((10, total, LANES), jnp.float32), SMEM((cells,), jnp.int32)],
         compiler_params=big,
         name="prep",
-    )(dests, places, gathered.reshape(-1), me, main_count[0], count_column,
-      main_pos, main_vel, main_force, main_seed, prec_pos, prec_vel, prec_force, prec_seed)
-
-    def ring(value, axis, step):
-        count = lax.axis_size(axis)
-        return lax.ppermute(value, axis, [(i, (i + step) % count) for i in range(count)])
-
-    top = jnp.concatenate([msort[:, flow_rows - 1], psort[:, 0]], axis=1)
-    bottom = jnp.concatenate([msort[:, 0], psort[:, 0]], axis=1)
-    below = ring(top, "flow", 1)
-    above = ring(bottom, "flow", -1)
-
-    def column(at_main, at_prec):
-        return jnp.stack(
-            [below[:, at_main]]
-            + [msort[:, f, at_main] for f in range(flow_rows)]
-            + [above[:, at_main], below[:, cells + at_prec], psort[:, 0, at_prec],
-               above[:, cells + at_prec]],
-            axis=1,
-        )
-
-    left = ring(column(cells - 1, prec_cells - 1), "trans", 1)
-    right = ring(column(0, 0), "trans", -1)
+    )(got[:, 0:2].reshape(-1), me, main_count[0], share, count_column, coef, got,
+      *main_state, main_seed, *prec_state, prec_seed)
+
+    span = cells + prec_cells
+    below, above, side = pl.pallas_call(
+        halo_kernel,
+        out_shape=(shape((8, span, LANES)), shape((8, span, LANES)), shape((6, 8, 8, LANES))),
+        in_specs=whole(VMEM, 4),
+        out_specs=tuple(whole(VMEM, 3)),
+        scratch_shapes=[pltpu.SemaphoreType.DMA((10,))] * 2,
+        compiler_params=linked(1),
+        name="halo",
+    )(msort, psort, left, right)
     ends = jnp.stack([
         flow_index > 0,
         flow_index < flow_devices - 1,
@@ -496,12 +591,12 @@
         trans_index < trans_devices - 1,
     ]).astype(jnp.int32)
 
-    out_main = shape((flow_rows, cells, 3, LANES))
-    out_prec = shape((1, prec_cells, 3, LANES))
-    return pl.pallas_call(
+    out_main = shape((flow_rows, 3, cells, LANES))
+    out_prec = shape((1, 3, prec_cells, LANES))
+    outs = pl.pallas_call(
         force_kernel,
         out_shape=(out_main, out_main, out_main, out_prec, out_prec, out_prec),
-        in_specs=whole(SMEM, 1) + whole(VMEM, 12),
+        in_specs=whole(SMEM, 1) + whole(VMEM, 11),
         out_specs=tuple(whole(VMEM, 6)),
         scratch_shapes=[
             VMEM((8, flow_rows + 2, cells + 16, LANES), jnp.float32),
@@ -520,7 +615,8 @@
         ],
         compiler_params=big,
         name="force",
-    )(ends, msort, psort, mraw, praw, mrank, prank, below, above, left, right, outlet_bin, push)
+    )(ends, msort, psort, mraw, praw, mrank, prank, below, above, side, outlet_bin, push)
+    return tuple(planes(v) for v in outs)
 
 
 def solution(mesh):

time: 218 us -> 113 us (0.52)
  the two profiles are of different devices: /device:TPU:231 before, /device:TPU:199 now
where the time goes in v2:
time: 113 us; the launch traced here: 112 us
  Pallas kernels  106 us (94%)
  local copies, waits for them, and re-layouts  4.51 us (4%)
    pallas_call x1, Pallas kernels, shards(): pl.pallas_call(force_kernel, out_shape=(out_main, out_main, out_main, out...  64.9 us
    pallas_call x1, Pallas kernels, shards(): pl.pallas_call(halo_kernel, out_shape=(shape((8, span, LANES)), shape((8,...  16 us
    pallas_call x1, Pallas kernels, shards(): pl.pallas_call(exchange_kernel, out_shape=shape((trans_devices, 8, LANES)...  12.7 us
    pallas_call x1, Pallas kernels, shards(): pl.pallas_call(prep_kernel, out_shape=(shape((8, flow_rows, cells, LANES)...  11.5 us
    unnamed x30, local copies, waits for them, and re-layouts  4.36 us

profile of v2, /device:TPU:199, one launch (start us, length us, event | category | flops | bytes accessed | tf_op | source)
XLA Modules:
  0.0 111.7 jit_solution(9239112314067763341)
XLA Ops:
  0.6 0.0 copy-start.14
  0.6 0.0 copy-start.13
  0.7 0.0 copy-start.12
  0.7 0.0 copy-start.8
  0.7 0.0 copy-start.1
  0.7 0.0 copy-start
  0.7 0.1 add_convert_fusion.end_ref
  0.8 0.5 copy-done.14
  1.3 0.0 copy-done.13
  1.3 0.0 copy-start.10
  1.3 0.0 copy-start.11
  1.3 0.1 reshape.20.count_ref
  1.5 0.0 copy-done.12
  1.5 0.0 copy-done.8
  1.5 0.0 copy-done.1
  1.5 0.0 copy-done
  1.5 0.5 copy-done.10
  2.0 0.0 copy-done.11
  2.0 0.0 copy-start.2
  2.0 0.8 copy-done.2
  2.8 0.0 copy-start.6
  2.8 0.8 copy-done.6
  3.6 0.0 copy-start.3
  3.6 0.0 copy-start.4
  3.6 1.1 %start.1.own_ref = f32[8,128]{1,0:T(8,128)S(1)} custom-call(s32[16]{0:T(128)S(1)} %copy-done.10, s32[16]{0:T(128)S(1)} %copy-done.11, s32[16]{0:T(128)S(1)} %copy-done.12, s32[128,1]{1,0:T(8,128)S(1)} %reshape.20.count_ref, f32[1,3,32,128]{3,2,1,0:T(8,128)S(1)} %bitcast.23, f32[1,3,32,128]{3,2,1,0:T(8,128)S(1)} %bitcast.25, f32[1,3,32,128]{3,2,1,0:T(8,128)S(1)} %bitcast.27, ...), custom_call_target="tpu_custom_call" | custom-call | tf_op jit(solution)/shard_map/start/pallas_call | solution.py:534
  4.7 12.7 %exchange.1.got_ref = f32[32,8,128]{2,1,0:T(8,128)S(1)} custom-call(f32[8,128]{1,0:T(8,128)S(1)} %start.1.own_ref), custom_call_target="tpu_custom_call" | custom-call | tf_op jit(solution)/shard_map/exchange/pallas_call | solution.py:542
  17.4 0.0 copy-start.9
  17.5 0.0 copy-done.3
  17.5 0.0 copy-done.4
  17.5 0.8 copy-done.9
  18.3 0.0 copy-start.5
  18.3 0.9 copy-done.5
  19.2 11.5 %prep.1 = (f32[8,2,64,128]{3,2,1,0:T(8,128)S(1)}, f32[8,1,32,128]{3,2,1,0:T(8,128)S(1)}, f32[7,128,128]{2,1,0:T(8,128)S(1)}, f32[7,32,128]{2,1,0:T(8,128)S(1)}, ...) custom-call(f32[8192]{0:T(1024)S(1)} %bitcast.32, ...), custom_call_target="tpu_custom_call" | custom-call | tf_op jit(solution)/shard_map/prep/pallas_call | solution.py:556
  30.7 0.0 copy-start.7
  30.7 16.0 %halo.1 = (f32[8,96,128]{2,1,0:T(8,128)S(1)}, f32[8,96,128]{2,1,0:T(8,128)S(1)}, f32[6,8,8,128]{3,2,1,0:T(8,128)S(1)}) custom-call(f32[8,2,64,128]{3,2,1,0:T(8,128)S(1)} %get-tuple-element.24.msort_ref, f32[8,1,32,128]{3,2,1,0:T(8,128)S(1)} %get-tuple-element.25.psort_ref, f32[8,8,128]{2,1,0:T(8,128)S(1)} %get-tuple-element.30.left_ref, ...), custom_call_target="tpu_custom_call" | custom-call | tf_op jit(solution)/shard_map/halo/pallas_call | solution.py:578
  46.7 0.0 copy-done.7
  46.7 64.9 %force.1 = (f32[2,3,64,128]{3,2,1,0:T(8,128)}, f32[2,3,64,128]{3,2,1,0:T(8,128)}, f32[2,3,64,128]{3,2,1,0:T(8,128)}, f32[1,3,32,128]{3,2,1,0:T(8,128)}, f32[1,3,...) custom-call(s32[4]{0:T(128)S(1)} %add_convert_fusion.end_ref, f32[8,2,64,128]{3,2,1,0:T(8,128)S(1)} %get-tuple-element.24.msort_ref, ...), custom_call_target="tpu_custom_call" | custom-call | tf_op jit(solution)/shard_map/force/pallas_call | solution.py:596
  (3 shorter events, 0.0 us)
Async XLA Ops:
  0.6 0.7 copy-start.14
  0.6 0.7 copy-start.13
  0.7 0.8 copy-start.12
  0.7 0.8 copy-start.8
  0.7 0.8 copy-start.1
  0.7 0.8 copy-start
  1.3 0.7 copy-start.10
  1.3 0.7 copy-start.11
  2.0 0.8 copy-start.2
  2.8 0.8 copy-start.6
  3.6 13.9 %copy-start.3 = (f32[2,64,3,128]{3,1,2,0:T(8,128)S(1)}, f32[2,64,3,128]{3,1,2,0:T(8,128)}, u32[]{:S(2)}) copy-start(f32[2,64,3,128]{3,1,2,0:T(8,128)} %param.14) | copy-start | bytes 589828
  3.6 13.9 %copy-start.4 = (f32[2,64,3,128]{3,1,2,0:T(8,128)S(1)}, f32[2,64,3,128]{3,1,2,0:T(8,128)}, u32[]{:S(2)}) copy-start(f32[2,64,3,128]{3,1,2,0:T(8,128)} %param.15) | copy-start | bytes 589828
  17.4 0.8 copy-start.9
  18.3 0.9 copy-start.5
  30.7 16.0 %copy-start.7 = (s32[64,128]{1,0:T(8,128)S(1)}, s32[64,128]{1,0:T(8,128)}, u32[]{:S(2)}) copy-start(s32[64,128]{1,0:T(8,128)} %bin_ref.3) | copy-start | bytes 98308

commit v3 on v2

--- a/solution.py
+++ b/solution.py
@@ -23,7 +23,8 @@
 table_rate = 8.0
 hash_shift = 2047.0 / 4093.0
 noise_slope = noise_amp * unit_spread
-noise_base = repulsion - noise_slope * 0.5 / 4093.0
+drag = friction / noise_slope
+noise_lift = repulsion / noise_slope - 0.5 / 4093.0 - hash_shift
 
 VMEM = pltpu.VMEM
 SMEM = pltpu.SMEM
@@ -43,8 +44,7 @@
     return jnp.where(code > 2046, code - seed_modulus, code)
 
 
-def start_kernel(row_ref, dest_ref, cell_ref, count_ref, pos_ref, vel_ref, force_ref, seed_ref,
-                 bin_ref, out_ref):
+def first_tile(row_ref, dest_ref, cell_ref, count_ref, arrays, seed_ref, bin_ref, out_ref):
     rows = row_ref.shape[0]
     lane = lane_iota(1)
     lines = [jnp.zeros((1, LANES), jnp.float32) for _ in range(2)]
@@ -57,7 +57,7 @@
         cell = row_ref[q] // LANES
         slot = row_ref[q] % LANES
         hit = lane == slot
-        for a, ref in enumerate((pos_ref, vel_ref, force_ref)):
+        for a, ref in enumerate(arrays):
             for c in range(3):
                 value = jnp.where(hit, ref[0, c, pl.ds(cell, 1), :], 0.0)
                 put(3 * a + c, q, jnp.sum(value, axis=1, keepdims=True))
@@ -65,8 +65,9 @@
         put(9, q, jnp.sum(seed, axis=1, keepdims=True))
         put(10, q, dest_ref[q].astype(jnp.float32))
         put(11, q, cell_ref[q].astype(jnp.float32))
-    last = count_ref.shape[0] // 2
-    bins = jnp.where(lane_iota(last) < count_ref[last:, :], bin_ref[...], BINS)
+    cells = bin_ref.shape[0]
+    last = count_ref.shape[0] - cells
+    bins = jnp.where(lane_iota(cells) < count_ref[last:, :], bin_ref[...], BINS)
     profile = jnp.zeros((1, LANES), jnp.float32)
     for b in range(BINS):
         hits = jnp.sum((bins == b).astype(jnp.float32), axis=0, keepdims=True)
@@ -77,55 +78,29 @@
     out_ref[2:3, :] = profile
 
 
-def exchange_kernel(own_ref, out_ref, send_sem, recv_sem):
-    me = lax.axis_index("trans")
-    count = out_ref.shape[0]
-    barrier = pltpu.get_barrier_semaphore()
-
-    def greet(s, carry):
-        pl.semaphore_signal(barrier, inc=1, device_id={"trans": lax.rem(me + s, count)},
-                            device_id_type=pl.DeviceIdType.MESH)
-        return carry
-
-    lax.fori_loop(1, count, greet, 0)
-    pl.semaphore_wait(barrier, count - 1)
-
-    def copy(s, slot):
-        return pltpu.make_async_remote_copy(
-            src_ref=own_ref, dst_ref=out_ref.at[slot], send_sem=send_sem.at[s],
-            recv_sem=recv_sem.at[slot], device_id={"trans": lax.rem(me + s, count)},
-            device_id_type=pl.DeviceIdType.MESH)
-
-    def send(s, carry):
-        copy(s, me).start()
-        return carry
-
-    def finish(s, carry):
-        copy(s, lax.rem(me + count - s, count)).wait_recv()
-        copy(s, me).wait_send()
-        return carry
-
-    lax.fori_loop(1, count, send, 0)
-    out_ref[me] = own_ref[...]
-    lax.fori_loop(1, count, finish, 0)
-
-
-def halo_kernel(msort_ref, psort_ref, left_ref, right_ref, below_ref, above_ref, side_ref,
-                send_sem, recv_sem):
+def link_kernel(own_ref, msort_ref, psort_ref, left_ref, right_ref,
+                got_ref, below_ref, above_ref, side_ref,
+                tile_send, tile_recv, send_sem, recv_sem):
     flow, trans = lax.axis_index("flow"), lax.axis_index("trans")
-    flows, transes = lax.axis_size("flow"), lax.axis_size("trans")
+    flows, count = lax.axis_size("flow"), got_ref.shape[0]
     flow_rows, cells = msort_ref.shape[1], msort_ref.shape[2]
     prec_cells = psort_ref.shape[2]
 
     def at(df, dt):
-        return (lax.rem(flow + flows + df, flows), lax.rem(trans + transes + dt, transes))
+        return (lax.rem(flow + flows + df, flows), lax.rem(trans + count + dt, count))
 
     mesh_id = pl.DeviceIdType.MESH
     barrier = pltpu.get_barrier_semaphore()
-    around = [(df, dt) for df in (-1, 0, 1) for dt in (-1, 0, 1) if (df, dt) != (0, 0)]
-    for df, dt in around:
+    across = [(df, dt) for df in (-1, 1) for dt in (-1, 0, 1)]
+    for df, dt in across:
         pl.semaphore_signal(barrier, inc=1, device_id=at(df, dt), device_id_type=mesh_id)
-    pl.semaphore_wait(barrier, len(around))
+
+    def greet(s, carry):
+        pl.semaphore_signal(barrier, inc=1, device_id=at(0, s), device_id_type=mesh_id)
+        return carry
+
+    lax.fori_loop(1, count, greet, 0)
+    pl.semaphore_wait(barrier, len(across) + count - 1)
     main_part, prec_part = pl.ds(0, cells), pl.ds(cells, prec_cells)
     plan = [
         (msort_ref.at[:, flow_rows - 1], below_ref.at[:, main_part], (1, 0)),
@@ -147,28 +122,47 @@
     ]
     for copy in copies:
         copy.start()
+
+    def tile(s, slot):
+        return pltpu.make_async_remote_copy(
+            src_ref=own_ref, dst_ref=got_ref.at[slot], send_sem=tile_send.at[s],
+            recv_sem=tile_recv.at[slot], device_id=at(0, s), device_id_type=mesh_id)
+
+    def send(s, carry):
+        tile(s, trans).start()
+        return carry
+
+    def finish(s, carry):
+        tile(s, lax.rem(trans + count - s, count)).wait_recv()
+        tile(s, trans).wait_send()
+        return carry
+
+    lax.fori_loop(1, count, send, 0)
+    got_ref[trans] = own_ref[...]
+    lax.fori_loop(1, count, finish, 0)
     for copy in copies:
         copy.wait()
 
 
-def sorted_by(key, rows):
+def sorted_lanes(key):
+    rows = key.shape[0]
     lane = lane_iota(rows)
-    load = lane
+    held = key * LANES + lane
     size = 2
     while size <= LANES:
         dist = size // 2
         while dist >= 1:
-            partner = lane ^ dist
             low = ((lane & size) == 0) == ((lane & dist) == 0)
-            sign = jnp.where(low, 1.0, -1.0)
-            other_key = take(key, partner)
-            other_load = take(load, partner)
-            swap = (other_key - key) * sign < 0.0
-            key = jnp.where(swap, other_key, key)
-            load = jnp.where(swap, other_load, load)
+            other = take(held, lane ^ dist)
+            held = jnp.where(low, jnp.minimum(held, other), jnp.maximum(held, other))
             dist //= 2
         size *= 2
-    return key, load
+    return held & (LANES - 1)
+
+
+def height_order(height):
+    level = jnp.minimum(height, 16.25) * float(1 << 19)
+    return sorted_lanes(level.astype(jnp.int32))
 
 
 def first_at_least(sorted_rows, bound, rows):
@@ -181,97 +175,59 @@
     return jnp.where(take(sorted_rows, at) < bound, at + 1, at)
 
 
-def prep_kernel(pay_ref, me_ref, count0_ref, share_ref, count_ref, coef_ref, got_ref,
+def prep_kernel(row_ref, dest_ref, cell_ref, count_ref,
+                bin_ref, ppos_ref, pvel_ref, pforce_ref, pseed_ref,
                 mpos_ref, mvel_ref, mforce_ref, mseed_ref,
-                ppos_ref, pvel_ref, pforce_ref, pseed_ref,
-                msort_ref, psort_ref, mraw_ref, praw_ref, mrank_ref, prank_ref,
-                left_ref, right_ref, push_ref, raw_ref, filled_ref):
-    flow_rows, cells = mseed_ref.shape[0], mseed_ref.shape[1]
-    sources = got_ref.shape[0]
-    stride = pay_ref.shape[0] // sources
-    per = 16
-    profile = jnp.sum(got_ref[:, 2:3, :], axis=0)
-    push_ref[...] = -coef_ref[...] * (profile * share_ref[0])
-    for f in range(flow_rows):
-        for c in range(3):
-            raw_ref[c, f * cells : (f + 1) * cells, :] = mpos_ref[f, c]
-            raw_ref[3 + c, f * cells : (f + 1) * cells, :] = mvel_ref[f, c]
-            raw_ref[6 + c, f * cells : (f + 1) * cells, :] = mforce_ref[f, c]
-        seed = mseed_ref[f]
-        occupied = lane_iota(cells) < count_ref[f * cells : (f + 1) * cells, :]
-        raw_ref[9, f * cells : (f + 1) * cells, :] = jnp.where(occupied, seed, -1).astype(jnp.float32)
-
-    me = me_ref[0]
-
-    def fill(cell, carry):
-        filled_ref[cell] = count0_ref[cell]
-        return carry
-
-    lax.fori_loop(0, cells, fill, 0)
-    lane1 = lane_iota(1)
-
-    def look(source, carry):
-        start = source * stride
-        found = pay_ref[start + 10 * per] == me
-        for u in range(1, per):
-            found = found | (pay_ref[start + 10 * per + u] == me)
-
-        @pl.when(found)
-        def _():
-            def one(u, inner):
-                origin = start + u
-
-                @pl.when(pay_ref[origin + 10 * per] == me)
-                def _():
-                    cell = pay_ref[origin + 11 * per].astype(jnp.int32)
-                    slot = filled_ref[cell]
-                    filled_ref[cell] = slot + 1
-                    for c in range(10):
-                        row = raw_ref[c, pl.ds(cell, 1), :]
-                        raw_ref[c, pl.ds(cell, 1), :] = jnp.where(
-                            lane1 == slot, pay_ref[origin + c * per], row
-                        )
-
-                return inner
-
-            lax.fori_loop(0, per, one, 0)
-
-        return carry
-
-    @pl.when(me >= 0.0)
-    def _():
-        lax.fori_loop(0, sources, look, 0)
-
-    def finish(state, seed, rows, sort_ref, rank_ref, raw_out, f, at):
+                own_ref, msort_ref, psort_ref, mraw_ref, praw_ref, mrank_ref, prank_ref,
+                left_ref, right_ref,
+                bin_in, ppos_in, pvel_in, pforce_in, pseed_in,
+                mpos_in, mvel_in, mforce_in, mseed_in, sem_ref):
+    outside = (ppos_ref, pvel_ref, pforce_ref, pseed_ref, bin_ref, mpos_ref, mvel_ref, mforce_ref,
+               mseed_ref)
+    inside = (ppos_in, pvel_in, pforce_in, pseed_in, bin_in, mpos_in, mvel_in, mforce_in, mseed_in)
+    loads = [pltpu.make_async_copy(a, b, sem_ref.at[n])
+             for n, (a, b) in enumerate(zip(outside, inside))]
+    for load in loads:
+        load.start()
+    for load in loads[:5]:
+        load.wait()
+    first_tile(row_ref, dest_ref, cell_ref, count_ref, (ppos_in, pvel_in, pforce_in), pseed_in,
+               bin_in, own_ref)
+    flow_rows, cells = mseed_in.shape[0], mseed_in.shape[1]
+    prec_cells = pseed_in.shape[1]
+
+    def finish(arrays, f, seed, rows, sort_ref, rank_ref, raw_out, at):
         occupied = seed >= 0
-        half = [state[3 + c] + 0.5 * time_step * state[6 + c] for c in range(3)]
-        moved = [state[c] + time_step * half[c] for c in range(3)]
+        pos, vel, force = [[ref[f, c] for c in range(3)] for ref in arrays]
+        half = [vel[c] + 0.5 * time_step * force[c] for c in range(3)]
+        moved = [pos[c] + time_step * half[c] for c in range(3)]
         for c in range(3):
             raw_out[c, at : at + rows, :] = moved[c]
             raw_out[3 + c, at : at + rows, :] = half[c]
         raw_out[6, at : at + rows, :] = seed.astype(jnp.float32)
         height = moved[2] - box_height * jnp.floor(moved[2] * (1.0 / box_height))
-        key, order = sorted_by(jnp.where(occupied, height, nowhere), rows)
-        _, rank = sorted_by(order.astype(jnp.float32), rows)
-        rank_ref[at : at + rows, :] = rank
+        height = jnp.where(occupied, height, nowhere)
+        order = height_order(height)
+        rank_ref[at : at + rows, :] = sorted_lanes(order)
         hashed = centred(seed).astype(jnp.float32) / seed_modulus
-        fields = [moved[0], moved[1], None] + [friction * v for v in half] + [hashed]
+        fields = [moved[0], moved[1], None] + [drag * v for v in half] + [hashed]
         for c, field in enumerate(fields):
             if field is None:
-                sort_ref[c, f, :, :] = key
+                height = take(height, order)
+                sort_ref[c, f, :, :] = height
             else:
                 sort_ref[c, f, :, :] = take(jnp.where(occupied, field, 0.0), order)
-        edges = lane_iota(rows).astype(jnp.float32) * (1.0 / table_rate)
-        sort_ref[7, f, :, :] = first_at_least(key, edges, rows).astype(jnp.float32)
-
+        sort_ref[7, f, :, :] = starts_of(height)
+
+    finish((ppos_in, pvel_in, pforce_in), 0, pseed_in[0], prec_cells, psort_ref, prank_ref,
+           praw_ref, 0)
+    for load in loads[5:]:
+        load.wait()
     for f in range(flow_rows):
         at = f * cells
-        state = [raw_ref[c, at : at + cells, :] for c in range(9)]
-        finish(state, raw_ref[9, at : at + cells, :].astype(jnp.int32), cells,
-               msort_ref, mrank_ref, mraw_ref, f, at)
-    state = [ref[0, c] for ref in (ppos_ref, pvel_ref, pforce_ref) for c in range(3)]
-    prec_cells = pseed_ref.shape[1]
-    finish(state, pseed_ref[0], prec_cells, psort_ref, prank_ref, praw_ref, 0, 0)
+        occupied = lane_iota(cells) < count_ref[at : at + cells, :]
+        finish((mpos_in, mvel_in, mforce_in), f, jnp.where(occupied, mseed_in[f], -1), cells,
+               msort_ref, mrank_ref, mraw_ref, at)
     left_ref[...] = jnp.zeros(left_ref.shape, jnp.float32)
     right_ref[...] = jnp.zeros(right_ref.shape, jnp.float32)
     for c in range(msort_ref.shape[0]):
@@ -280,6 +236,86 @@
             right_ref[c, f : f + 1, :] = msort_ref[c, f, cells - 1 : cells, :]
         left_ref[c, flow_rows : flow_rows + 1, :] = psort_ref[c, 0, 0:1, :]
         right_ref[c, flow_rows : flow_rows + 1, :] = psort_ref[c, 0, prec_cells - 1 : prec_cells, :]
+
+
+def starts_of(height):
+    edges = lane_iota(height.shape[0]).astype(jnp.float32) * (1.0 / table_rate)
+    return first_at_least(height, edges, height.shape[0]).astype(jnp.float32)
+
+
+def arrivals(me, pay_ref, count0_ref, count_ref, j_ref, raw_ref, rank_ref, filled_ref):
+    cells = count0_ref.shape[0]
+    per = 16
+    stride = 2 * LANES
+    sources = pay_ref.shape[0] // stride
+    lane = lane_iota(1)
+    for row in (7, 8 + cells):
+        real = (j_ref[2, 1, row : row + 1, :] < 500.0).astype(jnp.float32)
+        filled_ref[row] = jnp.sum(real).astype(jnp.int32)
+
+    def fill(cell, carry):
+        filled_ref[8 + cell] = count0_ref[cell]
+        return carry
+
+    lax.fori_loop(0, cells, fill, 0)
+
+    def near(origin):
+        return jnp.abs(pay_ref[origin + 10 * per] - me) < 1.5
+
+    def look(source, carry):
+        start = source * stride
+        found = near(start)
+        for u in range(1, per):
+            found = found | near(start + u)
+
+        @pl.when(found)
+        def _():
+            def one(u, inner):
+                origin = start + u
+                off = pay_ref[origin + 10 * per] - me
+                cell = pay_ref[origin + 11 * per].astype(jnp.int32)
+                own = off == 0.0
+                before = (off == -1.0) & (cell == cells - 1)
+                after = (off == 1.0) & (cell == 0)
+
+                @pl.when(own | before | after)
+                def _():
+                    row = jnp.where(own, 8 + cell, jnp.where(before, 7, 8 + cells))
+                    slot = filled_ref[row]
+                    filled_ref[row] = slot + 1
+                    hit = lane == slot
+                    state = [jnp.full((1, LANES), pay_ref[origin + c * per], jnp.float32)
+                             for c in range(10)]
+                    half = [state[3 + c] + 0.5 * time_step * state[6 + c] for c in range(3)]
+                    moved = [state[c] + time_step * half[c] for c in range(3)]
+                    height = moved[2] - box_height * jnp.floor(moved[2] * (1.0 / box_height))
+                    hashed = centred(state[9].astype(jnp.int32)).astype(jnp.float32) / seed_modulus
+                    fields = [moved[0], moved[1], height] + [drag * v for v in half] + [hashed]
+                    for c in range(7):
+                        old = j_ref[c, 1, pl.ds(row, 1), :]
+                        j_ref[c, 1, pl.ds(row, 1), :] = jnp.where(hit, fields[c], old)
+
+                    @pl.when(own)
+                    def _():
+                        for c, value in enumerate(moved + half + [state[9]]):
+                            old = raw_ref[c, pl.ds(cell, 1), :]
+                            raw_ref[c, pl.ds(cell, 1), :] = jnp.where(hit, value, old)
+
+                return inner
+
+            lax.fori_loop(0, per, one, 0)
+
+        return carry
+
+    lax.fori_loop(0, sources, look, 0)
+    order = height_order(j_ref[2, 1])
+    for c in range(7):
+        j_ref[c, 1] = take(j_ref[c, 1], order)
+    j_ref[7, 1] = starts_of(j_ref[2, 1])
+    back = sorted_lanes(order[8 : 8 + cells, :])
+    lanes = lane_iota(cells)
+    listed = jnp.where(lanes < count_ref[0:cells, :], rank_ref[0:cells, :], lanes)
+    rank_ref[0:cells, :] = take(back, listed)
 
 
 def assemble(j_ref, sort_ref, below, above, side_ref, shift, open_ends):
@@ -377,13 +413,15 @@
             for v in range(SHARE):
                 own = beads[v]
                 dx, dy, dz = own[0] - other[0], own[1] - other[1], own[2] - other[2]
-                dist_sq = jnp.maximum(dx * dx + dy * dy + dz * dz, 1e-30)
+                dist_sq = dx * dx + dy * dy + dz * dz
+                if nb == 4:
+                    dist_sq = jnp.maximum(dist_sq, 1e-30)
                 weight = jnp.maximum(lax.rsqrt(dist_sq) - 1.0, 0.0)
                 along = ((own[3] - other[3]) * dx + (own[4] - other[4]) * dy
                          + (own[5] - other[5]) * dz)
-                ratio = own[6] * other[6] - hash_shift
-                noise = ratio - jnp.round(ratio)
-                scalar = weight * ((noise_slope * noise + noise_base) - weight * along)
+                ratio = own[6] * other[6]
+                noise = (ratio + noise_lift) - jnp.round(ratio - hash_shift)
+                scalar = weight * (noise - weight * along)
                 sums[v] = sums[v] + scalar * dx
                 sums[SHARE + v] = sums[SHARE + v] + scalar * dy
                 sums[2 * SHARE + v] = sums[2 * SHARE + v] + scalar * dz
@@ -405,26 +443,28 @@
             part = part + pltpu.roll(part, LANES // 4, 1)
             part = take(part, lanes)
             total = part if total is None else jnp.where(which == v, part, total)
-        out.append(total)
+        out.append(noise_slope * total)
     return out
 
 
-def arrange(i_ref, sort_ref, f, cells, at):
+def arrange(i_ref, j_ref, f, cells, at):
     lane = lane_iota(cells) % CLASSES
     for v in range(SHARE):
         lanes = lane * SHARE + v
         for c in range(7):
-            field = take(sort_ref[c, f], lanes)
+            field = take(j_ref[c, 1 + f, 8 : 8 + cells, :], lanes)
             if c == 6:
                 field = jnp.round(field * seed_modulus)
             i_ref[c * SHARE + v, at : at + cells, :] = field
 
 
-def force_kernel(end_ref, msort_ref, psort_ref, mraw_ref, praw_ref, mrank_ref, prank_ref,
-                 below_ref, above_ref, side_ref, bin_ref, push_ref,
+def force_kernel(end_ref, pay_ref, me_ref, count0_ref, share_ref, count_ref, coef_ref, got_ref,
+                 msort_ref, psort_ref, mraw_in, praw_ref, mrank_in, prank_ref,
+                 below_ref, above_ref, side_ref, bin_ref,
                  mpos_out, mvel_out, mforce_out, ppos_out, pvel_out, pforce_out,
                  mj_ref, pj_ref, mi_ref, pi_ref, mbase_ref, mcount_ref, pbase_ref, pcount_ref,
-                 mheld_ref, pheld_ref, mreach_ref, preach_ref, steps_ref):
+                 mheld_ref, pheld_ref, mreach_ref, preach_ref, steps_ref,
+                 mraw_ref, mrank_ref, filled_ref):
     flow_rows, cells = msort_ref.shape[1], msort_ref.shape[2]
     prec_cells = psort_ref.shape[2]
     ends = tuple(end_ref[e] > 0 for e in range(4))
@@ -433,14 +473,23 @@
     assemble(pj_ref, psort_ref, lambda c: below_ref[c, cells : cells + prec_cells, :],
              lambda c: above_ref[c, cells : cells + prec_cells, :], side_ref,
              flow_rows, None)
+    mraw_ref[...] = mraw_in[...]
+    mrank_ref[...] = mrank_in[...]
+
+    @pl.when(me_ref[0] >= 0.0)
+    def _():
+        arrivals(me_ref[0], pay_ref, count0_ref, count_ref, mj_ref, mraw_ref, mrank_ref, filled_ref)
+
+    push_row = -coef_ref[...] * (jnp.sum(got_ref[:, 2:3, :], axis=0) * share_ref[0])
+    push_row = jnp.broadcast_to(push_row, (8, LANES))
     for j_ref, held_ref, n in ((mj_ref, mheld_ref, cells), (pj_ref, pheld_ref, prec_cells)):
         for f in range(held_ref.shape[0]):
             real = (j_ref[2, f, 0 : n + 16, :] < 500.0).astype(jnp.float32)
             held = jnp.sum(real, axis=1, keepdims=True).astype(jnp.int32)
             held_ref[f] = jnp.broadcast_to(held, (n + 16, LANES))
     for f in range(flow_rows):
-        arrange(mi_ref, msort_ref, f, cells, f * cells)
-    arrange(pi_ref, psort_ref, 0, prec_cells, 0)
+        arrange(mi_ref, mj_ref, f, cells, f * cells)
+    arrange(pi_ref, pj_ref, 0, prec_cells, 0)
     for f in range(flow_rows):
         search(mj_ref, f, cells, mi_ref, mbase_ref, mcount_ref, mheld_ref, mreach_ref, 0)
     search(pj_ref, 0, prec_cells, pi_ref, pbase_ref, pcount_ref, pheld_ref, preach_ref, 0)
@@ -458,7 +507,7 @@
         sums = pair_sums(mj_ref, f, r0, mi_ref, i0, mbase_ref, mcount_ref, mheld_ref, steps_ref[g])
         force = unsorted_sums(sums, mrank_ref[pl.ds(i0, 8), :])
         occupied = mraw_ref[6, pl.ds(i0, 8), :] >= 0.0
-        push = take(jnp.broadcast_to(push_ref[...], (8, LANES)), bin_ref[pl.ds(r0, 8), :])
+        push = take(push_row, bin_ref[pl.ds(r0, 8), :])
         force[0] = force[0] + push * (f == flow_rows - 1).astype(jnp.float32)
         for c in range(3):
             half = mraw_ref[3 + c, pl.ds(i0, 8), :]
@@ -493,6 +542,28 @@
 
 def shape(dims, dtype=jnp.float32):
     return jax.ShapeDtypeStruct(dims, dtype)
+
+
+def scratches(flow_rows, cells, prec_cells):
+    total = flow_rows * cells
+    return [
+        VMEM((8, flow_rows + 2, cells + 16, LANES), jnp.float32),
+        VMEM((8, 3, prec_cells + 16, LANES), jnp.float32),
+        VMEM((7 * SHARE, total, LANES), jnp.float32),
+        VMEM((7 * SHARE, prec_cells, LANES), jnp.float32),
+        VMEM((9, total, LANES), jnp.int32),
+        VMEM((9, total, LANES), jnp.int32),
+        VMEM((9, prec_cells, LANES), jnp.int32),
+        VMEM((9, prec_cells, LANES), jnp.int32),
+        VMEM((flow_rows + 2, cells + 16, LANES), jnp.int32),
+        VMEM((3, prec_cells + 16, LANES), jnp.int32),
+        VMEM((total, LANES), jnp.int32),
+        VMEM((prec_cells, LANES), jnp.int32),
+        SMEM((total // 8 + prec_cells // 8,), jnp.int32),
+        VMEM((7, total, LANES), jnp.float32),
+        VMEM((total, LANES), jnp.int32),
+        SMEM((cells + 16,), jnp.int32),
+    ]
 
 
 def shards(
@@ -527,35 +598,16 @@
     main_state = [planes(v) for v in (main_pos, main_vel, main_force)]
     prec_state = [planes(v) for v in (prec_pos, prec_vel, prec_force)]
 
-    def linked(n):
-        return pltpu.CompilerParams(vmem_limit_bytes=48 << 20, collective_id=n,
-                                    has_side_effects=True)
-
-    own = pl.pallas_call(
-        start_kernel,
-        out_shape=shape((8, LANES)),
-        in_specs=whole(SMEM, 3) + whole(VMEM, 6),
-        out_specs=pl.BlockSpec(memory_space=VMEM),
-        compiler_params=big,
-        name="start",
-    )(cross_row, cross_dest, cross_cell, count_column, *prec_state, prec_seed, outlet_bin)
-    got = pl.pallas_call(
-        exchange_kernel,
-        out_shape=shape((trans_devices, 8, LANES)),
-        in_specs=whole(VMEM, 1),
-        out_specs=pl.BlockSpec(memory_space=VMEM),
-        scratch_shapes=[pltpu.SemaphoreType.DMA((trans_devices,))] * 2,
-        compiler_params=linked(0),
-        name="exchange",
-    )(own)
     share = BINS / (cells * trans_devices * LANES)
     share = jnp.where(flow_index == flow_devices - 1, jnp.float32(share), 0.0)[None]
     coef = jnp.concatenate([outlet_coef, jnp.zeros((LANES - BINS,), jnp.float32)])[None]
-    me = jnp.where(flow_index == 0, trans_index, -1).astype(jnp.float32)[None]
-
-    msort, psort, mraw, praw, mrank, prank, left, right, push = pl.pallas_call(
+    me = jnp.where(flow_index == 0, trans_index, -9).astype(jnp.float32)[None]
+
+    inputs = [outlet_bin, *prec_state, prec_seed, *main_state, main_seed]
+    own, msort, psort, mraw, praw, mrank, prank, left, right = pl.pallas_call(
         prep_kernel,
         out_shape=(
+            shape((8, LANES)),
             shape((8, flow_rows, cells, LANES)),
             shape((8, 1, prec_cells, LANES)),
             shape((7, total, LANES)),
@@ -564,26 +616,27 @@
             shape((prec_cells, LANES), jnp.int32),
             shape((8, 8, LANES)),
             shape((8, 8, LANES)),
-            shape((1, LANES)),
         ),
-        in_specs=whole(SMEM, 4) + whole(VMEM, 11),
+        in_specs=whole(SMEM, 3) + whole(VMEM, 1) + whole(pl.ANY, 9),
         out_specs=tuple(whole(VMEM, 9)),
-        scratch_shapes=[VMEM((10, total, LANES), jnp.float32), SMEM((cells,), jnp.int32)],
+        scratch_shapes=[VMEM(v.shape, v.dtype) for v in inputs] + [pltpu.SemaphoreType.DMA((9,))],
         compiler_params=big,
         name="prep",
-    )(got[:, 0:2].reshape(-1), me, main_count[0], share, count_column, coef, got,
-      *main_state, main_seed, *prec_state, prec_seed)
+    )(cross_row, cross_dest, cross_cell, count_column, *inputs)
 
     span = cells + prec_cells
-    below, above, side = pl.pallas_call(
-        halo_kernel,
-        out_shape=(shape((8, span, LANES)), shape((8, span, LANES)), shape((6, 8, 8, LANES))),
-        in_specs=whole(VMEM, 4),
-        out_specs=tuple(whole(VMEM, 3)),
-        scratch_shapes=[pltpu.SemaphoreType.DMA((10,))] * 2,
-        compiler_params=linked(1),
-        name="halo",
-    )(msort, psort, left, right)
+    got, below, above, side = pl.pallas_call(
+        link_kernel,
+        out_shape=(shape((trans_devices, 8, LANES)), shape((8, span, LANES)),
+                   shape((8, span, LANES)), shape((6, 8, 8, LANES))),
+        in_specs=whole(VMEM, 5),
+        out_specs=tuple(whole(VMEM, 4)),
+        scratch_shapes=[pltpu.SemaphoreType.DMA((trans_devices,))] * 2
+        + [pltpu.SemaphoreType.DMA((10,))] * 2,
+        compiler_params=pltpu.CompilerParams(vmem_limit_bytes=48 << 20, collective_id=0,
+                                             has_side_effects=True),
+        name="link",
+    )(own, msort, psort, left, right)
     ends = jnp.stack([
         flow_index > 0,
         flow_index < flow_devices - 1,
@@ -596,26 +649,13 @@
     outs = pl.pallas_call(
         force_kernel,
         out_shape=(out_main, out_main, out_main, out_prec, out_prec, out_prec),
-        in_specs=whole(SMEM, 1) + whole(VMEM, 11),
+        in_specs=whole(SMEM, 5) + whole(VMEM, 13),
         out_specs=tuple(whole(VMEM, 6)),
-        scratch_shapes=[
-            VMEM((8, flow_rows + 2, cells + 16, LANES), jnp.float32),
-            VMEM((8, 3, prec_cells + 16, LANES), jnp.float32),
-            VMEM((7 * SHARE, total, LANES), jnp.float32),
-            VMEM((7 * SHARE, prec_cells, LANES), jnp.float32),
-            VMEM((9, total, LANES), jnp.int32),
-            VMEM((9, total, LANES), jnp.int32),
-            VMEM((9, prec_cells, LANES), jnp.int32),
-            VMEM((9, prec_cells, LANES), jnp.int32),
-            VMEM((flow_rows + 2, cells + 16, LANES), jnp.int32),
-            VMEM((3, prec_cells + 16, LANES), jnp.int32),
-            VMEM((total, LANES), jnp.int32),
-            VMEM((prec_cells, LANES), jnp.int32),
-            SMEM((total // 8 + prec_cells // 8,), jnp.int32),
-        ],
+        scratch_shapes=scratches(flow_rows, cells, prec_cells),
         compiler_params=big,
         name="force",
-    )(ends, msort, psort, mraw, praw, mrank, prank, below, above, side, outlet_bin, push)
+    )(ends, got[:, 0:2].reshape(-1), me, main_count[0], share, count_column, coef, got,
+      msort, psort, mraw, praw, mrank, prank, below, above, side, outlet_bin)
     return tuple(planes(v) for v in outs)
 
 

time: 113 us -> 127 us (1.12)
  Pallas kernels: 106 us -> 118 us
  local copies, waits for them, and re-layouts: 4.51 us -> 7.41 us
    pallas_call x1, Pallas kernels: 64.9 us -> 82.7 us  [shards(): pl.pallas_call(force_kernel, out_shape=(out_main, out_main, out_main, out...]
    pallas_call x4 -> x2, Pallas kernels: 41.3 us -> 35.3 us  [the longest x1 25.1 us: shards(): pl.pallas_call(link_kernel, out_shape=(shape((trans_devices, 8, LANES)),...]
    unnamed x30 -> x24, local copies, waits for them, and re-layouts: 4.36 us -> 5.19 us
where the time goes in v3:
time: 127 us; the launch traced here: 126 us
  Pallas kernels  118 us (93%)
  local copies, waits for them, and re-layouts  7.41 us (6%)
    pallas_call x1, Pallas kernels, shards(): pl.pallas_call(force_kernel, out_shape=(out_main, out_main, out_main, out...  82.7 us
    pallas_call x1, Pallas kernels, shards(): pl.pallas_call(link_kernel, out_shape=(shape((trans_devices, 8, LANES)),...  25.1 us
    pallas_call x1, Pallas kernels, shards(): pl.pallas_call(prep_kernel, out_shape=(shape((8, LANES)), shape((8, flow_...  10.2 us
    unnamed x24, local copies, waits for them, and re-layouts  5.19 us

profile of v3, /device:TPU:199, one launch (start us, length us, event | category | flops | bytes accessed | tf_op | source)
XLA Modules:
  0.0 126.2 jit_solution(13229146082973550284)
XLA Ops:
  0.6 0.0 copy-start.4
  0.7 0.1 add_convert_fusion.end_ref
  0.7 0.7 pad_bitcast_fusion.coef_ref
  1.4 0.7 slice_bitcast_fusion.count0_ref
  2.1 0.0 copy-start.3
  2.1 0.0 copy-start.8
  2.1 0.0 copy-start.9
  2.1 0.0 copy-start.10
  2.1 0.0 copy-start.11
  2.1 0.9 reshape.20.count_ref
  3.0 0.0 copy-done.4
  3.0 0.0 copy-done.3
  3.0 0.0 copy-done.8
  3.0 0.0 copy-done.9
  3.0 0.0 copy-done.10
  3.0 0.0 copy-done.11
  3.0 0.0 copy-start
  3.0 0.9 copy-done
  4.0 0.0 copy-start.1
  4.0 0.9 copy-done.1
  4.9 0.0 copy-start.2
  4.9 0.9 copy-done.2
  5.8 0.0 copy-start.5
  5.8 0.8 copy-done.5
  6.6 0.0 copy-start.6
  6.6 0.8 copy-done.6
  7.4 0.0 copy-start.7
  7.4 0.8 copy-done.7
  8.2 10.2 %prep.1 = (f32[8,128]{1,0:T(8,128)S(1)}, f32[8,2,64,128]{3,2,1,0:T(8,128)S(1)}, f32[8,1,32,128]{3,2,1,0:T(8,128)S(1)}, f32[7,128,128]{2,1,0:T(8,128)S(1)}, f32[7...) custom-call(s32[16]{0:T(128)S(1)} %copy-done.9, ...), custom_call_target="tpu_custom_call" | custom-call | tf_op jit(solution)/shard_map/prep/pallas_call | solution.py:607
  18.4 25.1 %link.1 = (f32[32,8,128]{2,1,0:T(8,128)S(1)}, f32[8,96,128]{2,1,0:T(8,128)S(1)}, f32[8,96,128]{2,1,0:T(8,128)S(1)}, f32[6,8,8,128]{3,2,1,0:T(8,128)S(1)}) custom-call(f32[8,128]{1,0:T(8,128)S(1)} %get-tuple-element.25.own_ref, f32[8,2,64,128]{3,2,1,0:T(8,128)S(1)} %get-tuple-element.26.msort_ref, f32[8,1,32,128]{3,2,1,0:T(8,128)S(1)} %get-tuple-element.27.psort_ref, ...), custom_call_target="tpu_custom_call" | custom-call | tf_op jit(solution)/shard_map/link/pallas_call | solution.py:628
  43.5 82.7 %force.1 = (f32[2,3,64,128]{3,2,1,0:T(8,128)}, f32[2,3,64,128]{3,2,1,0:T(8,128)}, f32[2,3,64,128]{3,2,1,0:T(8,128)}, f32[1,3,32,128]{3,2,1,0:T(8,128)}, f32[1,3,...) custom-call(s32[4]{0:T(128)S(1)} %add_convert_fusion.end_ref, f32[8192]{0:T(1024)S(1)} %bitcast.26, f32[1]{0:T(128)} %bitcast.11.me_ref, ...), custom_call_target="tpu_custom_call" | custom-call | tf_op jit(solution)/shard_map/force/pallas_call | solution.py:649
  (1 shorter events, 0.0 us)
Async XLA Ops:
  0.6 2.3 %copy-start.4 = (s32[2,64,128]{2,1,0:T(8,128)S(1)}, s32[2,64,128]{2,1,0:T(8,128)}, u32[]{:S(2)}) copy-start(s32[2,64,128]{2,1,0:T(8,128)} %mseed_ref.1) | copy-start | bytes 196612
  2.1 0.9 copy-start.3
  2.1 0.9 copy-start.8
  2.1 0.9 copy-start.9
  2.1 0.9 copy-start.10
  2.1 0.9 copy-start.11
  3.0 0.9 copy-start
  4.0 0.9 copy-start.1
  4.9 0.9 copy-start.2
  5.8 0.8 copy-start.5
  6.6 0.8 copy-start.6
  7.4 0.8 copy-start.7

commit v4 on v3

--- a/solution.py
+++ b/solution.py
@@ -38,13 +38,20 @@
     return lax.broadcasted_iota(jnp.int32, (rows, LANES), 1)
 
 
+def column_of(row):
+    n = row.shape[1]
+    here = (lax.broadcasted_iota(jnp.int32, (n, n), 0) == lax.broadcasted_iota(jnp.int32, (n, n), 1))
+    wide = jnp.where(here, jnp.broadcast_to(row.astype(jnp.float32), (n, n)), 0.0)
+    return jnp.sum(wide, axis=1, keepdims=True).astype(jnp.int32)
+
+
 def centred(seed):
     code = seed + 1
     code = jnp.where(code > 2046, code - seed_modulus, code)
     return jnp.where(code > 2046, code - seed_modulus, code)
 
 
-def first_tile(row_ref, dest_ref, cell_ref, count_ref, arrays, seed_ref, bin_ref, out_ref):
+def first_tile(row_ref, dest_ref, cell_ref, last_count, arrays, seed_ref, bin_ref, out_ref):
     rows = row_ref.shape[0]
     lane = lane_iota(1)
     lines = [jnp.zeros((1, LANES), jnp.float32) for _ in range(2)]
@@ -63,11 +70,10 @@
                 put(3 * a + c, q, jnp.sum(value, axis=1, keepdims=True))
         seed = jnp.where(hit, seed_ref[0, pl.ds(cell, 1), :].astype(jnp.float32), 0.0)
         put(9, q, jnp.sum(seed, axis=1, keepdims=True))
-        put(10, q, dest_ref[q].astype(jnp.float32))
-        put(11, q, cell_ref[q].astype(jnp.float32))
+        place = dest_ref[q] * bin_ref.shape[0] + cell_ref[q]
+        put(10, q, place.astype(jnp.float32))
     cells = bin_ref.shape[0]
-    last = count_ref.shape[0] - cells
-    bins = jnp.where(lane_iota(cells) < count_ref[last:, :], bin_ref[...], BINS)
+    bins = jnp.where(lane_iota(cells) < last_count, bin_ref[...], BINS)
     profile = jnp.zeros((1, LANES), jnp.float32)
     for b in range(BINS):
         hits = jnp.sum((bins == b).astype(jnp.float32), axis=0, keepdims=True)
@@ -99,8 +105,18 @@
         pl.semaphore_signal(barrier, inc=1, device_id=at(0, s), device_id_type=mesh_id)
         return carry
 
-    lax.fori_loop(1, count, greet, 0)
-    pl.semaphore_wait(barrier, len(across) + count - 1)
+    meets = (flow == 0) | (flow == flows - 1)
+
+    @pl.when(meets)
+    def _():
+        lax.fori_loop(1, count, greet, 0)
+
+    @pl.when(jnp.logical_not(meets))
+    def _():
+        greet(1, 0)
+        greet(count - 1, 0)
+
+    pl.semaphore_wait(barrier, len(across) + jnp.where(meets, count - 1, 2))
     main_part, prec_part = pl.ds(0, cells), pl.ds(cells, prec_cells)
     plan = [
         (msort_ref.at[:, flow_rows - 1], below_ref.at[:, main_part], (1, 0)),
@@ -137,9 +153,16 @@
         tile(s, trans).wait_send()
         return carry
 
-    lax.fori_loop(1, count, send, 0)
-    got_ref[trans] = own_ref[...]
-    lax.fori_loop(1, count, finish, 0)
+    @pl.when(meets)
+    def _():
+        lax.fori_loop(1, count, send, 0)
+        got_ref[trans] = own_ref[...]
+        lax.fori_loop(1, count, finish, 0)
+
+    @pl.when(jnp.logical_not(meets))
+    def _():
+        got_ref[...] = jnp.zeros(got_ref.shape, jnp.float32)
+
     for copy in copies:
         copy.wait()
 
@@ -191,7 +214,9 @@
         load.start()
     for load in loads[:5]:
         load.wait()
-    first_tile(row_ref, dest_ref, cell_ref, count_ref, (ppos_in, pvel_in, pforce_in), pseed_in,
+    flow_rows, cells = mseed_in.shape[0], mseed_in.shape[1]
+    counts = [column_of(count_ref[f : f + 1, :]) for f in range(flow_rows)]
+    first_tile(row_ref, dest_ref, cell_ref, counts[-1], (ppos_in, pvel_in, pforce_in), pseed_in,
                bin_in, own_ref)
     flow_rows, cells = mseed_in.shape[0], mseed_in.shape[1]
     prec_cells = pseed_in.shape[1]
@@ -225,7 +250,7 @@
         load.wait()
     for f in range(flow_rows):
         at = f * cells
-        occupied = lane_iota(cells) < count_ref[at : at + cells, :]
+        occupied = lane_iota(cells) < counts[f]
         finish((mpos_in, mvel_in, mforce_in), f, jnp.where(occupied, mseed_in[f], -1), cells,
                msort_ref, mrank_ref, mraw_ref, at)
     left_ref[...] = jnp.zeros(left_ref.shape, jnp.float32)
@@ -243,8 +268,8 @@
     return first_at_least(height, edges, height.shape[0]).astype(jnp.float32)
 
 
-def arrivals(me, pay_ref, count0_ref, count_ref, j_ref, raw_ref, rank_ref, filled_ref):
-    cells = count0_ref.shape[0]
+def arrivals(first, place_ref, pay_ref, count0_ref, count_ref, j_ref, raw_ref, rank_ref, filled_ref):
+    cells = count0_ref.shape[1]
     per = 16
     stride = 2 * LANES
     sources = pay_ref.shape[0] // stride
@@ -254,33 +279,33 @@
         filled_ref[row] = jnp.sum(real).astype(jnp.int32)
 
     def fill(cell, carry):
-        filled_ref[8 + cell] = count0_ref[cell]
+        filled_ref[8 + cell] = count0_ref[0, cell]
         return carry
 
     lax.fori_loop(0, cells, fill, 0)
 
-    def near(origin):
-        return jnp.abs(pay_ref[origin + 10 * per] - me) < 1.5
+    def place(source, u):
+        return place_ref[source * per + u] - first
+
+    def near(row):
+        return (row >= 7) & (row <= 8 + cells)
 
     def look(source, carry):
         start = source * stride
-        found = near(start)
+        found = near(place(source, 0))
         for u in range(1, per):
-            found = found | near(start + u)
+            found = found | near(place(source, u))
 
         @pl.when(found)
         def _():
-            def one(u, inner):
+            for u in range(per):
                 origin = start + u
-                off = pay_ref[origin + 10 * per] - me
-                cell = pay_ref[origin + 11 * per].astype(jnp.int32)
-                own = off == 0.0
-                before = (off == -1.0) & (cell == cells - 1)
-                after = (off == 1.0) & (cell == 0)
-
-                @pl.when(own | before | after)
-                def _():
-                    row = jnp.where(own, 8 + cell, jnp.where(before, 7, 8 + cells))
+                row = place(source, u)
+
+                @pl.when(near(row))
+                def _(row=row, origin=origin):
+                    cell = row - 8
+                    own = (cell >= 0) & (cell < cells)
                     slot = filled_ref[row]
                     filled_ref[row] = slot + 1
                     hit = lane == slot
@@ -296,14 +321,10 @@
                         j_ref[c, 1, pl.ds(row, 1), :] = jnp.where(hit, fields[c], old)
 
                     @pl.when(own)
-                    def _():
-                        for c, value in enumerate(moved + half + [state[9]]):
+                    def _(cell=cell, hit=hit, values=moved + half + [state[9]]):
+                        for c, value in enumerate(values):
                             old = raw_ref[c, pl.ds(cell, 1), :]
                             raw_ref[c, pl.ds(cell, 1), :] = jnp.where(hit, value, old)
-
-                return inner
-
-            lax.fori_loop(0, per, one, 0)
 
         return carry
 
@@ -314,7 +335,7 @@
     j_ref[7, 1] = starts_of(j_ref[2, 1])
     back = sorted_lanes(order[8 : 8 + cells, :])
     lanes = lane_iota(cells)
-    listed = jnp.where(lanes < count_ref[0:cells, :], rank_ref[0:cells, :], lanes)
+    listed = jnp.where(lanes < column_of(count_ref[0:1, :]), rank_ref[0:cells, :], lanes)
     rank_ref[0:cells, :] = take(back, listed)
 
 
@@ -458,13 +479,13 @@
             i_ref[c * SHARE + v, at : at + cells, :] = field
 
 
-def force_kernel(end_ref, pay_ref, me_ref, count0_ref, share_ref, count_ref, coef_ref, got_ref,
+def force_kernel(end_ref, place_ref, pay_ref, count0_ref, share_ref, count_ref, coef_ref, got_ref,
                  msort_ref, psort_ref, mraw_in, praw_ref, mrank_in, prank_ref,
                  below_ref, above_ref, side_ref, bin_ref,
                  mpos_out, mvel_out, mforce_out, ppos_out, pvel_out, pforce_out,
                  mj_ref, pj_ref, mi_ref, pi_ref, mbase_ref, mcount_ref, pbase_ref, pcount_ref,
                  mheld_ref, pheld_ref, mreach_ref, preach_ref, steps_ref,
-                 mraw_ref, mrank_ref, filled_ref):
+                 mraw_ref, mrank_ref, filled_ref, push_ref):
     flow_rows, cells = msort_ref.shape[1], msort_ref.shape[2]
     prec_cells = psort_ref.shape[2]
     ends = tuple(end_ref[e] > 0 for e in range(4))
@@ -476,12 +497,15 @@
     mraw_ref[...] = mraw_in[...]
     mrank_ref[...] = mrank_in[...]
 
-    @pl.when(me_ref[0] >= 0.0)
+    @pl.when(end_ref[0] == 0)
     def _():
-        arrivals(me_ref[0], pay_ref, count0_ref, count_ref, mj_ref, mraw_ref, mrank_ref, filled_ref)
-
-    push_row = -coef_ref[...] * (jnp.sum(got_ref[:, 2:3, :], axis=0) * share_ref[0])
-    push_row = jnp.broadcast_to(push_row, (8, LANES))
+        arrivals(end_ref[4], place_ref, pay_ref, count0_ref, count_ref, mj_ref, mraw_ref, mrank_ref,
+                 filled_ref)
+
+    profile = jnp.sum(got_ref[:, 2:3, :], axis=0)[:, 0:BINS]
+    push_ref[...] = jnp.zeros(push_ref.shape, jnp.float32)
+    push_ref[:, 0:BINS] = jnp.broadcast_to(-coef_ref[...] * (profile * share_ref[0]), (8, BINS))
+    push_row = push_ref[...]
     for j_ref, held_ref, n in ((mj_ref, mheld_ref, cells), (pj_ref, pheld_ref, prec_cells)):
         for f in range(held_ref.shape[0]):
             real = (j_ref[2, f, 0 : n + 16, :] < 500.0).astype(jnp.float32)
@@ -563,6 +587,7 @@
         VMEM((7, total, LANES), jnp.float32),
         VMEM((total, LANES), jnp.int32),
         SMEM((cells + 16,), jnp.int32),
+        VMEM((8, LANES), jnp.float32),
     ]
 
 
@@ -589,7 +614,6 @@
     flow_devices = lax.axis_size("flow")
     trans_devices = lax.axis_size("trans")
     total = flow_rows * cells
-    count_column = main_count.reshape(total, 1)
     big = pltpu.CompilerParams(vmem_limit_bytes=48 << 20)
 
     def planes(value):
@@ -600,8 +624,6 @@
 
     share = BINS / (cells * trans_devices * LANES)
     share = jnp.where(flow_index == flow_devices - 1, jnp.float32(share), 0.0)[None]
-    coef = jnp.concatenate([outlet_coef, jnp.zeros((LANES - BINS,), jnp.float32)])[None]
-    me = jnp.where(flow_index == 0, trans_index, -9).astype(jnp.float32)[None]
 
     inputs = [outlet_bin, *prec_state, prec_seed, *main_state, main_seed]
     own, msort, psort, mraw, praw, mrank, prank, left, right = pl.pallas_call(
@@ -617,12 +639,12 @@
             shape((8, 8, LANES)),
             shape((8, 8, LANES)),
         ),
-        in_specs=whole(SMEM, 3) + whole(VMEM, 1) + whole(pl.ANY, 9),
+        in_specs=whole(SMEM, 3) + whole(VMEM, 1) + whole(pltpu.HBM, 9),
         out_specs=tuple(whole(VMEM, 9)),
         scratch_shapes=[VMEM(v.shape, v.dtype) for v in inputs] + [pltpu.SemaphoreType.DMA((9,))],
         compiler_params=big,
         name="prep",
-    )(cross_row, cross_dest, cross_cell, count_column, *inputs)
+    )(cross_row, cross_dest, cross_cell, main_count, *inputs)
 
     span = cells + prec_cells
     got, below, above, side = pl.pallas_call(
@@ -642,6 +664,7 @@
         flow_index < flow_devices - 1,
         trans_index > 0,
         trans_index < trans_devices - 1,
+        trans_index * cells - 8,
     ]).astype(jnp.int32)
 
     out_main = shape((flow_rows, 3, cells, LANES))
@@ -654,7 +677,8 @@
         scratch_shapes=scratches(flow_rows, cells, prec_cells),
         compiler_params=big,
         name="force",
-    )(ends, got[:, 0:2].reshape(-1), me, main_count[0], share, count_column, coef, got,
+    )(ends, got[:, 1, 32:48].reshape(-1).astype(jnp.int32), got[:, 0:2].reshape(-1), main_count,
+      share, main_count, outlet_coef[None], got,
       msort, psort, mraw, praw, mrank, prank, below, above, side, outlet_bin)
     return tuple(planes(v) for v in outs)
 

time: 127 us -> 116 us (0.913)
  Pallas kernels: 118 us -> 108 us
    pallas_call x1, Pallas kernels: 82.7 us -> 73.5 us  [shards(): pl.pallas_call(force_kernel, out_shape=(out_main, out_main, out_main, out...]
    unnamed x24 -> x28, local copies, waits for them, and re-layouts: 5.19 us -> 7.37 us
where the time goes in v4:
time: 116 us
  Pallas kernels  108 us (93%)
  local copies, waits for them, and re-layouts  7.55 us (7%)
    pallas_call x1, Pallas kernels, shards(): pl.pallas_call(force_kernel, out_shape=(out_main, out_main, out_main, out...  73.5 us
    pallas_call x1, Pallas kernels, shards(): pl.pallas_call(link_kernel, out_shape=(shape((trans_devices, 8, LANES)),...  24 us
    pallas_call x1, Pallas kernels, shards(): pl.pallas_call(prep_kernel, out_shape=(shape((8, LANES)), shape((8, flow_...  10.1 us
    unnamed x28, local copies, waits for them, and re-layouts  7.37 us

profile of v4, /device:TPU:199, one launch (start us, length us, event | category | flops | bytes accessed | tf_op | source)
XLA Modules:
  0.0 116.0 jit_solution(3546497050102314635)
XLA Ops:
  0.6 0.0 copy-start.3
  0.7 0.0 copy-start.8
  0.7 0.1 stack.39.end_ref
  0.8 0.0 copy-start.11
  0.8 0.0 copy-start.12
  0.8 0.0 copy-start.9
  0.8 0.0 copy-start.10
  0.8 0.6 copy-done.3
  1.4 0.0 copy-done.8
  1.4 0.0 copy-done.11
  1.4 0.0 copy-done.12
  1.4 0.0 copy-done.9
  1.5 0.0 copy-done.10
  1.5 0.0 copy-start
  1.5 0.9 copy-done
  2.4 0.0 copy-start.1
  2.4 0.9 copy-done.1
  3.3 0.0 copy-start.2
  3.3 0.9 copy-done.2
  4.3 0.0 copy-start.4
  4.3 0.8 copy-done.4
  5.1 0.0 copy-start.5
  5.1 0.8 copy-done.5
  5.9 0.0 copy-start.6
  5.9 0.8 copy-done.6
  6.7 0.0 copy-start.7
  6.7 0.8 copy-done.7
  7.5 10.1 %prep.1 = (f32[8,128]{1,0:T(8,128)S(1)}, f32[8,2,64,128]{3,2,1,0:T(8,128)S(1)}, f32[8,1,32,128]{3,2,1,0:T(8,128)S(1)}, f32[7,128,128]{2,1,0:T(8,128)S(1)}, f32[7...) custom-call(s32[16]{0:T(128)S(1)} %copy-done.10, ...), custom_call_target="tpu_custom_call" | custom-call | tf_op jit(solution)/shard_map/prep/pallas_call | solution.py:629
  17.6 24.0 %link.1 = (f32[32,8,128]{2,1,0:T(8,128)S(1)}, f32[8,96,128]{2,1,0:T(8,128)S(1)}, f32[8,96,128]{2,1,0:T(8,128)S(1)}, f32[6,8,8,128]{3,2,1,0:T(8,128)S(1)}) custom-call(f32[8,128]{1,0:T(8,128)S(1)} %get-tuple-element.25.own_ref, f32[8,2,64,128]{3,2,1,0:T(8,128)S(1)} %get-tuple-element.26.msort_ref, f32[8,1,32,128]{3,2,1,0:T(8,128)S(1)} %get-tuple-element.27.psort_ref, ...), custom_call_target="tpu_custom_call" | custom-call | tf_op jit(solution)/shard_map/link/pallas_call | solution.py:650
  41.6 0.1 convert_reduce_fusion
  41.7 0.1 convert_element_type.10.place_ref
  41.8 0.0 copy-start.13
  41.8 0.6 copy-done.13
  42.5 73.5 %force.1 = (f32[2,3,64,128]{3,2,1,0:T(8,128)}, f32[2,3,64,128]{3,2,1,0:T(8,128)}, f32[2,3,64,128]{3,2,1,0:T(8,128)}, f32[1,3,32,128]{3,2,1,0:T(8,128)}, f32[1,3,...) custom-call(s32[5]{0:T(128)S(1)} %stack.39.end_ref, s32[512]{0:T(512)S(1)} %convert_element_type.10.place_ref, ...), custom_call_target="tpu_custom_call" | custom-call | tf_op jit(solution)/shard_map/force/pallas_call | solution.py:672
  (1 shorter events, 0.0 us)
Async XLA Ops:
  0.6 0.8 copy-start.3
  0.7 0.7 copy-start.8
  0.8 0.7 copy-start.11
  0.8 0.7 copy-start.12
  0.8 0.7 copy-start.9
  0.8 0.7 copy-start.10
  1.5 0.9 copy-start
  2.4 0.9 copy-start.1
  3.3 0.9 copy-start.2
  4.3 0.8 copy-start.4
  5.1 0.8 copy-start.5
  5.9 0.8 copy-start.6
  6.7 0.8 copy-start.7
  41.8 0.7 copy-start.13

commit v5 on v4

--- a/solution.py
+++ b/solution.py
@@ -167,25 +167,24 @@
         copy.wait()
 
 
-def sorted_lanes(key):
+def sorted_keys(key):
     rows = key.shape[0]
     lane = lane_iota(rows)
-    held = key * LANES + lane
     size = 2
     while size <= LANES:
         dist = size // 2
         while dist >= 1:
             low = ((lane & size) == 0) == ((lane & dist) == 0)
-            other = take(held, lane ^ dist)
-            held = jnp.where(low, jnp.minimum(held, other), jnp.maximum(held, other))
+            other = take(key, lane ^ dist)
+            key = jnp.where(low, jnp.minimum(key, other), jnp.maximum(key, other))
             dist //= 2
         size *= 2
-    return held & (LANES - 1)
-
-
-def height_order(height):
+    return key
+
+
+def height_keys(height):
     level = jnp.minimum(height, 16.25) * float(1 << 19)
-    return sorted_lanes(level.astype(jnp.int32))
+    return level.astype(jnp.int32) * LANES + lane_iota(height.shape[0])
 
 
 def first_at_least(sorted_rows, bound, rows):
@@ -198,61 +197,56 @@
     return jnp.where(take(sorted_rows, at) < bound, at + 1, at)
 
 
-def prep_kernel(row_ref, dest_ref, cell_ref, count_ref,
-                bin_ref, ppos_ref, pvel_ref, pforce_ref, pseed_ref,
-                mpos_ref, mvel_ref, mforce_ref, mseed_ref,
-                own_ref, msort_ref, psort_ref, mraw_ref, praw_ref, mrank_ref, prank_ref,
-                left_ref, right_ref,
-                bin_in, ppos_in, pvel_in, pforce_in, pseed_in,
-                mpos_in, mvel_in, mforce_in, mseed_in, sem_ref):
-    outside = (ppos_ref, pvel_ref, pforce_ref, pseed_ref, bin_ref, mpos_ref, mvel_ref, mforce_ref,
-               mseed_ref)
-    inside = (ppos_in, pvel_in, pforce_in, pseed_in, bin_in, mpos_in, mvel_in, mforce_in, mseed_in)
-    loads = [pltpu.make_async_copy(a, b, sem_ref.at[n])
-             for n, (a, b) in enumerate(zip(outside, inside))]
-    for load in loads:
-        load.start()
-    for load in loads[:5]:
-        load.wait()
-    flow_rows, cells = mseed_in.shape[0], mseed_in.shape[1]
-    counts = [column_of(count_ref[f : f + 1, :]) for f in range(flow_rows)]
-    first_tile(row_ref, dest_ref, cell_ref, counts[-1], (ppos_in, pvel_in, pforce_in), pseed_in,
-               bin_in, own_ref)
-    flow_rows, cells = mseed_in.shape[0], mseed_in.shape[1]
-    prec_cells = pseed_in.shape[1]
-
-    def finish(arrays, f, seed, rows, sort_ref, rank_ref, raw_out, at):
+def sort_state(pos_ref, vel_ref, force_ref, seeds, sort_ref, rank_ref, raw_out):
+    flow_rows, rows = len(seeds), seeds[0].shape[0]
+    fields, keys = [], []
+    for f, seed in enumerate(seeds):
+        at = f * rows
         occupied = seed >= 0
-        pos, vel, force = [[ref[f, c] for c in range(3)] for ref in arrays]
-        half = [vel[c] + 0.5 * time_step * force[c] for c in range(3)]
-        moved = [pos[c] + time_step * half[c] for c in range(3)]
+        half = [vel_ref[f, c] + 0.5 * time_step * force_ref[f, c] for c in range(3)]
+        moved = [pos_ref[f, c] + time_step * half[c] for c in range(3)]
         for c in range(3):
             raw_out[c, at : at + rows, :] = moved[c]
             raw_out[3 + c, at : at + rows, :] = half[c]
         raw_out[6, at : at + rows, :] = seed.astype(jnp.float32)
         height = moved[2] - box_height * jnp.floor(moved[2] * (1.0 / box_height))
         height = jnp.where(occupied, height, nowhere)
-        order = height_order(height)
-        rank_ref[at : at + rows, :] = sorted_lanes(order)
         hashed = centred(seed).astype(jnp.float32) / seed_modulus
-        fields = [moved[0], moved[1], None] + [drag * v for v in half] + [hashed]
-        for c, field in enumerate(fields):
-            if field is None:
-                height = take(height, order)
-                sort_ref[c, f, :, :] = height
-            else:
-                sort_ref[c, f, :, :] = take(jnp.where(occupied, field, 0.0), order)
-        sort_ref[7, f, :, :] = starts_of(height)
-
-    finish((ppos_in, pvel_in, pforce_in), 0, pseed_in[0], prec_cells, psort_ref, prank_ref,
-           praw_ref, 0)
-    for load in loads[5:]:
-        load.wait()
+        fields.append([jnp.where(occupied, v, 0.0) if c != 2 else height for c, v in enumerate(
+            moved[0:2] + [height] + [drag * v for v in half] + [hashed])])
+        keys.append(height_keys(height))
+    key = jnp.concatenate(keys, axis=0)
+    total = flow_rows * rows
+    ordered = sorted_keys(key)
+    order = ordered & (LANES - 1)
+    rank_ref[...] = first_at_least(ordered, key, total)
+    for c in range(7):
+        field = take(jnp.concatenate([v[c] for v in fields], axis=0), order)
+        if c == 2:
+            starts = starts_of(field)
+        for f in range(flow_rows):
+            sort_ref[c, f] = field[f * rows : (f + 1) * rows]
     for f in range(flow_rows):
-        at = f * cells
-        occupied = lane_iota(cells) < counts[f]
-        finish((mpos_in, mvel_in, mforce_in), f, jnp.where(occupied, mseed_in[f], -1), cells,
-               msort_ref, mrank_ref, mraw_ref, at)
+        sort_ref[7, f] = starts[f * rows : (f + 1) * rows]
+
+
+def prec_kernel(row_ref, dest_ref, cell_ref, count_ref, bin_ref, pos_ref, vel_ref, force_ref,
+                seed_ref, own_ref, sort_ref, raw_ref, rank_ref):
+    last = count_ref.shape[0] - 1
+    first_tile(row_ref, dest_ref, cell_ref, column_of(count_ref[last : last + 1, :]),
+               (pos_ref, vel_ref, force_ref), seed_ref, bin_ref, own_ref)
+    sort_state(pos_ref, vel_ref, force_ref, [seed_ref[0]], sort_ref, rank_ref, raw_ref)
+
+
+def main_kernel(count_ref, pos_ref, vel_ref, force_ref, seed_ref, psort_ref,
+                msort_ref, raw_ref, rank_ref, left_ref, right_ref):
+    flow_rows, cells = seed_ref.shape[0], seed_ref.shape[1]
+    prec_cells = psort_ref.shape[2]
+    seeds = [
+        jnp.where(lane_iota(cells) < column_of(count_ref[f : f + 1, :]), seed_ref[f], -1)
+        for f in range(flow_rows)
+    ]
+    sort_state(pos_ref, vel_ref, force_ref, seeds, msort_ref, rank_ref, raw_ref)
     left_ref[...] = jnp.zeros(left_ref.shape, jnp.float32)
     right_ref[...] = jnp.zeros(right_ref.shape, jnp.float32)
     for c in range(msort_ref.shape[0]):
@@ -268,12 +262,13 @@
     return first_at_least(height, edges, height.shape[0]).astype(jnp.float32)
 
 
-def arrivals(first, place_ref, pay_ref, count0_ref, count_ref, j_ref, raw_ref, rank_ref, filled_ref):
+def arrivals(first, place_ref, got_ref, count0_ref, count_ref, j_ref, raw_ref, rank_ref,
+             filled_ref, from_ref):
     cells = count0_ref.shape[1]
     per = 16
-    stride = 2 * LANES
-    sources = pay_ref.shape[0] // stride
+    sources = got_ref.shape[0]
     lane = lane_iota(1)
+    from_ref[...] = jnp.full(from_ref.shape, -1, jnp.int32)
     for row in (7, 8 + cells):
         real = (j_ref[2, 1, row : row + 1, :] < 500.0).astype(jnp.float32)
         filled_ref[row] = jnp.sum(real).astype(jnp.int32)
@@ -284,56 +279,61 @@
 
     lax.fori_loop(0, cells, fill, 0)
 
-    def place(source, u):
-        return place_ref[source * per + u] - first
-
     def near(row):
         return (row >= 7) & (row <= 8 + cells)
 
     def look(source, carry):
-        start = source * stride
-        found = near(place(source, 0))
+        rows = [place_ref[source * per + u] - first for u in range(per)]
+        found = near(rows[0])
         for u in range(1, per):
-            found = found | near(place(source, u))
+            found = found | near(rows[u])
 
         @pl.when(found)
         def _():
             for u in range(per):
-                origin = start + u
-                row = place(source, u)
-
-                @pl.when(near(row))
-                def _(row=row, origin=origin):
-                    cell = row - 8
-                    own = (cell >= 0) & (cell < cells)
+
+                @pl.when(near(rows[u]))
+                def _(row=rows[u], which=source * per + u):
                     slot = filled_ref[row]
                     filled_ref[row] = slot + 1
-                    hit = lane == slot
-                    state = [jnp.full((1, LANES), pay_ref[origin + c * per], jnp.float32)
-                             for c in range(10)]
-                    half = [state[3 + c] + 0.5 * time_step * state[6 + c] for c in range(3)]
-                    moved = [state[c] + time_step * half[c] for c in range(3)]
-                    height = moved[2] - box_height * jnp.floor(moved[2] * (1.0 / box_height))
-                    hashed = centred(state[9].astype(jnp.int32)).astype(jnp.float32) / seed_modulus
-                    fields = [moved[0], moved[1], height] + [drag * v for v in half] + [hashed]
-                    for c in range(7):
-                        old = j_ref[c, 1, pl.ds(row, 1), :]
-                        j_ref[c, 1, pl.ds(row, 1), :] = jnp.where(hit, fields[c], old)
-
-                    @pl.when(own)
-                    def _(cell=cell, hit=hit, values=moved + half + [state[9]]):
-                        for c, value in enumerate(values):
-                            old = raw_ref[c, pl.ds(cell, 1), :]
-                            raw_ref[c, pl.ds(cell, 1), :] = jnp.where(hit, value, old)
+                    old = from_ref[pl.ds(row, 1), :]
+                    from_ref[pl.ds(row, 1), :] = jnp.where(lane == slot, which, old)
 
         return carry
 
     lax.fori_loop(0, sources, look, 0)
-    order = height_order(j_ref[2, 1])
+    rows = from_ref.shape[0]
+    came = from_ref[...]
+    here = came >= 0
+    block, at = came // LANES, came & (LANES - 1)
+    lane8 = lane_iota(8)
+    mine = lane8 // per == lax.broadcasted_iota(jnp.int32, (8, LANES), 0)
+    state = []
+    for c in range(10):
+        value = jnp.zeros((rows, LANES), jnp.float32)
+        for a in range(sources * per // LANES):
+            line = got_ref[8 * a : 8 * a + 8, c // 8, :]
+            line = take(line, lane8 % per + (c % 8) * per)
+            line = jnp.sum(jnp.where(mine, line, 0.0), axis=0, keepdims=True)
+            part = take(jnp.broadcast_to(line, (rows, LANES)), at)
+            value = jnp.where(block == a, part, value)
+        state.append(value)
+    half = [state[3 + c] + 0.5 * time_step * state[6 + c] for c in range(3)]
+    moved = [state[c] + time_step * half[c] for c in range(3)]
+    height = moved[2] - box_height * jnp.floor(moved[2] * (1.0 / box_height))
+    hashed = centred(state[9].astype(jnp.int32)).astype(jnp.float32) / seed_modulus
+    inner = slice(8, 8 + cells)
+    for c, value in enumerate(moved + half + [state[9]]):
+        raw_ref[c, 0:cells, :] = jnp.where(here[inner], value[inner], raw_ref[c, 0:cells, :])
+    fields = [moved[0], moved[1], height] + [drag * v for v in half] + [hashed]
+    fields = [jnp.where(here, fields[c], j_ref[c, 1]) for c in range(7)]
+    key = height_keys(fields[2])
+    ordered = sorted_keys(key)
+    order = ordered & (LANES - 1)
     for c in range(7):
-        j_ref[c, 1] = take(j_ref[c, 1], order)
+        j_ref[c, 1] = take(fields[c], order)
     j_ref[7, 1] = starts_of(j_ref[2, 1])
-    back = sorted_lanes(order[8 : 8 + cells, :])
+    back = first_at_least(ordered, key, rows)[inner]
     lanes = lane_iota(cells)
     listed = jnp.where(lanes < column_of(count_ref[0:1, :]), rank_ref[0:cells, :], lanes)
     rank_ref[0:cells, :] = take(back, listed)
@@ -479,13 +479,14 @@
             i_ref[c * SHARE + v, at : at + cells, :] = field
 
 
-def force_kernel(end_ref, place_ref, pay_ref, count0_ref, share_ref, count_ref, coef_ref, got_ref,
+def force_kernel(end_ref, place_ref, count0_ref, share_ref, count_ref, coef_ref, got_ref,
                  msort_ref, psort_ref, mraw_in, praw_ref, mrank_in, prank_ref,
                  below_ref, above_ref, side_ref, bin_ref,
                  mpos_out, mvel_out, mforce_out, ppos_out, pvel_out, pforce_out,
                  mj_ref, pj_ref, mi_ref, pi_ref, mbase_ref, mcount_ref, pbase_ref, pcount_ref,
                  mheld_ref, pheld_ref, mreach_ref, preach_ref, steps_ref,
-                 mraw_ref, mrank_ref, filled_ref, push_ref):
+                 mraw_ref, mrank_ref, filled_ref, push_ref,
+                 from_ref):
     flow_rows, cells = msort_ref.shape[1], msort_ref.shape[2]
     prec_cells = psort_ref.shape[2]
     ends = tuple(end_ref[e] > 0 for e in range(4))
@@ -499,8 +500,8 @@
 
     @pl.when(end_ref[0] == 0)
     def _():
-        arrivals(end_ref[4], place_ref, pay_ref, count0_ref, count_ref, mj_ref, mraw_ref, mrank_ref,
-                 filled_ref)
+        arrivals(end_ref[4], place_ref, got_ref, count0_ref, count_ref, mj_ref, mraw_ref, mrank_ref,
+                 filled_ref, from_ref)
 
     profile = jnp.sum(got_ref[:, 2:3, :], axis=0)[:, 0:BINS]
     push_ref[...] = jnp.zeros(push_ref.shape, jnp.float32)
@@ -588,6 +589,7 @@
         VMEM((total, LANES), jnp.int32),
         SMEM((cells + 16,), jnp.int32),
         VMEM((8, LANES), jnp.float32),
+        VMEM((cells + 16, LANES), jnp.int32),
     ]
 
 
@@ -625,26 +627,33 @@
     share = BINS / (cells * trans_devices * LANES)
     share = jnp.where(flow_index == flow_devices - 1, jnp.float32(share), 0.0)[None]
 
-    inputs = [outlet_bin, *prec_state, prec_seed, *main_state, main_seed]
-    own, msort, psort, mraw, praw, mrank, prank, left, right = pl.pallas_call(
-        prep_kernel,
+    own, psort, praw, prank = pl.pallas_call(
+        prec_kernel,
         out_shape=(
             shape((8, LANES)),
+            shape((8, 1, prec_cells, LANES)),
+            shape((7, prec_cells, LANES)),
+            shape((prec_cells, LANES), jnp.int32),
+        ),
+        in_specs=whole(SMEM, 3) + whole(VMEM, 6),
+        out_specs=tuple(whole(VMEM, 4)),
+        compiler_params=big,
+        name="prec",
+    )(cross_row, cross_dest, cross_cell, main_count, outlet_bin, *prec_state, prec_seed)
+    msort, mraw, mrank, left, right = pl.pallas_call(
+        main_kernel,
+        out_shape=(
             shape((8, flow_rows, cells, LANES)),
-            shape((8, 1, prec_cells, LANES)),
             shape((7, total, LANES)),
-            shape((7, prec_cells, LANES)),
             shape((total, LANES), jnp.int32),
-            shape((prec_cells, LANES), jnp.int32),
             shape((8, 8, LANES)),
             shape((8, 8, LANES)),
         ),
-        in_specs=whole(SMEM, 3) + whole(VMEM, 1) + whole(pltpu.HBM, 9),
-        out_specs=tuple(whole(VMEM, 9)),
-        scratch_shapes=[VMEM(v.shape, v.dtype) for v in inputs] + [pltpu.SemaphoreType.DMA((9,))],
+        in_specs=whole(VMEM, 6),
+        out_specs=tuple(whole(VMEM, 5)),
         compiler_params=big,
-        name="prep",
-    )(cross_row, cross_dest, cross_cell, main_count, *inputs)
+        name="main",
+    )(main_count, *main_state, main_seed, psort)
 
     span = cells + prec_cells
     got, below, above, side = pl.pallas_call(
@@ -672,12 +681,12 @@
     outs = pl.pallas_call(
         force_kernel,
         out_shape=(out_main, out_main, out_main, out_prec, out_prec, out_prec),
-        in_specs=whole(SMEM, 5) + whole(VMEM, 13),
+        in_specs=whole(SMEM, 4) + whole(VMEM, 13),
         out_specs=tuple(whole(VMEM, 6)),
         scratch_shapes=scratches(flow_rows, cells, prec_cells),
         compiler_params=big,
         name="force",
-    )(ends, got[:, 1, 32:48].reshape(-1).astype(jnp.int32), got[:, 0:2].reshape(-1), main_count,
+    )(ends, got[:, 1, 32:48].reshape(-1).astype(jnp.int32), main_count,
       share, main_count, outlet_coef[None], got,
       msort, psort, mraw, praw, mrank, prank, below, above, side, outlet_bin)
     return tuple(planes(v) for v in outs)

time: 116 us -> 116 us (level)
  Pallas kernels: 108 us -> 104 us
  local copies, waits for them, and re-layouts: 7.55 us -> 10.5 us
    pallas_call x1 -> x2, Pallas kernels: 10.1 us -> 6.4 us  [the longest x1 3.22 us: shards(): pl.pallas_call(prec_kernel, out_shape=(shape((8, LANES)), shape((8, 1, pr...]
    unnamed x28 -> x30, local copies, waits for them, and re-layouts: 7.37 us -> 10.3 us
where the time goes in v5:
time: 116 us; the launch traced here: 115 us
  Pallas kernels  104 us (90%)
  local copies, waits for them, and re-layouts  10.5 us (9%)
    pallas_call x1, Pallas kernels, shards(): pl.pallas_call(force_kernel, out_shape=(out_main, out_main, out_main, out...  73.5 us
    pallas_call x1, Pallas kernels, shards(): pl.pallas_call(link_kernel, out_shape=(shape((trans_devices, 8, LANES)),...  24 us
    unnamed x30, local copies, waits for them, and re-layouts  10.3 us
    pallas_call x1, Pallas kernels, shards(): pl.pallas_call(prec_kernel, out_shape=(shape((8, LANES)), shape((8, 1, pr...  3.22 us
    pallas_call x1, Pallas kernels, shards(): pl.pallas_call(main_kernel, out_shape=(shape((8, flow_rows, cells, LANES)...  3.18 us

profile of v5, /device:TPU:199, one launch (start us, length us, event | category | flops | bytes accessed | tf_op | source)
XLA Modules:
  0.0 115.2 jit_solution(9696755404032930184)
XLA Ops:
  0.6 0.0 copy-start.3
  0.6 0.0 copy-start
  0.7 0.1 stack.39.end_ref
  0.8 0.6 copy-done.3
  1.4 0.0 copy-start.5
  1.4 0.8 copy-done.5
  2.2 0.0 copy-start.6
  2.2 0.8 copy-done.6
  3.0 0.0 copy-start.7
  3.0 0.8 copy-done.7
  3.8 0.0 copy-start.8
  3.8 0.7 copy-done.8
  4.5 0.0 copy-start.10
  4.5 0.7 copy-done.10
  5.2 0.0 copy-start.11
  5.2 0.7 copy-done.11
  5.8 0.0 copy-start.12
  5.8 0.7 copy-done.12
  6.5 0.0 copy-start.13
  6.5 0.7 copy-done.13
  7.2 3.2 %prec.1 = (f32[8,128]{1,0:T(8,128)S(1)}, f32[8,1,32,128]{3,2,1,0:T(8,128)S(1)}, f32[7,32,128]{2,1,0:T(8,128)S(1)}, s32[32,128]{1,0:T(8,128)S(1)}) custom-call(s32[16]{0:T(128)S(1)} %copy-done.11, s32[16]{0:T(128)S(1)} %copy-done.12, s32[16]{0:T(128)S(1)} %copy-done.13, s32[2,64]{1,0:T(2,128)S(1)} %copy-done.8, s32[64,128]{1,0:T(8,128)S(1)} %copy-done.3, ...), custom_call_target="tpu_custom_call" | custom-call | tf_op jit(solution)/shard_map/prec/pallas_call | solution.py:630
  10.4 0.0 copy-start.9
  10.4 0.0 copy-done
  10.4 0.7 copy-done.9
  11.1 0.0 copy-start.1
  11.1 0.9 copy-done.1
  12.0 0.0 copy-start.2
  12.0 0.9 copy-done.2
  12.9 0.0 copy-start.4
  12.9 0.8 copy-done.4
  13.8 3.2 %main.1 = (f32[8,2,64,128]{3,2,1,0:T(8,128)S(1)}, f32[7,128,128]{2,1,0:T(8,128)S(1)}, s32[128,128]{1,0:T(8,128)S(1)}, f32[8,8,128]{2,1,0:T(8,128)S(1)}, f32[8,8,128]{2,1,0:T(8,128)S(1)}) custom-call(s32[2,64]{1,0:T(2,128)S(1)} %copy-done.9, f32[2,3,64,128]{3,2,1,0:T(8,128)S(1)} %bitcast.19, f32[2,3,64,128]{3,2,1,0:T(8,128)S(1)} %bitcast.20, ...), custom_call_target="tpu_custom_call" | custom-call | tf_op jit(solution)/shard_map/main/pallas_call | solution.py:643
  16.9 24.0 %link.1 = (f32[32,8,128]{2,1,0:T(8,128)S(1)}, f32[8,96,128]{2,1,0:T(8,128)S(1)}, f32[8,96,128]{2,1,0:T(8,128)S(1)}, f32[6,8,8,128]{3,2,1,0:T(8,128)S(1)}) custom-call(f32[8,128]{1,0:T(8,128)S(1)} %get-tuple-element.25.own_ref, f32[8,2,64,128]{3,2,1,0:T(8,128)S(1)} %get-tuple-element.27.msort_ref, f32[8,1,32,128]{3,2,1,0:T(8,128)S(1)} %get-tuple-element.26.psort_ref, ...), custom_call_target="tpu_custom_call" | custom-call | tf_op jit(solution)/shard_map/link/pallas_call | solution.py:659
  40.9 0.1 convert_reduce_fusion
  41.0 0.0 copy-start.14
  41.1 0.1 convert_element_type.10.place_ref
  41.1 0.6 copy-done.14
  41.7 73.5 %force.1 = (f32[2,3,64,128]{3,2,1,0:T(8,128)}, f32[2,3,64,128]{3,2,1,0:T(8,128)}, f32[2,3,64,128]{3,2,1,0:T(8,128)}, f32[1,3,32,128]{3,2,1,0:T(8,128)}, f32[1,3,...) custom-call(s32[5]{0:T(128)S(1)} %stack.39.end_ref, s32[512]{0:T(512)S(1)} %convert_element_type.10.place_ref, ...), custom_call_target="tpu_custom_call" | custom-call | tf_op jit(solution)/shard_map/force/pallas_call | solution.py:681
Async XLA Ops:
  0.6 0.8 copy-start.3
  0.6 9.8 %copy-start = (f32[2,64,3,128]{3,1,2,0:T(8,128)S(1)}, f32[2,64,3,128]{3,1,2,0:T(8,128)}, u32[]{:S(2)}) copy-start(f32[2,64,3,128]{3,1,2,0:T(8,128)} %param.14) | copy-start | bytes 589828
  1.4 0.8 copy-start.5
  2.2 0.8 copy-start.6
  3.0 0.8 copy-start.7
  3.8 0.7 copy-start.8
  4.5 0.7 copy-start.10
  5.2 0.7 copy-start.11
  5.8 0.7 copy-start.12
  6.5 0.7 copy-start.13
  10.4 0.7 copy-start.9
  11.1 0.9 copy-start.1
  12.0 0.9 copy-start.2
  12.9 0.8 copy-start.4
  41.0 0.7 copy-start.14

commit v6 on v5

--- a/solution.py
+++ b/solution.py
@@ -262,48 +262,23 @@
     return first_at_least(height, edges, height.shape[0]).astype(jnp.float32)
 
 
-def arrivals(first, place_ref, got_ref, count0_ref, count_ref, j_ref, raw_ref, rank_ref,
-             filled_ref, from_ref):
-    cells = count0_ref.shape[1]
+def arrivals(first, place_ref, got_ref, count_ref, j_ref, raw_ref, rank_ref):
+    cells = count_ref.shape[1]
     per = 16
-    sources = got_ref.shape[0]
-    lane = lane_iota(1)
-    from_ref[...] = jnp.full(from_ref.shape, -1, jnp.int32)
-    for row in (7, 8 + cells):
-        real = (j_ref[2, 1, row : row + 1, :] < 500.0).astype(jnp.float32)
-        filled_ref[row] = jnp.sum(real).astype(jnp.int32)
-
-    def fill(cell, carry):
-        filled_ref[8 + cell] = count0_ref[0, cell]
-        return carry
-
-    lax.fori_loop(0, cells, fill, 0)
-
-    def near(row):
-        return (row >= 7) & (row <= 8 + cells)
-
-    def look(source, carry):
-        rows = [place_ref[source * per + u] - first for u in range(per)]
-        found = near(rows[0])
-        for u in range(1, per):
-            found = found | near(rows[u])
-
-        @pl.when(found)
-        def _():
-            for u in range(per):
-
-                @pl.when(near(rows[u]))
-                def _(row=rows[u], which=source * per + u):
-                    slot = filled_ref[row]
-                    filled_ref[row] = slot + 1
-                    old = from_ref[pl.ds(row, 1), :]
-                    from_ref[pl.ds(row, 1), :] = jnp.where(lane == slot, which, old)
-
-        return carry
-
-    lax.fori_loop(0, sources, look, 0)
-    rows = from_ref.shape[0]
-    came = from_ref[...]
+    rows = j_ref.shape[2]
+    row = lax.broadcasted_iota(jnp.int32, (rows, LANES), 0)
+    order_of = lax.broadcasted_iota(jnp.int32, (LANES, LANES), 0)
+    upto = (order_of <= lane_iota(LANES)).astype(jnp.float32)
+    held = jnp.sum((j_ref[2, 1] < 500.0).astype(jnp.float32), axis=1, keepdims=True)
+    turn = lane_iota(rows).astype(jnp.float32) - held + 1.0
+    before = jnp.zeros((rows, 1), jnp.float32)
+    came = jnp.zeros((rows, LANES), jnp.int32)
+    for a in range(place_ref.shape[0]):
+        match = (place_ref[a : a + 1, :] - first == row).astype(jnp.float32)
+        seen = jnp.dot(match, upto, preferred_element_type=jnp.float32) + before
+        before = seen[:, LANES - 1 : LANES]
+        came = came + first_at_least(seen, turn, rows)
+    came = jnp.where((turn >= 1.0) & (turn <= before), came, -1)
     here = came >= 0
     block, at = came // LANES, came & (LANES - 1)
     lane8 = lane_iota(8)
@@ -311,7 +286,7 @@
     state = []
     for c in range(10):
         value = jnp.zeros((rows, LANES), jnp.float32)
-        for a in range(sources * per // LANES):
+        for a in range(place_ref.shape[0]):
             line = got_ref[8 * a : 8 * a + 8, c // 8, :]
             line = take(line, lane8 % per + (c % 8) * per)
             line = jnp.sum(jnp.where(mine, line, 0.0), axis=0, keepdims=True)
@@ -479,14 +454,13 @@
             i_ref[c * SHARE + v, at : at + cells, :] = field
 
 
-def force_kernel(end_ref, place_ref, count0_ref, share_ref, count_ref, coef_ref, got_ref,
+def force_kernel(end_ref, share_ref, place_ref, count_ref, coef_ref, got_ref,
                  msort_ref, psort_ref, mraw_in, praw_ref, mrank_in, prank_ref,
                  below_ref, above_ref, side_ref, bin_ref,
                  mpos_out, mvel_out, mforce_out, ppos_out, pvel_out, pforce_out,
                  mj_ref, pj_ref, mi_ref, pi_ref, mbase_ref, mcount_ref, pbase_ref, pcount_ref,
                  mheld_ref, pheld_ref, mreach_ref, preach_ref, steps_ref,
-                 mraw_ref, mrank_ref, filled_ref, push_ref,
-                 from_ref):
+                 mraw_ref, mrank_ref, push_ref):
     flow_rows, cells = msort_ref.shape[1], msort_ref.shape[2]
     prec_cells = psort_ref.shape[2]
     ends = tuple(end_ref[e] > 0 for e in range(4))
@@ -500,8 +474,7 @@
 
     @pl.when(end_ref[0] == 0)
     def _():
-        arrivals(end_ref[4], place_ref, got_ref, count0_ref, count_ref, mj_ref, mraw_ref, mrank_ref,
-                 filled_ref, from_ref)
+        arrivals(end_ref[4], place_ref, got_ref, count_ref, mj_ref, mraw_ref, mrank_ref)
 
     profile = jnp.sum(got_ref[:, 2:3, :], axis=0)[:, 0:BINS]
     push_ref[...] = jnp.zeros(push_ref.shape, jnp.float32)
@@ -587,9 +560,7 @@
         SMEM((total // 8 + prec_cells // 8,), jnp.int32),
         VMEM((7, total, LANES), jnp.float32),
         VMEM((total, LANES), jnp.int32),
-        SMEM((cells + 16,), jnp.int32),
         VMEM((8, LANES), jnp.float32),
-        VMEM((cells + 16, LANES), jnp.int32),
     ]
 
 
@@ -616,7 +587,7 @@
     flow_devices = lax.axis_size("flow")
     trans_devices = lax.axis_size("trans")
     total = flow_rows * cells
-    big = pltpu.CompilerParams(vmem_limit_bytes=48 << 20)
+    big = pltpu.CompilerParams(vmem_limit_bytes=63 << 20)
 
     def planes(value):
         return jnp.transpose(value, (0, 2, 1, 3))
@@ -660,11 +631,11 @@
         link_kernel,
         out_shape=(shape((trans_devices, 8, LANES)), shape((8, span, LANES)),
                    shape((8, span, LANES)), shape((6, 8, 8, LANES))),
-        in_specs=whole(VMEM, 5),
-        out_specs=tuple(whole(VMEM, 4)),
+        in_specs=whole(VMEM, 1) + whole(pl.ANY, 4),
+        out_specs=tuple(whole(VMEM, 1) + whole(pl.ANY, 3)),
         scratch_shapes=[pltpu.SemaphoreType.DMA((trans_devices,))] * 2
         + [pltpu.SemaphoreType.DMA((10,))] * 2,
-        compiler_params=pltpu.CompilerParams(vmem_limit_bytes=48 << 20, collective_id=0,
+        compiler_params=pltpu.CompilerParams(vmem_limit_bytes=63 << 20, collective_id=0,
                                              has_side_effects=True),
         name="link",
     )(own, msort, psort, left, right)
@@ -681,13 +652,13 @@
     outs = pl.pallas_call(
         force_kernel,
         out_shape=(out_main, out_main, out_main, out_prec, out_prec, out_prec),
-        in_specs=whole(SMEM, 4) + whole(VMEM, 13),
+        in_specs=whole(SMEM, 2) + whole(VMEM, 14),
         out_specs=tuple(whole(VMEM, 6)),
         scratch_shapes=scratches(flow_rows, cells, prec_cells),
         compiler_params=big,
         name="force",
-    )(ends, got[:, 1, 32:48].reshape(-1).astype(jnp.int32), main_count,
-      share, main_count, outlet_coef[None], got,
+    )(ends, share, got[:, 1, 32:48].reshape(-1, LANES).astype(jnp.int32), main_count,
+      outlet_coef[None], got,
       msort, psort, mraw, praw, mrank, prank, below, above, side, outlet_bin)
     return tuple(planes(v) for v in outs)
 

time: 116 us -> 108 us (0.931)
  local copies, waits for them, and re-layouts: 10.5 us -> 1.27 us
    unnamed x30 -> x0, local copies, waits for them, and re-layouts: 10.3 us -> none
    pallas_call x1, Pallas kernels: 73.5 us -> 70.2 us  [shards(): pl.pallas_call(force_kernel, out_shape=(out_main, out_main, out_main, out...]
    pallas_call x1, Pallas kernels: 3.18 us -> 5.19 us  [shards(): pl.pallas_call(main_kernel, out_shape=(shape((8, flow_rows, cells, LANES)...]
    pallas_call x1, Pallas kernels: 24 us -> 25.3 us  [shards(): pl.pallas_call(link_kernel, out_shape=(shape((trans_devices, 8, LANES)),...]
where the time goes in v6:
time: 108 us
  Pallas kernels  105 us (97%)
  local copies, waits for them, and re-layouts  1.27 us (1%)
    pallas_call x1, Pallas kernels, shards(): pl.pallas_call(force_kernel, out_shape=(out_main, out_main, out_main, out...  70.2 us
    pallas_call x1, Pallas kernels, shards(): pl.pallas_call(link_kernel, out_shape=(shape((trans_devices, 8, LANES)),...  25.3 us
    pallas_call x1, Pallas kernels, shards(): pl.pallas_call(main_kernel, out_shape=(shape((8, flow_rows, cells, LANES)...  5.19 us
    pallas_call x1, Pallas kernels, shards(): pl.pallas_call(prec_kernel, out_shape=(shape((8, LANES)), shape((8, 1, pr...  4.25 us

profile of v6, /device:TPU:199, one launch (start us, length us, event | category | flops | bytes accessed | tf_op | source)
XLA Modules:
  0.0 108.0 jit_solution(10360015831519101587)
XLA Ops:
  0.6 0.6 stack.39.end_ref
  1.3 4.2 %prec.1 = (f32[8,128]{1,0:T(8,128)}, f32[8,1,32,128]{3,2,1,0:T(8,128)}, f32[7,32,128]{2,1,0:T(8,128)}, s32[32,128]{1,0:T(8,128)}) custom-call(s32[16]{0:T(128)} %row_ref.1, s32[16]{0:T(128)} %dest_ref.1, s32[16]{0:T(128)} %cell_ref.1, s32[2,64]{1,0:T(2,128)} %count_ref.5, s32[64,128]{1,0:T(8,128)} %bin_ref.3, f32[1,3,32,128]{3,2,1,0:T(8,128)} %bitcast.22, ...), custom_call_target="tpu_custom_call" | custom-call | tf_op jit(solution)/shard_map/prec/pallas_call | solution.py:601
  5.5 5.2 %main.1 = (f32[8,2,64,128]{3,2,1,0:T(8,128)}, f32[7,128,128]{2,1,0:T(8,128)}, s32[128,128]{1,0:T(8,128)}, f32[8,8,128]{2,1,0:T(8,128)}, f32[8,8,128]{2,1,0:T(8,128)}) custom-call(s32[2,64]{1,0:T(2,128)} %count_ref.5, f32[2,3,64,128]{3,2,1,0:T(8,128)} %bitcast.19, f32[2,3,64,128]{3,2,1,0:T(8,128)} %bitcast.20, f32[2,3,64,128]{3,2,1,0:T(8,128)} %bitcast.21, ...), custom_call_target="tpu_custom_call" | custom-call | tf_op jit(solution)/shard_map/main/pallas_call | solution.py:614
  10.7 25.3 %link.1 = (f32[32,8,128]{2,1,0:T(8,128)}, f32[8,96,128]{2,1,0:T(8,128)}, f32[8,96,128]{2,1,0:T(8,128)}, f32[6,8,8,128]{3,2,1,0:T(8,128)}) custom-call(f32[8,128]{1,0:T(8,128)} %get-tuple-element.25.own_ref, f32[8,2,64,128]{3,2,1,0:T(8,128)} %get-tuple-element.27.msort_ref, f32[8,1,32,128]{3,2,1,0:T(8,128)} %get-tuple-element.26.psort_ref, ...), custom_call_target="tpu_custom_call" | custom-call | tf_op jit(solution)/shard_map/link/pallas_call | solution.py:630
  36.0 1.0 convert_reduce_fusion
  37.0 0.7 convert_element_type.10.place_ref
  37.7 70.2 %force.1 = (f32[2,3,64,128]{3,2,1,0:T(8,128)}, f32[2,3,64,128]{3,2,1,0:T(8,128)}, f32[2,3,64,128]{3,2,1,0:T(8,128)}, f32[1,3,32,128]{3,2,1,0:T(8,128)}, f32[1,3,...) custom-call(s32[5]{0:T(128)} %stack.39.end_ref, f32[1]{0:T(128)} %bitcast.5.share_ref, ...), custom_call_target="tpu_custom_call" | custom-call | tf_op jit(solution)/shard_map/force/pallas_call | solution.py:652

commit v7 on v6

--- a/solution.py
+++ b/solution.py
@@ -1,3 +1,5 @@
+import functools
+
 import jax
 import jax.numpy as jnp
 from jax import lax
@@ -101,22 +103,28 @@
     for df, dt in across:
         pl.semaphore_signal(barrier, inc=1, device_id=at(df, dt), device_id_type=mesh_id)
 
-    def greet(s, carry):
-        pl.semaphore_signal(barrier, inc=1, device_id=at(0, s), device_id_type=mesh_id)
-        return carry
-
+    for dt in (-1, 1):
+        pl.semaphore_signal(barrier, inc=1, device_id=at(0, dt), device_id_type=mesh_id)
+    inner = 8
+    outer = count // inner
+    high, low = trans // inner, lax.rem(trans, inner)
     meets = (flow == 0) | (flow == flows - 1)
+
+    def near(s):
+        return high * inner + lax.rem(low + inner + s, inner)
+
+    def far(s):
+        return lax.rem(high + outer + s, outer)
 
     @pl.when(meets)
     def _():
-        lax.fori_loop(1, count, greet, 0)
-
-    @pl.when(jnp.logical_not(meets))
-    def _():
-        greet(1, 0)
-        greet(count - 1, 0)
-
-    pl.semaphore_wait(barrier, len(across) + jnp.where(meets, count - 1, 2))
+        for s in range(1, inner):
+            pl.semaphore_signal(barrier, inc=1, device_id=(flow, near(s)), device_id_type=mesh_id)
+        for s in range(1, outer):
+            pl.semaphore_signal(barrier, inc=1, device_id=(flow, far(s) * inner + low),
+                                device_id_type=mesh_id)
+
+    pl.semaphore_wait(barrier, len(across) + 2 + jnp.where(meets, inner + outer - 2, 0))
     main_part, prec_part = pl.ds(0, cells), pl.ds(cells, prec_cells)
     plan = [
         (msort_ref.at[:, flow_rows - 1], below_ref.at[:, main_part], (1, 0)),
@@ -136,28 +144,40 @@
                                      device_id_type=mesh_id)
         for n, (src, dst, step) in enumerate(plan)
     ]
-    for copy in copies:
-        copy.start()
-
     def tile(s, slot):
         return pltpu.make_async_remote_copy(
             src_ref=own_ref, dst_ref=got_ref.at[slot], send_sem=tile_send.at[s],
-            recv_sem=tile_recv.at[slot], device_id=at(0, s), device_id_type=mesh_id)
-
-    def send(s, carry):
-        tile(s, trans).start()
-        return carry
-
-    def finish(s, carry):
-        tile(s, lax.rem(trans + count - s, count)).wait_recv()
-        tile(s, trans).wait_send()
-        return carry
+            recv_sem=tile_recv.at[lax.rem(slot, inner)], device_id=(flow, near(s)),
+            device_id_type=mesh_id)
+
+    def block(s, part):
+        rows = pl.ds(part * inner, inner)
+        return pltpu.make_async_remote_copy(
+            src_ref=got_ref.at[rows], dst_ref=got_ref.at[rows], send_sem=tile_send.at[inner + s],
+            recv_sem=tile_recv.at[inner + part], device_id=(flow, far(s) * inner + low),
+            device_id_type=mesh_id)
 
     @pl.when(meets)
     def _():
-        lax.fori_loop(1, count, send, 0)
+        for s in range(1, inner):
+            tile(s, trans).start()
+
+    for copy in copies:
+        copy.start()
+
+    @pl.when(meets)
+    def _():
         got_ref[trans] = own_ref[...]
-        lax.fori_loop(1, count, finish, 0)
+        for s in range(1, inner):
+            tile(s, near(-s)).wait_recv()
+        for s in range(1, outer):
+            block(s, high).start()
+        for s in range(1, outer):
+            block(s, far(-s)).wait_recv()
+        for s in range(1, inner):
+            tile(s, trans).wait_send()
+        for s in range(1, outer):
+            block(s, high).wait_send()
 
     @pl.when(jnp.logical_not(meets))
     def _():
@@ -262,7 +282,7 @@
     return first_at_least(height, edges, height.shape[0]).astype(jnp.float32)
 
 
-def arrivals(first, place_ref, got_ref, count_ref, j_ref, raw_ref, rank_ref):
+def arrivals(first, got_ref, count_ref, j_ref, raw_ref, rank_ref):
     cells = count_ref.shape[1]
     per = 16
     rows = j_ref.shape[2]
@@ -273,23 +293,27 @@
     turn = lane_iota(rows).astype(jnp.float32) - held + 1.0
     before = jnp.zeros((rows, 1), jnp.float32)
     came = jnp.zeros((rows, LANES), jnp.int32)
-    for a in range(place_ref.shape[0]):
-        match = (place_ref[a : a + 1, :] - first == row).astype(jnp.float32)
+    lane8 = lane_iota(8)
+    mine = lane8 // per == lax.broadcasted_iota(jnp.int32, (8, LANES), 0)
+    blocks = got_ref.shape[0] * per // LANES
+
+    def line_of(c, a):
+        line = take(got_ref[8 * a : 8 * a + 8, c // 8, :], lane8 % per + (c % 8) * per)
+        return jnp.sum(jnp.where(mine, line, 0.0), axis=0, keepdims=True)
+
+    for a in range(blocks):
+        match = (line_of(10, a).astype(jnp.int32) - first == row).astype(jnp.float32)
         seen = jnp.dot(match, upto, preferred_element_type=jnp.float32) + before
         before = seen[:, LANES - 1 : LANES]
         came = came + first_at_least(seen, turn, rows)
     came = jnp.where((turn >= 1.0) & (turn <= before), came, -1)
     here = came >= 0
     block, at = came // LANES, came & (LANES - 1)
-    lane8 = lane_iota(8)
-    mine = lane8 // per == lax.broadcasted_iota(jnp.int32, (8, LANES), 0)
     state = []
     for c in range(10):
         value = jnp.zeros((rows, LANES), jnp.float32)
-        for a in range(place_ref.shape[0]):
-            line = got_ref[8 * a : 8 * a + 8, c // 8, :]
-            line = take(line, lane8 % per + (c % 8) * per)
-            line = jnp.sum(jnp.where(mine, line, 0.0), axis=0, keepdims=True)
+        for a in range(blocks):
+            line = line_of(c, a)
             part = take(jnp.broadcast_to(line, (rows, LANES)), at)
             value = jnp.where(block == a, part, value)
         state.append(value)
@@ -454,7 +478,7 @@
             i_ref[c * SHARE + v, at : at + cells, :] = field
 
 
-def force_kernel(end_ref, share_ref, place_ref, count_ref, coef_ref, got_ref,
+def force_kernel(share, count_ref, coef_ref, got_ref,
                  msort_ref, psort_ref, mraw_in, praw_ref, mrank_in, prank_ref,
                  below_ref, above_ref, side_ref, bin_ref,
                  mpos_out, mvel_out, mforce_out, ppos_out, pvel_out, pforce_out,
@@ -463,7 +487,9 @@
                  mraw_ref, mrank_ref, push_ref):
     flow_rows, cells = msort_ref.shape[1], msort_ref.shape[2]
     prec_cells = psort_ref.shape[2]
-    ends = tuple(end_ref[e] > 0 for e in range(4))
+    flow, trans = lax.axis_index("flow"), lax.axis_index("trans")
+    last_flow = flow == lax.axis_size("flow") - 1
+    ends = (flow > 0, jnp.logical_not(last_flow), trans > 0, trans < lax.axis_size("trans") - 1)
     assemble(mj_ref, msort_ref, lambda c: below_ref[c, 0:cells, :], lambda c: above_ref[c, 0:cells, :],
              side_ref, 0, ends)
     assemble(pj_ref, psort_ref, lambda c: below_ref[c, cells : cells + prec_cells, :],
@@ -472,13 +498,13 @@
     mraw_ref[...] = mraw_in[...]
     mrank_ref[...] = mrank_in[...]
 
-    @pl.when(end_ref[0] == 0)
+    @pl.when(flow == 0)
     def _():
-        arrivals(end_ref[4], place_ref, got_ref, count_ref, mj_ref, mraw_ref, mrank_ref)
+        arrivals(trans * cells - 8, got_ref, count_ref, mj_ref, mraw_ref, mrank_ref)
 
     profile = jnp.sum(got_ref[:, 2:3, :], axis=0)[:, 0:BINS]
     push_ref[...] = jnp.zeros(push_ref.shape, jnp.float32)
-    push_ref[:, 0:BINS] = jnp.broadcast_to(-coef_ref[...] * (profile * share_ref[0]), (8, BINS))
+    push_ref[:, 0:BINS] = jnp.broadcast_to(-coef_ref[...] * (profile * jnp.where(last_flow, share, 0.0)), (8, BINS))
     push_row = push_ref[...]
     for j_ref, held_ref, n in ((mj_ref, mheld_ref, cells), (pj_ref, pheld_ref, prec_cells)):
         for f in range(held_ref.shape[0]):
@@ -582,9 +608,6 @@
 ):
     flow_rows, cells = main_seed.shape[0], main_seed.shape[1]
     prec_cells = prec_seed.shape[1]
-    flow_index = lax.axis_index("flow")
-    trans_index = lax.axis_index("trans")
-    flow_devices = lax.axis_size("flow")
     trans_devices = lax.axis_size("trans")
     total = flow_rows * cells
     big = pltpu.CompilerParams(vmem_limit_bytes=63 << 20)
@@ -596,7 +619,6 @@
     prec_state = [planes(v) for v in (prec_pos, prec_vel, prec_force)]
 
     share = BINS / (cells * trans_devices * LANES)
-    share = jnp.where(flow_index == flow_devices - 1, jnp.float32(share), 0.0)[None]
 
     own, psort, praw, prank = pl.pallas_call(
         prec_kernel,
@@ -633,32 +655,23 @@
                    shape((8, span, LANES)), shape((6, 8, 8, LANES))),
         in_specs=whole(VMEM, 1) + whole(pl.ANY, 4),
         out_specs=tuple(whole(VMEM, 1) + whole(pl.ANY, 3)),
-        scratch_shapes=[pltpu.SemaphoreType.DMA((trans_devices,))] * 2
+        scratch_shapes=[pltpu.SemaphoreType.DMA((8 + trans_devices // 8,))] * 2
         + [pltpu.SemaphoreType.DMA((10,))] * 2,
         compiler_params=pltpu.CompilerParams(vmem_limit_bytes=63 << 20, collective_id=0,
                                              has_side_effects=True),
         name="link",
     )(own, msort, psort, left, right)
-    ends = jnp.stack([
-        flow_index > 0,
-        flow_index < flow_devices - 1,
-        trans_index > 0,
-        trans_index < trans_devices - 1,
-        trans_index * cells - 8,
-    ]).astype(jnp.int32)
-
     out_main = shape((flow_rows, 3, cells, LANES))
     out_prec = shape((1, 3, prec_cells, LANES))
     outs = pl.pallas_call(
-        force_kernel,
+        functools.partial(force_kernel, share),
         out_shape=(out_main, out_main, out_main, out_prec, out_prec, out_prec),
-        in_specs=whole(SMEM, 2) + whole(VMEM, 14),
+        in_specs=whole(VMEM, 13),
         out_specs=tuple(whole(VMEM, 6)),
         scratch_shapes=scratches(flow_rows, cells, prec_cells),
         compiler_params=big,
         name="force",
-    )(ends, share, got[:, 1, 32:48].reshape(-1, LANES).astype(jnp.int32), main_count,
-      outlet_coef[None], got,
+    )(main_count, outlet_coef[None], got,
       msort, psort, mraw, praw, mrank, prank, below, above, side, outlet_bin)
     return tuple(planes(v) for v in outs)
 

time: 108 us -> 104 us (0.963)
  Pallas kernels: 105 us -> 103 us
  local copies, waits for them, and re-layouts: 1.27 us -> 0 us
    pallas_call x1, Pallas kernels: 25.3 us -> 22.9 us  [shards(): pl.pallas_call(link_kernel, out_shape=(shape((trans_devices, 8, LANES)),...]
where the time goes in v7:
time: 104 us
  Pallas kernels  103 us (99%)
    pallas_call x1, Pallas kernels, shards(): pl.pallas_call(functools.partial(force_kernel, share), out_shape=(out_mai...  70.7 us
    pallas_call x1, Pallas kernels, shards(): pl.pallas_call(link_kernel, out_shape=(shape((trans_devices, 8, LANES)),...  22.9 us
    pallas_call x1, Pallas kernels, shards(): pl.pallas_call(main_kernel, out_shape=(shape((8, flow_rows, cells, LANES)...  5.2 us
    pallas_call x1, Pallas kernels, shards(): pl.pallas_call(prec_kernel, out_shape=(shape((8, LANES)), shape((8, 1, pr...  4.24 us

profile of v7, /device:TPU:199, one launch (start us, length us, event | category | flops | bytes accessed | tf_op | source)
XLA Modules:
  0.0 103.7 jit_solution(2463063738196697967)
XLA Ops:
  0.6 4.2 %prec.1 = (f32[8,128]{1,0:T(8,128)}, f32[8,1,32,128]{3,2,1,0:T(8,128)}, f32[7,32,128]{2,1,0:T(8,128)}, s32[32,128]{1,0:T(8,128)}) custom-call(s32[16]{0:T(128)} %row_ref.1, s32[16]{0:T(128)} %dest_ref.1, s32[16]{0:T(128)} %cell_ref.1, s32[2,64]{1,0:T(2,128)} %count_ref.5, s32[64,128]{1,0:T(8,128)} %bin_ref.3, f32[1,3,32,128]{3,2,1,0:T(8,128)} %bitcast.16, ...), custom_call_target="tpu_custom_call" | custom-call | tf_op jit(solution)/shard_map/prec/pallas_call | solution.py:623
  4.9 5.2 %main.1 = (f32[8,2,64,128]{3,2,1,0:T(8,128)}, f32[7,128,128]{2,1,0:T(8,128)}, s32[128,128]{1,0:T(8,128)}, f32[8,8,128]{2,1,0:T(8,128)}, f32[8,8,128]{2,1,0:T(8,128)}) custom-call(s32[2,64]{1,0:T(2,128)} %count_ref.5, f32[2,3,64,128]{3,2,1,0:T(8,128)} %bitcast.13, f32[2,3,64,128]{3,2,1,0:T(8,128)} %bitcast.14, f32[2,3,64,128]{3,2,1,0:T(8,128)} %bitcast.15, ...), custom_call_target="tpu_custom_call" | custom-call | tf_op jit(solution)/shard_map/main/pallas_call | solution.py:636
  10.1 22.9 %link.1 = (f32[32,8,128]{2,1,0:T(8,128)}, f32[8,96,128]{2,1,0:T(8,128)}, f32[8,96,128]{2,1,0:T(8,128)}, f32[6,8,8,128]{3,2,1,0:T(8,128)}) custom-call(f32[8,128]{1,0:T(8,128)} %get-tuple-element.25.own_ref, f32[8,2,64,128]{3,2,1,0:T(8,128)} %get-tuple-element.27.msort_ref, f32[8,1,32,128]{3,2,1,0:T(8,128)} %get-tuple-element.26.psort_ref, ...), custom_call_target="tpu_custom_call" | custom-call | tf_op jit(solution)/shard_map/link/pallas_call | solution.py:652
  33.0 70.7 %force.1 = (f32[2,3,64,128]{3,2,1,0:T(8,128)}, f32[2,3,64,128]{3,2,1,0:T(8,128)}, f32[2,3,64,128]{3,2,1,0:T(8,128)}, f32[1,3,32,128]{3,2,1,0:T(8,128)}, f32[1,3,...) custom-call(s32[2,64]{1,0:T(2,128)} %count_ref.5, f32[1,64]{1,0:T(1,128)} %bitcast.19, ...), custom_call_target="tpu_custom_call" | custom-call | tf_op jit(solution)/shard_map/force/pallas_call | solution.py:666

commit v8 on v7

--- a/solution.py
+++ b/solution.py
@@ -484,7 +484,7 @@
                  mpos_out, mvel_out, mforce_out, ppos_out, pvel_out, pforce_out,
                  mj_ref, pj_ref, mi_ref, pi_ref, mbase_ref, mcount_ref, pbase_ref, pcount_ref,
                  mheld_ref, pheld_ref, mreach_ref, preach_ref, steps_ref,
-                 mraw_ref, mrank_ref, push_ref):
+                 mraw_ref, mrank_ref, push_ref, table_ref, sem_ref):
     flow_rows, cells = msort_ref.shape[1], msort_ref.shape[2]
     prec_cells = psort_ref.shape[2]
     flow, trans = lax.axis_index("flow"), lax.axis_index("trans")
@@ -519,16 +519,19 @@
     search(pj_ref, 0, prec_cells, pi_ref, pbase_ref, pcount_ref, pheld_ref, preach_ref, 0)
     groups = flow_rows * cells // 8
     prec_groups = prec_cells // 8
-    for g in range(groups):
-        steps_ref[g] = (jnp.max(mreach_ref[8 * g : 8 * g + 8, :]) + (SHARE - 1)) // SHARE
-    for g in range(prec_groups):
-        steps_ref[groups + g] = (jnp.max(preach_ref[8 * g : 8 * g + 8, :]) + (SHARE - 1)) // SHARE
+    for ref, start, n in ((mreach_ref, 0, groups), (preach_ref, groups, prec_groups)):
+        most = jnp.max(ref[...].reshape(n, 8, LANES), axis=1)
+        most = (jnp.max(most, axis=1, keepdims=True) + (SHARE - 1)) // SHARE
+        table_ref[start : start + n, :] = jnp.broadcast_to(most, (n, LANES))
+    to_scalars = pltpu.make_async_copy(table_ref, steps_ref, sem_ref.at[0])
+    to_scalars.start()
+    to_scalars.wait()
 
     def main_group(g, carry):
         f = g // (cells // 8)
         r0 = pl.multiple_of((g % (cells // 8)) * 8, 8)
         i0 = pl.multiple_of(g * 8, 8)
-        sums = pair_sums(mj_ref, f, r0, mi_ref, i0, mbase_ref, mcount_ref, mheld_ref, steps_ref[g])
+        sums = pair_sums(mj_ref, f, r0, mi_ref, i0, mbase_ref, mcount_ref, mheld_ref, steps_ref[g, 0])
         force = unsorted_sums(sums, mrank_ref[pl.ds(i0, 8), :])
         occupied = mraw_ref[6, pl.ds(i0, 8), :] >= 0.0
         push = take(push_row, bin_ref[pl.ds(r0, 8), :])
@@ -547,7 +550,7 @@
     def prec_group(g, carry):
         r0 = pl.multiple_of(g * 8, 8)
         sums = pair_sums(pj_ref, 0, r0, pi_ref, r0, pbase_ref, pcount_ref, pheld_ref,
-                         steps_ref[groups + g])
+                         steps_ref[groups + g, 0])
         force = unsorted_sums(sums, prank_ref[pl.ds(r0, 8), :])
         for c in range(3):
             half = praw_ref[3 + c, pl.ds(r0, 8), :]
@@ -583,10 +586,12 @@
         VMEM((3, prec_cells + 16, LANES), jnp.int32),
         VMEM((total, LANES), jnp.int32),
         VMEM((prec_cells, LANES), jnp.int32),
-        SMEM((total // 8 + prec_cells // 8,), jnp.int32),
+        SMEM((total // 8 + prec_cells // 8, LANES), jnp.int32),
         VMEM((7, total, LANES), jnp.float32),
         VMEM((total, LANES), jnp.int32),
         VMEM((8, LANES), jnp.float32),
+        VMEM((total // 8 + prec_cells // 8, LANES), jnp.int32),
+        pltpu.SemaphoreType.DMA((1,)),
     ]
 
 

time: 104 us -> 104 us (level)
  no operation moved by 1% of the time
where the time goes in v8:
time: 104 us
  Pallas kernels  104 us (100%)
    pallas_call x1, Pallas kernels, shards(): pl.pallas_call(functools.partial(force_kernel, share), out_shape=(out_mai...  71.2 us
    pallas_call x1, Pallas kernels, shards(): pl.pallas_call(link_kernel, out_shape=(shape((trans_devices, 8, LANES)),...  22.9 us
    pallas_call x1, Pallas kernels, shards(): pl.pallas_call(main_kernel, out_shape=(shape((8, flow_rows, cells, LANES)...  5.2 us
    pallas_call x1, Pallas kernels, shards(): pl.pallas_call(prec_kernel, out_shape=(shape((8, LANES)), shape((8, 1, pr...  4.24 us

profile of v8, /device:TPU:199, one launch (start us, length us, event | category | flops | bytes accessed | tf_op | source)
XLA Modules:
  0.0 104.2 jit_solution(13853237848023125948)
XLA Ops:
  0.6 4.2 %prec.1 = (f32[8,128]{1,0:T(8,128)}, f32[8,1,32,128]{3,2,1,0:T(8,128)}, f32[7,32,128]{2,1,0:T(8,128)}, s32[32,128]{1,0:T(8,128)}) custom-call(s32[16]{0:T(128)} %row_ref.1, s32[16]{0:T(128)} %dest_ref.1, s32[16]{0:T(128)} %cell_ref.1, s32[2,64]{1,0:T(2,128)} %count_ref.5, s32[64,128]{1,0:T(8,128)} %bin_ref.3, f32[1,3,32,128]{3,2,1,0:T(8,128)} %bitcast.16, ...), custom_call_target="tpu_custom_call" | custom-call | tf_op jit(solution)/shard_map/prec/pallas_call | solution.py:628
  4.9 5.2 %main.1 = (f32[8,2,64,128]{3,2,1,0:T(8,128)}, f32[7,128,128]{2,1,0:T(8,128)}, s32[128,128]{1,0:T(8,128)}, f32[8,8,128]{2,1,0:T(8,128)}, f32[8,8,128]{2,1,0:T(8,128)}) custom-call(s32[2,64]{1,0:T(2,128)} %count_ref.5, f32[2,3,64,128]{3,2,1,0:T(8,128)} %bitcast.13, f32[2,3,64,128]{3,2,1,0:T(8,128)} %bitcast.14, f32[2,3,64,128]{3,2,1,0:T(8,128)} %bitcast.15, ...), custom_call_target="tpu_custom_call" | custom-call | tf_op jit(solution)/shard_map/main/pallas_call | solution.py:641
  10.1 22.9 %link.1 = (f32[32,8,128]{2,1,0:T(8,128)}, f32[8,96,128]{2,1,0:T(8,128)}, f32[8,96,128]{2,1,0:T(8,128)}, f32[6,8,8,128]{3,2,1,0:T(8,128)}) custom-call(f32[8,128]{1,0:T(8,128)} %get-tuple-element.25.own_ref, f32[8,2,64,128]{3,2,1,0:T(8,128)} %get-tuple-element.27.msort_ref, f32[8,1,32,128]{3,2,1,0:T(8,128)} %get-tuple-element.26.psort_ref, ...), custom_call_target="tpu_custom_call" | custom-call | tf_op jit(solution)/shard_map/link/pallas_call | solution.py:657
  33.0 71.2 %force.1 = (f32[2,3,64,128]{3,2,1,0:T(8,128)}, f32[2,3,64,128]{3,2,1,0:T(8,128)}, f32[2,3,64,128]{3,2,1,0:T(8,128)}, f32[1,3,32,128]{3,2,1,0:T(8,128)}, f32[1,3,...) custom-call(s32[2,64]{1,0:T(2,128)} %count_ref.5, f32[1,64]{1,0:T(1,128)} %bitcast.19, ...), custom_call_target="tpu_custom_call" | custom-call | tf_op jit(solution)/shard_map/force/pallas_call | solution.py:671
